TPU v7x, 128 devices: a whole 4x4x4 slice. The times are simulated.
128 devices in a mesh: row: 16 (over y, z), col: 8 (over x, core).
Axes of the slice: x: 4, y: 4, z: 4, core: 2. Of those that a mesh axis runs over, the one named last changes fastest.
Arguments:
- tokens: bfloat16 [2048, 4096], P('row', 'col'), may hold values from -6 to 6
- w_in: bfloat16 [4096, 16384], P('col', 'row'), may hold values from -0.09375 to 0.09375
- w_out: bfloat16 [16384, 4096], P('row', 'col'), may hold values from -0.046875 to 0.046875
- cotangent: bfloat16 [2048, 4096], P('row', 'col'), may hold values from -6 to 6
Outputs:
- block_out: bfloat16 [2048, 4096], P(('row', 'col'))
- grad_tokens: bfloat16 [2048, 4096], P('row', 'col')
- grad_in: float32 [4096, 16384], P('col', 'row')
- grad_out: float32 [16384, 4096], P('row', 'col')
All inputs are finite; a program needn't handle non-finite values.
Results may differ from a plain program's by a relative error of at most 0.015.
Values may be sent and summed in bfloat16 or wider, within the bound.
A program may use at most 128 MiB of HBM per device.

v0:
```python
import jax
import jax.numpy as jnp
from jax import lax
from jax.sharding import PartitionSpec as P


def gelu_grad(value):
    cdf = 0.5 * (1.0 + jax.scipy.special.erf(value * 0.7071067811865476))
    pdf = jnp.exp(-0.5 * value * value) * 0.3989422804014327
    return cdf + value * pdf


def token_panel(local_rows):
    return lax.all_gather(local_rows, "row", axis=0, tiled=True)


def hidden_panel(local_rows):
    return lax.all_gather(local_rows, "col", axis=0, tiled=True)


def contract_last(left, right):
    return lax.dot_general(
        left, right, (((1,), (1,)), ((), ())), preferred_element_type=jnp.float32
    )


def width_split(left_all, right, transposed):

    def width_term():
        if transposed:
            return contract_last(left_all, right)
        return jnp.dot(left_all, right, preferred_element_type=jnp.float32)

    return lax.psum_scatter(
        width_term().astype(jnp.bfloat16), "col", scatter_dimension=0, tiled=True
    ).astype(jnp.float32)


def unit_sum(left_all, right, transposed):

    def unit_term():
        if transposed:
            return contract_last(left_all, right)
        return jnp.dot(left_all, right, preferred_element_type=jnp.float32)

    return lax.psum_scatter(
        unit_term().astype(jnp.bfloat16), "row", scatter_dimension=0, tiled=True
    ).astype(jnp.float32)


def local(tokens, w_in, w_out, cotangent):
    tokens_all = token_panel(tokens)
    upstream_all = token_panel(cotangent)
    pre_part = width_split(tokens_all, w_in, False)
    act_all = hidden_panel(jax.nn.gelu(pre_part, approximate=False).astype(jnp.bfloat16))
    dact_part = width_split(upstream_all, w_out, True)
    dpre_all = hidden_panel((dact_part * gelu_grad(pre_part)).astype(jnp.bfloat16))
    mixed = unit_sum(act_all, w_out, False)
    block_rows = (tokens.astype(jnp.float32) + mixed).astype(jnp.bfloat16)
    block_out = lax.all_to_all(block_rows, "col", split_axis=0, concat_axis=1, tiled=True)
    grad_out = lax.dot_general(
        act_all, upstream_all, (((0,), (0,)), ((), ())), preferred_element_type=jnp.float32
    )
    grad_in = lax.dot_general(
        tokens_all, dpre_all, (((0,), (0,)), ((), ())), preferred_element_type=jnp.float32
    )
    back = unit_sum(dpre_all, w_in, True)
    grad_tokens = (cotangent.astype(jnp.float32) + back).astype(jnp.bfloat16)
    return (block_out, grad_tokens, grad_in, grad_out)


def solution(mesh):
    in_specs = (P("row", "col"), P("col", "row"), P("row", "col"), P("row", "col"))
    out_specs = (P(("row", "col"), None), P("row", "col"), P("col", "row"), P("row", "col"))
    return jax.shard_map(local, mesh=mesh, in_specs=in_specs, out_specs=out_specs, check_vma=False)
```

profile of v0, /device:TPU:1, one launch (start us, length us, event | category | flops | bytes accessed | tf_op | source)
XLA Modules:
  0.0 416.6 jit_solution(6592428128549312227)
XLA Ops:
  7.2 0.7 all-gather.9.cloned.1.call-update
  8.0 0.7 all-gather.5.cloned.1.call-update
  8.7 48.9 %all-gather.9.cloned.1.call-done = bf16[2048,512]{1,0:T(8,128)(2,1)} async-done(((bf16[128,512]{1,0:T(8,128)(2,1)}), bf16[2048,512]{1,0:T(8,128)(2,1)}) %all-gather.9.cloned.1.call-update) | async-done | bytes 2097168 | tf_op jit(solution)/shard_map/all_gather | solution.py:14
  57.6 5.9 %convolution_convert_fusion = bf16[2048,1024]{1,0:T(8,128)(2,1)} fusion(bf16[2048,512]{1,0:T(8,128)(2,1)} %all-gather.9.cloned.1.call-done, bf16[1024,512]{1,0:T(8,128)(2,1)S(1)} %copy-done), kind=kOutput, calls=%fused_computation | convolution fusion | flops 2149580800 | bytes 7340032 | tf_op jit(solution)/shard_map/dot_general | solution.py:22
  63.6 40.7 %all-gather.5.cloned.1.call-done = bf16[2048,512]{1,0:T(8,128)(2,1)} async-done(((bf16[128,512]{1,0:T(8,128)(2,1)}), bf16[2048,512]{1,0:T(8,128)(2,1)}) %all-gather.5.cloned.1.call-update) | async-done | bytes 2097168 | tf_op jit(solution)/shard_map/all_gather | solution.py:14
  104.4 5.9 %convolution_convert_fusion.1 = bf16[2048,1024]{1,0:T(8,128)(2,1)} fusion(bf16[2048,512]{1,0:T(8,128)(2,1)} %all-gather.5.cloned.1.call-done, bf16[512,1024]{1,0:T(8,128)(2,1)S(1)} %copy-done.3), kind=kOutput, calls=%fused_computation.1 | convolution fusion | flops 2149580800 | bytes 7340032 | tf_op jit(solution)/shard_map/dot_general | solution.py:32
  110.3 31.7 %reduce-scatter.9.cloned.1.call-done = bf16[256,1024]{1,0:T(8,128)(2,1)} async-done(((bf16[2048,1024]{1,0:T(8,128)(2,1)}), bf16[256,1024]{1,0:T(8,128)(2,1)}) %reduce-scatter.9.cloned.1.call-update) | async-done | bytes 524304 | tf_op jit(solution)/shard_map/reduce_scatter | solution.py:34
  142.0 38.9 %reduce-scatter.5.cloned.1.call-done = bf16[256,1024]{1,0:T(8,128)(2,1)} async-done(((bf16[2048,1024]{1,0:T(8,128)(2,1)}), bf16[256,1024]{1,0:T(8,128)(2,1)}) %reduce-scatter.5.cloned.1.call-update) | async-done | bytes 524304 | tf_op jit(solution)/shard_map/reduce_scatter | solution.py:34
  181.0 4.6 %fusion.38 = (bf16[256,1024]{1,0:T(8,128)(2,1)}, bf16[256,1024]{1,0:T(8,128)(2,1)}) fusion(bf16[256,1024]{1,0:T(8,128)(2,1)} %reduce-scatter.5.cloned.1.call-done, bf16[256,1024]{1,0:T(8,128)(2,1)} %reduce-scatter.9.cloned.1.call-done), kind=kLoop, calls=%fused_computation.50 | loop fusion | flops 20185088 | bytes 2097152 | tf_op jit(solution)/shard_map/convert_element_type | solution.py:57
  185.6 0.5 all-gather.11.cloned.1.call-update
  186.2 34.0 %all-gather.7.cloned.1.call-done = bf16[2048,1024]{1,0:T(8,128)(2,1)} async-done(((bf16[256,1024]{1,0:T(8,128)(2,1)}), bf16[2048,1024]{1,0:T(8,128)(2,1)}) %all-gather.7.cloned.1.call-update) | async-done | bytes 4194320 | tf_op jit(solution)/shard_map/all_gather | solution.py:18
  220.2 5.9 %convolution_convert_fusion.3 = bf16[2048,512]{1,0:T(8,128)(2,1)} fusion(bf16[2048,1024]{1,0:T(8,128)(2,1)} %all-gather.7.cloned.1.call-done, bf16[1024,512]{1,0:T(8,128)(2,1)S(1)} %copy-done), kind=kOutput, calls=%fused_computation.3 | convolution fusion | flops 2148532224 | bytes 7340032 | tf_op jit(solution)/shard_map/dot_general | solution.py:44
  226.1 0.2 reduce-scatter.11.cloned.1.call-start
  226.3 28.1 %all-gather.11.cloned.1.call-done = bf16[2048,1024]{1,0:T(8,128)(2,1)} async-done(((bf16[256,1024]{1,0:T(8,128)(2,1)}), bf16[2048,1024]{1,0:T(8,128)(2,1)}) %all-gather.11.cloned.1.call-update) | async-done | bytes 4194320 | tf_op jit(solution)/shard_map/all_gather | solution.py:18
  254.4 5.9 %convolution_convert_fusion.2 = bf16[2048,512]{1,0:T(8,128)(2,1)} fusion(bf16[2048,1024]{1,0:T(8,128)(2,1)} %all-gather.11.cloned.1.call-done, bf16[512,1024]{1,0:T(8,128)(2,1)S(1)} %copy-done.3), kind=kOutput, calls=%fused_computation.2 | convolution fusion | flops 2148532224 | bytes 7340032 | tf_op jit(solution)/shard_map/dot_general | solution.py:22
  260.3 5.2 %convolution_bitcast_fusion = f32[512,1024]{0,1:T(8,128)S(1)} fusion(bf16[2048,1024]{1,0:T(8,128)(2,1)} %all-gather.11.cloned.1.call-done, bf16[2048,512]{1,0:T(8,128)(2,1)} %all-gather.5.cloned.1.call-done), kind=kOutput, calls=%fused_computation.10 | convolution fusion | flops 2147483648 | bytes 8388608 | tf_op jit(solution)/shard_map/dot_general | solution.py:64
  265.5 1.8 copy.9
  267.3 6.6 %fusion.39 = f32[1024,512]{1,0:T(8,128)} fusion(bf16[2048,1024]{1,0:T(8,128)(2,1)} %all-gather.7.cloned.1.call-done, bf16[2048,512]{1,0:T(8,128)(2,1)} %all-gather.9.cloned.1.call-done), kind=kOutput, calls=%fused_computation.53 | convolution fusion | flops 2147483648 | bytes 8388608 | tf_op jit(solution)/shard_map/dot_general | solution.py:61
  273.9 56.2 %reduce-scatter.7.cloned.1.call-done = bf16[128,512]{1,0:T(8,128)(2,1)} async-done(((bf16[2048,512]{1,0:T(8,128)(2,1)}), bf16[128,512]{1,0:T(8,128)(2,1)}) %reduce-scatter.7.cloned.1.call-update) | async-done | bytes 131088 | tf_op jit(solution)/shard_map/reduce_scatter | solution.py:46
  330.2 1.6 add_convert_fusion.1
  331.8 6.5 %all-to-all-start = ((bf16[8,16,512]{2,1,0:T(8,128)(2,1)}), bf16[8,16,512]{2,1,0:T(8,128)(2,1)S(1)}, u32[]{:S(2)}, u32[]{:S(2)}) async-start(bf16[8,16,512]{2,1,0:T(8,128)(2,1)} %bitcast), calls=%async_computation.2 | async-start | bytes 262144 | tf_op jit(solution)/shard_map/all_to_all | solution.py:60
  338.3 69.2 %reduce-scatter.11.cloned.1.call-done = bf16[128,512]{1,0:T(8,128)(2,1)} async-done(((bf16[2048,512]{1,0:T(8,128)(2,1)}), bf16[128,512]{1,0:T(8,128)(2,1)}) %reduce-scatter.11.cloned.1.call-update) | async-done | bytes 131088 | tf_op jit(solution)/shard_map/reduce_scatter | solution.py:46
  407.5 1.6 add_convert_fusion
  409.1 0.7 copy.10
  (21 shorter events, 0.4 us)
Async XLA Ops:
  7.2 50.5 %copy-start = (bf16[1024,512]{1,0:T(8,128)(2,1)S(1)}, bf16[1024,512]{1,0:T(8,128)(2,1)}, u32[]{:S(2)}) copy-start(bf16[1024,512]{1,0:T(8,128)(2,1)} %param.6) | copy-start | bytes 3145732
  7.2 50.5 %all-gather.9.cloned.1.call-start = ((), (), s32[]{:S(2)}) async-start(), calls=%async_computation.9 | async-start | bytes 2228224 | tf_op jit(solution)/shard_map/all_gather | solution.py:14
  7.9 96.4 %all-gather.5.cloned.1.call-start = ((), (), s32[]{:S(2)}) async-start(), calls=%async_computation.5 | async-start | bytes 2228224 | tf_op jit(solution)/shard_map/all_gather | solution.py:14
  8.7 133.4 %reduce-scatter.9.cloned.1.call-start = ((), (), s32[]{:S(2)}) async-start(), calls=%async_computation.10 | async-start | bytes 4718592 | tf_op jit(solution)/shard_map/reduce_scatter | solution.py:34
  63.6 40.8 %copy-start.3 = (bf16[512,1024]{1,0:T(8,128)(2,1)S(1)}, bf16[512,1024]{1,0:T(8,128)(2,1)}, u32[]{:S(2)}) copy-start(bf16[512,1024]{1,0:T(8,128)(2,1)} %param.5) | copy-start | bytes 3145732
  63.6 117.4 %reduce-scatter.5.cloned.1.call-start = ((), (), s32[]{:S(2)}) async-start(), calls=%async_computation.6 | async-start | bytes 4718592 | tf_op jit(solution)/shard_map/reduce_scatter | solution.py:34
  110.3 109.9 %all-gather.7.cloned.1.call-start = ((), (), s32[]{:S(2)}) async-start(), calls=%async_computation.7 | async-start | bytes 4718592 | tf_op jit(solution)/shard_map/all_gather | solution.py:18
  185.6 68.9 %all-gather.11.cloned.1.call-start = ((), (), s32[]{:S(2)}) async-start(), calls=%async_computation.11 | async-start | bytes 4718592 | tf_op jit(solution)/shard_map/all_gather | solution.py:18
  186.1 144.0 %reduce-scatter.7.cloned.1.call-start = ((), (), s32[]{:S(2)}) async-start(), calls=%async_computation.8 | async-start | bytes 2228224 | tf_op jit(solution)/shard_map/reduce_scatter | solution.py:46
  226.1 181.4 %reduce-scatter.11.cloned.1.call-start = ((), (), s32[]{:S(2)}) async-start(), calls=%async_computation.12 | async-start | bytes 2228224 | tf_op jit(solution)/shard_map/reduce_scatter | solution.py:46
  267.3 62.8 %copy-start.1 = (bf16[128,512]{1,0:T(8,128)(2,1)S(1)}, bf16[128,512]{1,0:T(8,128)(2,1)}, u32[]{:S(2)}) copy-start(bf16[128,512]{1,0:T(8,128)(2,1)} %param.4) | copy-start | bytes 393220
  267.3 140.2 %copy-start.2 = (bf16[128,512]{1,0:T(8,128)(2,1)S(1)}, bf16[128,512]{1,0:T(8,128)(2,1)}, u32[]{:S(2)}) copy-start(bf16[128,512]{1,0:T(8,128)(2,1)} %param.7) | copy-start | bytes 393220
  331.8 77.4 %all-to-all-start = ((bf16[8,16,512]{2,1,0:T(8,128)(2,1)}), bf16[8,16,512]{2,1,0:T(8,128)(2,1)S(1)}, u32[]{:S(2)}, u32[]{:S(2)}) async-start(bf16[8,16,512]{2,1,0:T(8,128)(2,1)} %bitcast), calls=%async_computation.2 | async-start | bytes 262144 | tf_op jit(solution)/shard_map/all_to_all | solution.py:60
Sparse Core Ops, SparseCore 0:
  10.2 47.4 all-gather.8
  59.8 44.5 all-gather.4
  106.8 35.2 reduce-scatter.8
  144.3 36.6 reduce-scatter.4
  185.7 34.4 all-gather.6
  222.3 32.0 all-gather.10
  257.7 72.4 reduce-scatter.6
  333.8 73.7 reduce-scatter.10
where the time goes:
time: 418 us; the launch traced here: 417 us
  waiting for transfers between devices  350 us (84%)
  matrix products  35.4 us (8%)
  between operations  14.2 us (3%)
  other arithmetic  7.74 us (2%)
  starting transfers between devices  7.05 us (2%)
    reduce_scatter x2, waiting for transfers between devices, unit_sum(): lax.psum_scatter(unit_term().astype(jnp.bfloat16), 'row', scatter_dimensi...  125 us
    all_gather x2, waiting for transfers between devices, token_panel(): return lax.all_gather(local_rows, 'row', axis=0, tiled=True)  89.6 us
    reduce_scatter x2, waiting for transfers between devices, width_split(): lax.psum_scatter(width_term().astype(jnp.bfloat16), 'col', scatter_dimens...  70.6 us
    all_gather x2, waiting for transfers between devices, hidden_panel(): return lax.all_gather(local_rows, 'col', axis=0, tiled=True)  62.1 us
    dot_general x2, matrix products, contract_last(): lax.dot_general(left, right, (((1,), (1,)), ((), ())), preferred_element_...  11.8 us
  transfers between devices with their start and end apart: 9, of which 8 were waited for; matrix products, arithmetic and copies ran while one was open for 10% of the time, Pallas kernels for 0%

commit v1 on v0

--- a/solution.py
+++ b/solution.py
@@ -14,6 +14,13 @@
     return lax.all_gather(local_rows, "row", axis=0, tiled=True)
 
 
+def token_panel_a2a(local_rows):
+    n = lax.axis_size("row")
+    copies = jnp.broadcast_to(local_rows[None], (n,) + local_rows.shape)
+    copies = copies.reshape(n * local_rows.shape[0], local_rows.shape[1])
+    return lax.all_to_all(copies, "row", split_axis=0, concat_axis=0, tiled=True)
+
+
 def hidden_panel(local_rows):
     return lax.all_gather(local_rows, "col", axis=0, tiled=True)
 
@@ -25,32 +32,29 @@
 
 
 def width_split(left_all, right, transposed):
-
-    def width_term():
-        if transposed:
-            return contract_last(left_all, right)
-        return jnp.dot(left_all, right, preferred_element_type=jnp.float32)
-
+    if transposed:
+        term = contract_last(left_all, right)
+    else:
+        term = jnp.dot(left_all, right, preferred_element_type=jnp.float32)
     return lax.psum_scatter(
-        width_term().astype(jnp.bfloat16), "col", scatter_dimension=0, tiled=True
+        term.astype(jnp.bfloat16), "col", scatter_dimension=0, tiled=True
     ).astype(jnp.float32)
 
 
 def unit_sum(left_all, right, transposed):
-
-    def unit_term():
-        if transposed:
-            return contract_last(left_all, right)
-        return jnp.dot(left_all, right, preferred_element_type=jnp.float32)
-
-    return lax.psum_scatter(
-        unit_term().astype(jnp.bfloat16), "row", scatter_dimension=0, tiled=True
-    ).astype(jnp.float32)
+    n = lax.axis_size("row")
+    if transposed:
+        term = contract_last(left_all, right)
+    else:
+        term = jnp.dot(left_all, right, preferred_element_type=jnp.float32)
+    pieces = term.astype(jnp.bfloat16).reshape(n, term.shape[0] // n, term.shape[1])
+    pieces = lax.all_to_all(pieces, "row", split_axis=0, concat_axis=0, tiled=True)
+    return jnp.sum(pieces.astype(jnp.float32), axis=0)
 
 
 def local(tokens, w_in, w_out, cotangent):
     tokens_all = token_panel(tokens)
-    upstream_all = token_panel(cotangent)
+    upstream_all = token_panel_a2a(cotangent)
     pre_part = width_split(tokens_all, w_in, False)
     act_all = hidden_panel(jax.nn.gelu(pre_part, approximate=False).astype(jnp.bfloat16))
     dact_part = width_split(upstream_all, w_out, True)

time: 418 us -> 261 us (0.62)
  waiting for transfers between devices: 350 us -> 136 us
  blocking collectives: 0 us -> 37.6 us
  starting transfers between devices: 7.05 us -> 20.9 us
    reduce_scatter x4 -> x2, waiting for transfers between devices: 196 us -> 54.6 us  [width_split(): lax.psum_scatter(term.astype(jnp.bfloat16), 'col', scatter_dimension=0, t...]
    all_gather x2 -> x1, waiting for transfers between devices: 89.6 us -> 12.5 us  [token_panel(): return lax.all_gather(local_rows, 'row', axis=0, tiled=True)]
    all_to_all x0 -> x1, blocking collectives: none -> 37.6 us  [token_panel_a2a(): lax.all_to_all(copies, 'row', split_axis=0, concat_axis=0, tiled=True)]
    all_to_all x0 -> x2, starting transfers between devices: none -> 12.1 us  [unit_sum(): lax.all_to_all(pieces, 'row', split_axis=0, concat_axis=0, tiled=True)]
    all_to_all x0 -> x2, waiting for transfers between devices: none -> 9.4 us  [unit_sum(): lax.all_to_all(pieces, 'row', split_axis=0, concat_axis=0, tiled=True)]
    all_gather x2, waiting for transfers between devices: 62.1 us -> 55.2 us  [hidden_panel(): return lax.all_gather(local_rows, 'col', axis=0, tiled=True)]
  transfers between devices with their start and end apart: 9 -> 8, of which waited for: 8 -> 8; matrix products, arithmetic and copies ran while one was open for 10% -> 17% of each run, Pallas kernels for 0% -> 0%
where the time goes in v1:
time: 261 us; the launch traced here: 260 us
  waiting for transfers between devices  136 us (52%)
  blocking collectives  37.6 us (14%)
  matrix products  35.4 us (14%)
  starting transfers between devices  20.9 us (8%)
  between operations  15.7 us (6%)
  other arithmetic  8.13 us (3%)
  local copies, waits for them, and re-layouts  6.64 us (3%)
    all_gather x2, waiting for transfers between devices, hidden_panel(): return lax.all_gather(local_rows, 'col', axis=0, tiled=True)  55.2 us
    reduce_scatter x2, waiting for transfers between devices, width_split(): lax.psum_scatter(term.astype(jnp.bfloat16), 'col', scatter_dimension=0, t...  54.6 us
    all_to_all x1, blocking collectives, token_panel_a2a(): lax.all_to_all(copies, 'row', split_axis=0, concat_axis=0, tiled=True)  37.6 us
    all_gather x1, waiting for transfers between devices, token_panel(): return lax.all_gather(local_rows, 'row', axis=0, tiled=True)  12.5 us
    all_to_all x2, starting transfers between devices, unit_sum(): lax.all_to_all(pieces, 'row', split_axis=0, concat_axis=0, tiled=True)  12.1 us
    dot_general x2, matrix products, contract_last(): lax.dot_general(left, right, (((1,), (1,)), ((), ())), preferred_element_...  10.5 us
    all_to_all x2, waiting for transfers between devices, unit_sum(): lax.all_to_all(pieces, 'row', split_axis=0, concat_axis=0, tiled=True)  9.4 us
    all_to_all x1, starting transfers between devices, local(): lax.all_to_all(block_rows, 'col', split_axis=0, concat_axis=1, tiled=True)  8.57 us
  transfers between devices with their start and end apart: 8, of which 8 were waited for; matrix products, arithmetic and copies ran while one was open for 17% of the time, Pallas kernels for 0%

profile of v1, /device:TPU:1, one launch (start us, length us, event | category | flops | bytes accessed | tf_op | source)
XLA Modules:
  0.0 260.2 jit_solution(16874489885100301524)
XLA Ops:
  8.8 1.1 broadcast_in_dim.2
  9.9 37.6 %all_to_all.38 = bf16[16,128,512]{2,1,0:T(8,128)(2,1)S(1)} all-to-all(bf16[16,128,512]{2,1,0:T(8,128)(2,1)S(1)} %broadcast_in_dim.2), channel_id=1, replica_groups=mesh['row'=16,'col'=8] {'row'}, dimensions={0} | all-to-all | bytes 4194304 | tf_op jit(solution)/shard_map/all_to_all | solution.py:21
  47.5 1.4 copy-done.1
  48.9 4.3 %convolution_convert_fusion = bf16[2048,1024]{1,0:T(8,128)(2,1)} fusion(bf16[2048,512]{1,0:T(8,128)(2,1)S(1)} %bitcast.21, bf16[1024,512]{1,0:T(8,128)(2,1)S(1)} %copy-done), kind=kOutput, calls=%fused_computation.2 | convolution fusion | flops 2149580800 | bytes 7340032 | tf_op jit(solution)/shard_map/dot_general | solution.py:29
  53.3 12.5 %all-gather.4.cloned.1.call-done = bf16[2048,512]{1,0:T(8,128)(2,1)} async-done(((bf16[128,512]{1,0:T(8,128)(2,1)}), bf16[2048,512]{1,0:T(8,128)(2,1)}) %all-gather.4.cloned.1.call-update) | async-done | bytes 2097168 | tf_op jit(solution)/shard_map/all_gather | solution.py:14
  65.8 5.9 %convolution_convert_fusion.1 = bf16[2048,1024]{1,0:T(8,128)(2,1)} fusion(bf16[2048,512]{1,0:T(8,128)(2,1)} %all-gather.4.cloned.1.call-done, bf16[512,1024]{1,0:T(8,128)(2,1)S(1)} %copy-done.4), kind=kOutput, calls=%fused_computation.3 | convolution fusion | flops 2149580800 | bytes 7340032 | tf_op jit(solution)/shard_map/dot_general | solution.py:38
  71.9 15.8 %reduce-scatter.5.cloned.1.call-done = bf16[256,1024]{1,0:T(8,128)(2,1)} async-done(((bf16[2048,1024]{1,0:T(8,128)(2,1)}), bf16[256,1024]{1,0:T(8,128)(2,1)}) %reduce-scatter.5.cloned.1.call-update) | async-done | bytes 524304 | tf_op jit(solution)/shard_map/reduce_scatter | solution.py:39
  87.7 38.8 %reduce-scatter.3.cloned.1.call-done = bf16[256,1024]{1,0:T(8,128)(2,1)} async-done(((bf16[2048,1024]{1,0:T(8,128)(2,1)}), bf16[256,1024]{1,0:T(8,128)(2,1)}) %reduce-scatter.3.cloned.1.call-update) | async-done | bytes 524304 | tf_op jit(solution)/shard_map/reduce_scatter | solution.py:39
  126.4 4.6 %fusion.38 = (bf16[256,1024]{1,0:T(8,128)(2,1)}, bf16[256,1024]{1,0:T(8,128)(2,1)}) fusion(bf16[256,1024]{1,0:T(8,128)(2,1)} %reduce-scatter.3.cloned.1.call-done, bf16[256,1024]{1,0:T(8,128)(2,1)} %reduce-scatter.5.cloned.1.call-done), kind=kLoop, calls=%fused_computation.52 | loop fusion | flops 20185088 | bytes 2097152 | tf_op jit(solution)/shard_map/convert_element_type | solution.py:61
  131.8 33.5 %all-gather.6.cloned.1.call-done = bf16[2048,1024]{1,0:T(8,128)(2,1)} async-done(((bf16[256,1024]{1,0:T(8,128)(2,1)}), bf16[2048,1024]{1,0:T(8,128)(2,1)}) %all-gather.6.cloned.1.call-update) | async-done | bytes 4194320 | tf_op jit(solution)/shard_map/all_gather | solution.py:25
  165.3 5.8 %convolution_convert_fusion.3 = bf16[2048,512]{1,0:T(8,128)(2,1)} fusion(bf16[2048,1024]{1,0:T(8,128)(2,1)} %all-gather.6.cloned.1.call-done, bf16[1024,512]{1,0:T(8,128)(2,1)S(1)} %copy-done), kind=kOutput, calls=%fused_computation.5 | convolution fusion | flops 2148532224 | bytes 7340032 | tf_op jit(solution)/shard_map/dot_general | solution.py:49
  171.1 6.7 %all-to-all-start = ((bf16[16,128,512]{2,1,0:T(8,128)(2,1)}), bf16[16,128,512]{2,1,0:T(8,128)(2,1)S(1)}, u32[]{:S(2)}, u32[]{:S(2)}) async-start(bf16[16,128,512]{2,1,0:T(8,128)(2,1)} %bitcast.24), calls=%async_computation.1 | async-start | bytes 4194304 | tf_op jit(solution)/shard_map/all_to_all | solution.py:51
  177.9 21.7 %all-gather.8.cloned.1.call-done = bf16[2048,1024]{1,0:T(8,128)(2,1)} async-done(((bf16[256,1024]{1,0:T(8,128)(2,1)}), bf16[2048,1024]{1,0:T(8,128)(2,1)}) %all-gather.8.cloned.1.call-update) | async-done | bytes 4194320 | tf_op jit(solution)/shard_map/all_gather | solution.py:25
  199.5 6.2 %convolution_convert_fusion.2 = bf16[2048,512]{1,0:T(8,128)(2,1)} fusion(bf16[2048,1024]{1,0:T(8,128)(2,1)} %all-gather.8.cloned.1.call-done, bf16[512,1024]{1,0:T(8,128)(2,1)} %param.5), kind=kOutput, calls=%fused_computation.4 | convolution fusion | flops 2148532224 | bytes 7340032 | tf_op jit(solution)/shard_map/dot_general | solution.py:29
  205.7 1.4 all-to-all-done
  207.1 5.4 %all-to-all-start.3 = ((bf16[16,128,512]{2,1,0:T(8,128)(2,1)}), bf16[16,128,512]{2,1,0:T(8,128)(2,1)}, u32[]{:S(2)}, u32[]{:S(2)}) async-start(bf16[16,128,512]{2,1,0:T(8,128)(2,1)} %bitcast.23), calls=%async_computation.5 | async-start | bytes 4194304 | tf_op jit(solution)/shard_map/all_to_all | solution.py:51
  212.5 6.6 %convolution_bitcast_fusion = f32[512,1024]{0,1:T(8,128)} fusion(bf16[2048,1024]{1,0:T(8,128)(2,1)} %all-gather.8.cloned.1.call-done, bf16[2048,512]{1,0:T(8,128)(2,1)} %all-gather.4.cloned.1.call-done), kind=kOutput, calls=%fused_computation.12 | convolution fusion | flops 2147483648 | bytes 8388608 | tf_op jit(solution)/shard_map/dot_general | solution.py:68
  219.0 2.9 %copy.12 = f32[512,1024]{1,0:T(8,128)} copy(f32[512,1024]{0,1:T(8,128)} %convolution_bitcast_fusion) | data formatting | bytes 4194304
  221.9 6.5 %fusion.39 = f32[1024,512]{1,0:T(8,128)} fusion(bf16[2048,1024]{1,0:T(8,128)(2,1)} %all-gather.6.cloned.1.call-done, bf16[2048,512]{1,0:T(8,128)(2,1)} %bitcast.22), kind=kOutput, calls=%fused_computation.55 | convolution fusion | flops 2147483648 | bytes 8388608 | tf_op jit(solution)/shard_map/dot_general | solution.py:65
  230.0 8.0 %all-to-all-done.3 = bf16[16,128,512]{2,1,0:T(8,128)(2,1)} async-done(((bf16[16,128,512]{2,1,0:T(8,128)(2,1)}), bf16[16,128,512]{2,1,0:T(8,128)(2,1)}, u32[]{:S(2)}, u32[]{:S(2)}) %all-to-all-start.3) | async-done | bytes 2097184 | tf_op jit(solution)/shard_map/all_to_all | solution.py:51
  238.1 8.6 %all-to-all-start.1 = ((bf16[8,16,512]{2,1,0:T(8,128)(2,1)}), bf16[8,16,512]{2,1,0:T(8,128)(2,1)S(1)}, u32[]{:S(2)}, u32[]{:S(2)}) async-start(bf16[8,16,512]{2,1,0:T(8,128)(2,1)} %bitcast.1), calls=%async_computation.2 | async-start | bytes 262144 | tf_op jit(solution)/shard_map/all_to_all | solution.py:64
  246.7 1.9 convert_reduce_fusion
  248.6 0.7 add_convert_fusion
  249.3 2.7 %all-to-all-done.1 = bf16[8,16,512]{2,1,0:T(8,128)(2,1)S(1)} async-done(((bf16[8,16,512]{2,1,0:T(8,128)(2,1)}), bf16[8,16,512]{2,1,0:T(8,128)(2,1)S(1)}, u32[]{:S(2)}, u32[]{:S(2)}) %all-to-all-start.1) | async-done | bytes 131104 | tf_op jit(solution)/shard_map/all_to_all | solution.py:64
  (22 shorter events, 3.9 us)
Async XLA Ops:
  8.0 40.9 %copy-start = (bf16[1024,512]{1,0:T(8,128)(2,1)S(1)}, bf16[1024,512]{1,0:T(8,128)(2,1)}, u32[]{:S(2)}) copy-start(bf16[1024,512]{1,0:T(8,128)(2,1)} %param.6) | copy-start | bytes 3145732
  8.0 57.8 %all-gather.4.cloned.1.call-start = ((), (), s32[]{:S(2)}) async-start(), calls=%async_computation.6 | async-start | bytes 2228224 | tf_op jit(solution)/shard_map/all_gather | solution.py:14
  8.7 78.9 %reduce-scatter.5.cloned.1.call-start = ((), (), s32[]{:S(2)}) async-start(), calls=%async_computation.9 | async-start | bytes 4718592 | tf_op jit(solution)/shard_map/reduce_scatter | solution.py:39
  47.5 1.4 copy-start.1
  53.2 12.6 %copy-start.4 = (bf16[512,1024]{1,0:T(8,128)(2,1)S(1)}, bf16[512,1024]{1,0:T(8,128)(2,1)}, u32[]{:S(2)}) copy-start(bf16[512,1024]{1,0:T(8,128)(2,1)} %param.5) | copy-start | bytes 3145732
  53.3 73.2 %reduce-scatter.3.cloned.1.call-start = ((), (), s32[]{:S(2)}) async-start(), calls=%async_computation.7 | async-start | bytes 4718592 | tf_op jit(solution)/shard_map/reduce_scatter | solution.py:39
  71.8 93.5 %all-gather.6.cloned.1.call-start = ((), (), s32[]{:S(2)}) async-start(), calls=%async_computation.8 | async-start | bytes 4718592 | tf_op jit(solution)/shard_map/all_gather | solution.py:25
  131.0 68.5 %all-gather.8.cloned.1.call-start = ((), (), s32[]{:S(2)}) async-start(), calls=%async_computation.10 | async-start | bytes 4718592 | tf_op jit(solution)/shard_map/all_gather | solution.py:25
  171.1 35.9 %all-to-all-start = ((bf16[16,128,512]{2,1,0:T(8,128)(2,1)}), bf16[16,128,512]{2,1,0:T(8,128)(2,1)S(1)}, u32[]{:S(2)}, u32[]{:S(2)}) async-start(bf16[16,128,512]{2,1,0:T(8,128)(2,1)} %bitcast.24), calls=%async_computation.1 | async-start | bytes 4194304 | tf_op jit(solution)/shard_map/all_to_all | solution.py:51
  207.1 31.0 %all-to-all-start.3 = ((bf16[16,128,512]{2,1,0:T(8,128)(2,1)}), bf16[16,128,512]{2,1,0:T(8,128)(2,1)}, u32[]{:S(2)}, u32[]{:S(2)}) async-start(bf16[16,128,512]{2,1,0:T(8,128)(2,1)} %bitcast.23), calls=%async_computation.5 | async-start | bytes 4194304 | tf_op jit(solution)/shard_map/all_to_all | solution.py:51
  228.5 0.9 copy-start.3
  229.4 19.2 %copy-start.2 = (bf16[128,512]{1,0:T(8,128)(2,1)S(1)}, bf16[128,512]{1,0:T(8,128)(2,1)}, u32[]{:S(2)}) copy-start(bf16[128,512]{1,0:T(8,128)(2,1)} %param.7) | copy-start | bytes 393220
  238.1 13.9 %all-to-all-start.1 = ((bf16[8,16,512]{2,1,0:T(8,128)(2,1)}), bf16[8,16,512]{2,1,0:T(8,128)(2,1)S(1)}, u32[]{:S(2)}, u32[]{:S(2)}) async-start(bf16[8,16,512]{2,1,0:T(8,128)(2,1)} %bitcast.1), calls=%async_computation.2 | async-start | bytes 262144 | tf_op jit(solution)/shard_map/all_to_all | solution.py:64
Sparse Core Ops, SparseCore 0:
  11.0 54.8 all-gather.3
Sparse Core Ops, SparseCore 1:
  53.4 34.3 reduce-scatter.4
  89.9 36.4 reduce-scatter.2
  131.1 34.1 all-gather.5
  167.6 31.9 all-gather.7

commit v2 on v1

--- a/solution.py
+++ b/solution.py
@@ -23,6 +23,24 @@
 
 def hidden_panel(local_rows):
     return lax.all_gather(local_rows, "col", axis=0, tiled=True)
+
+
+def hidden_panel_a2a(local_rows):
+    n = lax.axis_size("col")
+    copies = jnp.broadcast_to(local_rows[None], (n,) + local_rows.shape)
+    copies = copies.reshape(n * local_rows.shape[0], local_rows.shape[1])
+    return lax.all_to_all(copies, "col", split_axis=0, concat_axis=0, tiled=True)
+
+
+def width_split_a2a(left_all, right, transposed):
+    n = lax.axis_size("col")
+    if transposed:
+        term = contract_last(left_all, right)
+    else:
+        term = jnp.dot(left_all, right, preferred_element_type=jnp.float32)
+    pieces = term.astype(jnp.bfloat16).reshape(n, term.shape[0] // n, term.shape[1])
+    pieces = lax.all_to_all(pieces, "col", split_axis=0, concat_axis=0, tiled=True)
+    return jnp.sum(pieces.astype(jnp.float32), axis=0)
 
 
 def contract_last(left, right):
@@ -53,12 +71,14 @@
 
 
 def local(tokens, w_in, w_out, cotangent):
-    tokens_all = token_panel(tokens)
-    upstream_all = token_panel_a2a(cotangent)
+    both_all = token_panel_a2a(jnp.stack([tokens, cotangent], axis=1).reshape(2 * tokens.shape[0], tokens.shape[1]))
+    both_all = both_all.reshape(-1, 2, tokens.shape[1])
+    tokens_all = both_all[:, 0]
+    upstream_all = both_all[:, 1]
     pre_part = width_split(tokens_all, w_in, False)
     act_all = hidden_panel(jax.nn.gelu(pre_part, approximate=False).astype(jnp.bfloat16))
-    dact_part = width_split(upstream_all, w_out, True)
-    dpre_all = hidden_panel((dact_part * gelu_grad(pre_part)).astype(jnp.bfloat16))
+    dact_part = width_split_a2a(upstream_all, w_out, True)
+    dpre_all = hidden_panel_a2a((dact_part * gelu_grad(pre_part)).astype(jnp.bfloat16))
     mixed = unit_sum(act_all, w_out, False)
     block_rows = (tokens.astype(jnp.float32) + mixed).astype(jnp.bfloat16)
     block_out = lax.all_to_all(block_rows, "col", split_axis=0, concat_axis=1, tiled=True)

time: 261 us -> 336 us (1.29)
  blocking collectives: 37.6 us -> 199 us
  waiting for transfers between devices: 136 us -> 36.5 us
  local copies, waits for them, and re-layouts: 6.64 us -> 22 us
    all_to_all x0 -> x2, blocking collectives: none -> 141 us  [the longest x1 72 us: width_split_a2a(): lax.all_to_all(pieces, 'col', split_axis=0, concat_axis=0, tiled=True)]
    all_gather x2 -> x1, waiting for transfers between devices: 55.2 us -> 0.02 us  [hidden_panel(): return lax.all_gather(local_rows, 'col', axis=0, tiled=True)]
    reduce_scatter x2 -> x1, waiting for transfers between devices: 54.6 us -> 0.02 us  [width_split(): lax.psum_scatter(term.astype(jnp.bfloat16), 'col', scatter_dimension=0, t...]
    all_to_all x2, waiting for transfers between devices: 9.4 us -> 36.5 us  [unit_sum(): lax.all_to_all(pieces, 'row', split_axis=0, concat_axis=0, tiled=True)]
    all_to_all x1, blocking collectives: 37.6 us -> 57.7 us  [token_panel_a2a(): lax.all_to_all(copies, 'row', split_axis=0, concat_axis=0, tiled=True)]
    all_gather x1 -> x0, waiting for transfers between devices: 12.5 us -> none  [token_panel(): return lax.all_gather(local_rows, 'row', axis=0, tiled=True)]
    slice x0 -> x1, local copies, waits for them, and re-layouts: none -> 9.63 us  [local(): upstream_all = both_all[:, 1]]
    reshape x0 -> x1, local copies, waits for them, and re-layouts: none -> 7.26 us  [local(): both_all = both_all.reshape(-1, 2, tokens.shape[1])]
  transfers between devices with their start and end apart: 8 -> 5, of which waited for: 8 -> 2; matrix products, arithmetic and copies ran while one was open for 17% -> 9% of each run, Pallas kernels for 0% -> 0%
where the time goes in v2:
time: 336 us
  blocking collectives  199 us (59%)
  waiting for transfers between devices  36.5 us (11%)
  matrix products  33.1 us (10%)
  local copies, waits for them, and re-layouts  22 us (7%)
  starting transfers between devices  21.2 us (6%)
  between operations  14.2 us (4%)
  other arithmetic  9.9 us (3%)
    all_to_all x1, blocking collectives, width_split_a2a(): lax.all_to_all(pieces, 'col', split_axis=0, concat_axis=0, tiled=True)  72 us
    all_to_all x1, blocking collectives, hidden_panel_a2a(): lax.all_to_all(copies, 'col', split_axis=0, concat_axis=0, tiled=True)  69 us
    all_to_all x1, blocking collectives, token_panel_a2a(): lax.all_to_all(copies, 'row', split_axis=0, concat_axis=0, tiled=True)  57.7 us
    all_to_all x2, waiting for transfers between devices, unit_sum(): lax.all_to_all(pieces, 'row', split_axis=0, concat_axis=0, tiled=True)  36.5 us
    all_to_all x2, starting transfers between devices, unit_sum(): lax.all_to_all(pieces, 'row', split_axis=0, concat_axis=0, tiled=True)  11.9 us
    slice x1, local copies, waits for them, and re-layouts, local(): upstream_all = both_all[:, 1]  9.63 us
    all_to_all x1, starting transfers between devices, local(): lax.all_to_all(block_rows, 'col', split_axis=0, concat_axis=1, tiled=True)  9.16 us
    dot_general x2, matrix products, contract_last(): lax.dot_general(left, right, (((1,), (1,)), ((), ())), preferred_element_...  8.34 us
  transfers between devices with their start and end apart: 5, of which 2 were waited for; matrix products, arithmetic and copies ran while one was open for 9% of the time, Pallas kernels for 0%

profile of v2, /device:TPU:1, one launch (start us, length us, event | category | flops | bytes accessed | tf_op | source)
XLA Modules:
  0.0 335.7 jit_solution(2800088632536888944)
XLA Ops:
  7.2 1.1 pad_maximum_fusion
  9.1 57.7 %all_to_all.49 = bf16[16,256,512]{2,1,0:T(8,128)(2,1)} all-to-all(bf16[16,256,512]{2,1,0:T(8,128)(2,1)S(1)} %broadcast_in_dim.14), channel_id=1, replica_groups=mesh['row'=16,'col'=8] {'row'}, dimensions={0} | all-to-all | bytes 8388608 | tf_op jit(solution)/shard_map/all_to_all | solution.py:21
  66.8 7.3 %reshape.34 = bf16[2048,2,512]{2,1,0:T(2,128)(2,1)} reshape(bf16[16,256,512]{2,1,0:T(8,128)(2,1)} %all_to_all.49) | data formatting | bytes 8388608 | tf_op jit(solution)/shard_map/reshape | solution.py:75
  74.1 9.6 %fusion.49 = (bf16[2048,1,512]{2,1,0:T(2,128)(2,1)}, bf16[2048,1,512]{2,1,0:T(2,128)(2,1)S(1)}) fusion(bf16[2048,2,512]{2,1,0:T(2,128)(2,1)} %reshape.34), kind=kLoop, calls=%fused_computation.66 | loop fusion | bytes 8388608 | tf_op jit(solution)/shard_map/slice | solution.py:77
  83.7 2.0 copy-done.2
  85.7 4.3 %convolution_convert_fusion.1 = bf16[2048,1024]{1,0:T(8,128)(2,1)} fusion(bf16[512,1024]{1,0:T(8,128)(2,1)S(1)} %copy-done, bf16[2048,1,512]{2,1,0:T(2,128)(2,1)S(1)} %get-tuple-element.5), kind=kOutput, calls=%fused_computation.4 | convolution fusion | flops 2149580800 | bytes 7340032 | tf_op jit(solution)/shard_map/dot_general | solution.py:56
  90.1 1.1 copy-done.5
  91.2 4.6 %convolution_convert_fusion = bf16[2048,1024]{1,0:T(8,128)(2,1)S(1)} fusion(bf16[1024,512]{1,0:T(8,128)(2,1)S(1)} %copy-done.5, bf16[2048,1,512]{2,1,0:T(2,128)(2,1)} %get-tuple-element.4), kind=kOutput, calls=%fused_computation.3 | convolution fusion | flops 2149580800 | bytes 7340032 | tf_op jit(solution)/shard_map/dot_general | solution.py:47
  95.8 72.0 %all_to_all.50 = bf16[8,256,1024]{2,1,0:T(8,128)(2,1)S(1)} all-to-all(bf16[8,256,1024]{2,1,0:T(8,128)(2,1)S(1)} %bitcast.30), channel_id=1, replica_groups=mesh['row'=16,'col'=8] {'col'}, dimensions={0} | all-to-all | bytes 8388608 | tf_op jit(solution)/shard_map/all_to_all | solution.py:42
  167.8 0.9 convert_reduce_fusion
  168.7 4.4 %fusion.44 = (bf16[256,1024]{1,0:T(8,128)(2,1)S(1)}, bf16[256,1024]{1,0:T(8,128)(2,1)}) fusion(f32[256,1024]{1,0:T(8,128)S(1)} %convert_reduce_fusion, bf16[256,1024]{1,0:T(8,128)(2,1)} %reduce-scatter.2.cloned.1.call-done), kind=kLoop, calls=%fused_computation.58 | loop fusion | flops 19922944 | bytes 2621440 | tf_op jit(solution)/shard_map/convert_element_type | solution.py:81
  173.7 69.0 %all_to_all.51 = bf16[8,256,1024]{2,1,0:T(8,128)(2,1)S(1)} all-to-all(bf16[8,256,1024]{2,1,0:T(8,128)(2,1)S(1)} %broadcast_in_dim.15), channel_id=1, replica_groups=mesh['row'=16,'col'=8] {'col'}, dimensions={0} | all-to-all | bytes 8388608 | tf_op jit(solution)/shard_map/all_to_all | solution.py:32
  242.7 3.8 %convolution_convert_fusion.2 = bf16[2048,512]{1,0:T(8,128)(2,1)} fusion(bf16[2048,1024]{1,0:T(8,128)(2,1)S(1)} %bitcast.28, bf16[512,1024]{1,0:T(8,128)(2,1)S(1)} %copy-done), kind=kOutput, calls=%fused_computation.5 | convolution fusion | flops 2148532224 | bytes 7340032 | tf_op jit(solution)/shard_map/dot_general | solution.py:47
  246.5 6.1 %all-to-all-start.5 = ((bf16[16,128,512]{2,1,0:T(8,128)(2,1)}), bf16[16,128,512]{2,1,0:T(8,128)(2,1)S(1)}, u32[]{:S(2)}, u32[]{:S(2)}) async-start(bf16[16,128,512]{2,1,0:T(8,128)(2,1)} %bitcast.32), calls=%async_computation.6 | async-start | bytes 4194304 | tf_op jit(solution)/shard_map/all_to_all | solution.py:69
  252.6 6.1 %convolution_convert_fusion.3 = bf16[2048,512]{1,0:T(8,128)(2,1)} fusion(bf16[2048,1024]{1,0:T(8,128)(2,1)} %all-gather.2.cloned.1.call-done, bf16[1024,512]{1,0:T(8,128)(2,1)} %param.6), kind=kOutput, calls=%fused_computation.6 | convolution fusion | flops 2148532224 | bytes 7340032 | tf_op jit(solution)/shard_map/dot_general | solution.py:67
  258.8 19.6 %all-to-all-done.5 = bf16[16,128,512]{2,1,0:T(8,128)(2,1)S(1)} async-done(((bf16[16,128,512]{2,1,0:T(8,128)(2,1)}), bf16[16,128,512]{2,1,0:T(8,128)(2,1)S(1)}, u32[]{:S(2)}, u32[]{:S(2)}) %all-to-all-start.5) | async-done | bytes 2097184 | tf_op jit(solution)/shard_map/all_to_all | solution.py:69
  278.4 5.8 %all-to-all-start.1 = ((bf16[16,128,512]{2,1,0:T(8,128)(2,1)}), bf16[16,128,512]{2,1,0:T(8,128)(2,1)}, u32[]{:S(2)}, u32[]{:S(2)}) async-start(bf16[16,128,512]{2,1,0:T(8,128)(2,1)} %bitcast.31), calls=%async_computation.2 | async-start | bytes 4194304 | tf_op jit(solution)/shard_map/all_to_all | solution.py:69
  284.2 7.2 %fusion.3 = f32[512,1024]{1,0:T(8,128)} fusion(bf16[2048,1024]{1,0:T(8,128)(2,1)} %bitcast.29, bf16[2048,1,512]{2,1,0:T(2,128)(2,1)} %copy-done.2), kind=kOutput, calls=%fused_computation.16 | convolution fusion | flops 2147483648 | bytes 8388608 | tf_op jit(solution)/shard_map/dot_general | solution.py:88
  291.7 0.7 add_convert_fusion
  292.4 16.9 %all-to-all-done.1 = bf16[16,128,512]{2,1,0:T(8,128)(2,1)} async-done(((bf16[16,128,512]{2,1,0:T(8,128)(2,1)}), bf16[16,128,512]{2,1,0:T(8,128)(2,1)}, u32[]{:S(2)}, u32[]{:S(2)}) %all-to-all-start.1) | async-done | bytes 2097184 | tf_op jit(solution)/shard_map/all_to_all | solution.py:69
  309.2 1.9 convert_reduce_fusion.2
  311.2 0.7 add_convert_fusion.1
  311.8 9.2 %all-to-all-start.2 = ((bf16[8,16,512]{2,1,0:T(8,128)(2,1)}), bf16[8,16,512]{2,1,0:T(8,128)(2,1)S(1)}, u32[]{:S(2)}, u32[]{:S(2)}) async-start(bf16[8,16,512]{2,1,0:T(8,128)(2,1)} %bitcast.3), calls=%async_computation.3 | async-start | bytes 262144 | tf_op jit(solution)/shard_map/all_to_all | solution.py:84
  321.0 7.2 %fusion = f32[1024,512]{1,0:T(8,128)} fusion(bf16[2048,1024]{1,0:T(8,128)(2,1)} %all-gather.2.cloned.1.call-done, bf16[2048,1,512]{2,1,0:T(2,128)(2,1)} %get-tuple-element.4), kind=kOutput, calls=%fused_computation.13 | convolution fusion | flops 2147483648 | bytes 8388608 | tf_op jit(solution)/shard_map/dot_general | solution.py:85
  (23 shorter events, 2.4 us)
Async XLA Ops:
  7.2 78.5 %copy-start = (bf16[512,1024]{1,0:T(8,128)(2,1)S(1)}, bf16[512,1024]{1,0:T(8,128)(2,1)}, u32[]{:S(2)}) copy-start(bf16[512,1024]{1,0:T(8,128)(2,1)} %param.5) | copy-start | bytes 3145732
  7.2 161.5 %reduce-scatter.2.cloned.1.call-start = ((), (), s32[]{:S(2)}) async-start(), calls=%async_computation.7 | async-start | bytes 4718592 | tf_op jit(solution)/shard_map/reduce_scatter | solution.py:57
  83.7 2.0 copy-start.2
  90.0 1.2 copy-start.5
  90.0 162.6 %all-gather.2.cloned.1.call-start = ((), (), s32[]{:S(2)}) async-start(), calls=%async_computation.8 | async-start | bytes 4718592 | tf_op jit(solution)/shard_map/all_gather | solution.py:25
  242.7 3.8 %copy-start.1 = (bf16[8,256,1024]{2,1,0:T(8,128)(2,1)}, bf16[8,256,1024]{2,1,0:T(8,128)(2,1)S(1)}, u32[]{:S(2)}) copy-start(bf16[8,256,1024]{2,1,0:T(8,128)(2,1)S(1)} %all_to_all.51) | copy-start | bytes 12582916
  246.5 31.9 %all-to-all-start.5 = ((bf16[16,128,512]{2,1,0:T(8,128)(2,1)}), bf16[16,128,512]{2,1,0:T(8,128)(2,1)S(1)}, u32[]{:S(2)}, u32[]{:S(2)}) async-start(bf16[16,128,512]{2,1,0:T(8,128)(2,1)} %bitcast.32), calls=%async_computation.6 | async-start | bytes 4194304 | tf_op jit(solution)/shard_map/all_to_all | solution.py:69
  278.4 30.9 %all-to-all-start.1 = ((bf16[16,128,512]{2,1,0:T(8,128)(2,1)}), bf16[16,128,512]{2,1,0:T(8,128)(2,1)}, u32[]{:S(2)}, u32[]{:S(2)}) async-start(bf16[16,128,512]{2,1,0:T(8,128)(2,1)} %bitcast.31), calls=%async_computation.2 | async-start | bytes 4194304 | tf_op jit(solution)/shard_map/all_to_all | solution.py:69
  284.2 7.5 %copy-start.3 = (bf16[128,512]{1,0:T(8,128)(2,1)S(1)}, bf16[128,512]{1,0:T(8,128)(2,1)}, u32[]{:S(2)}) copy-start(bf16[128,512]{1,0:T(8,128)(2,1)} %param.7) | copy-start | bytes 393220
  291.4 19.8 %copy-start.4 = (bf16[128,512]{1,0:T(8,128)(2,1)S(1)}, bf16[128,512]{1,0:T(8,128)(2,1)}, u32[]{:S(2)}) copy-start(bf16[128,512]{1,0:T(8,128)(2,1)} %param.4) | copy-start | bytes 393220
  311.8 16.3 %all-to-all-start.2 = ((bf16[8,16,512]{2,1,0:T(8,128)(2,1)}), bf16[8,16,512]{2,1,0:T(8,128)(2,1)S(1)}, u32[]{:S(2)}, u32[]{:S(2)}) async-start(bf16[8,16,512]{2,1,0:T(8,128)(2,1)} %bitcast.3), calls=%async_computation.3 | async-start | bytes 262144 | tf_op jit(solution)/shard_map/all_to_all | solution.py:84
Sparse Core Ops, SparseCore 0:
  90.1 72.6 reduce-scatter.1
  173.2 65.1 all-gather.1

commit v3 on v1

--- a/solution.py
+++ b/solution.py
@@ -2,6 +2,163 @@
 import jax.numpy as jnp
 from jax import lax
 from jax.sharding import PartitionSpec as P
+import functools
+from jax.experimental import pallas as pl
+from jax.experimental.pallas import tpu as pltpu
+
+MESH = pl.DeviceIdType.MESH
+
+
+def _col_ids(nx):
+    me = lax.axis_index("col")
+    x = me // 2
+    k = me % 2
+    d = 1 - 2 * k
+    nxt = lax.rem(x + nx + d, nx)
+    prv = lax.rem(x + nx - d, nx)
+    return x, k, d, nxt, prv
+
+
+def _greet(row, k, x, nxt, prv):
+    barrier = pltpu.get_barrier_semaphore()
+    for peer in (2 * x + 1 - k, 2 * nxt + k, 2 * prv + k):
+        pl.semaphore_signal(barrier, inc=1, device_id=(row, peer), device_id_type=MESH)
+    pl.semaphore_wait(barrier, 3)
+
+
+def _rs_kernel(nx, narr, *refs):
+    parts = refs[:narr]
+    outs = refs[narr:2 * narr]
+    recv1, vsum, sendbuf, recv2, s1, r1, s2, r2 = refs[2 * narr:]
+    row = lax.axis_index("row")
+    x, k, d, nxt, prv = _col_ids(nx)
+    _greet(row, k, x, nxt, prv)
+    partner = (row, 2 * x + 1 - k)
+    nextdev = (row, 2 * nxt + k)
+    first = []
+    for a in range(narr):
+        for i in range(nx):
+            cp = pltpu.make_async_remote_copy(
+                src_ref=parts[a].at[2 * i + 1 - k], dst_ref=recv1.at[a, i],
+                send_sem=s1.at[a, i], recv_sem=r1.at[a, i],
+                device_id=partner, device_id_type=MESH)
+            cp.start()
+            first.append(cp)
+    for cp in first:
+        cp.wait()
+    for a in range(narr):
+        for i in range(nx):
+            vsum[a, i] = parts[a][2 * i + k].astype(jnp.float32) + recv1[a, i].astype(jnp.float32)
+    ring = []
+    for step in range(nx - 1):
+        for a in range(narr):
+            src_idx = lax.rem(x + 4 * nx - d * (step + 1), nx)
+            if step == 0:
+                sendbuf[a, step] = vsum[a, src_idx].astype(sendbuf.dtype)
+            else:
+                prevcp = ring[(step - 1) * narr + a]
+                prevcp.wait_recv()
+                sendbuf[a, step] = (recv2[a, step - 1].astype(jnp.float32) + vsum[a, src_idx]).astype(sendbuf.dtype)
+            cp = pltpu.make_async_remote_copy(
+                src_ref=sendbuf.at[a, step], dst_ref=recv2.at[a, step],
+                send_sem=s2.at[a, step], recv_sem=r2.at[a, step],
+                device_id=nextdev, device_id_type=MESH)
+            cp.start()
+            ring.append(cp)
+    for a in range(narr):
+        last = ring[(nx - 2) * narr + a]
+        last.wait_recv()
+        outs[a][...] = recv2[a, nx - 2].astype(jnp.float32) + vsum[a, x]
+    for cp in ring:
+        cp.wait_send()
+
+
+def col_reduce_scatter(arrays, cid):
+    n = lax.axis_size("col")
+    nx = n // 2
+    narr = len(arrays)
+    rows = arrays[0].shape[0] // n
+    cols = arrays[0].shape[1]
+    parts = [a.reshape(n, rows, cols) for a in arrays]
+    return pl.pallas_call(
+        functools.partial(_rs_kernel, nx, narr),
+        out_shape=[jax.ShapeDtypeStruct((rows, cols), jnp.float32)] * narr,
+        in_specs=[pl.BlockSpec(memory_space=pltpu.VMEM)] * narr,
+        out_specs=[pl.BlockSpec(memory_space=pltpu.VMEM)] * narr,
+        scratch_shapes=[
+            pltpu.VMEM((narr, nx, rows, cols), jnp.bfloat16),
+            pltpu.VMEM((narr, nx, rows, cols), jnp.float32),
+            pltpu.VMEM((narr, nx - 1, rows, cols), jnp.bfloat16),
+            pltpu.VMEM((narr, nx - 1, rows, cols), jnp.bfloat16),
+            pltpu.SemaphoreType.DMA((narr, nx)),
+            pltpu.SemaphoreType.DMA((narr, nx)),
+            pltpu.SemaphoreType.DMA((narr, nx - 1)),
+            pltpu.SemaphoreType.DMA((narr, nx - 1)),
+        ],
+        compiler_params=pltpu.CompilerParams(collective_id=cid, has_side_effects=True,
+                                             vmem_limit_bytes=64 * 1024 * 1024),
+    )(*parts)
+
+
+def _ag_kernel(nx, narr, *refs):
+    chunks = refs[:narr]
+    outs = refs[narr:2 * narr]
+    sr, rr, sc, rc = refs[2 * narr:]
+    row = lax.axis_index("row")
+    x, k, d, nxt, prv = _col_ids(nx)
+    _greet(row, k, x, nxt, prv)
+    me = 2 * x + k
+    partner = (row, 2 * x + 1 - k)
+    nextdev = (row, 2 * nxt + k)
+    for a in range(narr):
+        outs[a][me] = chunks[a][...]
+    ring, core = [], []
+    for step in range(nx):
+        for a in range(narr):
+            src_x = lax.rem(x + 4 * nx - d * step, nx)
+            slot = 2 * src_x + k
+            if step > 0:
+                ring[(step - 1) * narr + a].wait_recv()
+            src = chunks[a] if step == 0 else outs[a].at[slot]
+            if step < nx - 1:
+                cp = pltpu.make_async_remote_copy(
+                    src_ref=src, dst_ref=outs[a].at[slot],
+                    send_sem=sr.at[a, step], recv_sem=rr.at[a, step],
+                    device_id=nextdev, device_id_type=MESH)
+                cp.start()
+                ring.append(cp)
+            cc = pltpu.make_async_remote_copy(
+                src_ref=src, dst_ref=outs[a].at[slot],
+                send_sem=sc.at[a, step], recv_sem=rc.at[a, step],
+                device_id=partner, device_id_type=MESH)
+            cc.start()
+            core.append(cc)
+    for cp in ring:
+        cp.wait_send()
+    for cc in core:
+        cc.wait()
+
+
+def col_all_gather(arrays, cid):
+    n = lax.axis_size("col")
+    nx = n // 2
+    narr = len(arrays)
+    rows, cols = arrays[0].shape
+    outs = pl.pallas_call(
+        functools.partial(_ag_kernel, nx, narr),
+        out_shape=[jax.ShapeDtypeStruct((n, rows, cols), arrays[0].dtype)] * narr,
+        in_specs=[pl.BlockSpec(memory_space=pltpu.VMEM)] * narr,
+        out_specs=[pl.BlockSpec(memory_space=pltpu.VMEM)] * narr,
+        scratch_shapes=[
+            pltpu.SemaphoreType.DMA((narr, nx)),
+            pltpu.SemaphoreType.DMA((narr, nx)),
+            pltpu.SemaphoreType.DMA((narr, nx)),
+            pltpu.SemaphoreType.DMA((narr, nx)),
+        ],
+        compiler_params=pltpu.CompilerParams(collective_id=cid, has_side_effects=True,
+                                             vmem_limit_bytes=64 * 1024 * 1024),
+    )(*arrays)
+    return [o.reshape(n * rows, cols) for o in outs]
 
 
 def gelu_grad(value):
@@ -55,10 +212,12 @@
 def local(tokens, w_in, w_out, cotangent):
     tokens_all = token_panel(tokens)
     upstream_all = token_panel_a2a(cotangent)
-    pre_part = width_split(tokens_all, w_in, False)
-    act_all = hidden_panel(jax.nn.gelu(pre_part, approximate=False).astype(jnp.bfloat16))
-    dact_part = width_split(upstream_all, w_out, True)
-    dpre_all = hidden_panel((dact_part * gelu_grad(pre_part)).astype(jnp.bfloat16))
+    pre_term = jnp.dot(tokens_all, w_in, preferred_element_type=jnp.float32).astype(jnp.bfloat16)
+    dact_term = contract_last(upstream_all, w_out).astype(jnp.bfloat16)
+    pre_part, dact_part = col_reduce_scatter([pre_term, dact_term], 1)
+    act = jax.nn.gelu(pre_part, approximate=False).astype(jnp.bfloat16)
+    dpre = (dact_part * gelu_grad(pre_part)).astype(jnp.bfloat16)
+    act_all, dpre_all = col_all_gather([act, dpre], 2)
     mixed = unit_sum(act_all, w_out, False)
     block_rows = (tokens.astype(jnp.float32) + mixed).astype(jnp.bfloat16)
     block_out = lax.all_to_all(block_rows, "col", split_axis=0, concat_axis=1, tiled=True)

time: 261 us -> 268 us (1.027)
  Pallas kernels: 0 us -> 98.5 us
  waiting for transfers between devices: 136 us -> 48.6 us
    pallas_call x0 -> x2, Pallas kernels: none -> 98.5 us  [the longest x1 52.6 us: col_reduce_scatter(): pl.pallas_call(functools.partial(_rs_kernel, nx, narr), out_shape=[jax.Sh...]
    all_gather x2 -> x0, waiting for transfers between devices: 55.2 us -> none  [hidden_panel(): return lax.all_gather(local_rows, 'col', axis=0, tiled=True)]
    reduce_scatter x2 -> x0, waiting for transfers between devices: 54.6 us -> none  [width_split(): lax.psum_scatter(term.astype(jnp.bfloat16), 'col', scatter_dimension=0, t...]
    all_to_all x2, waiting for transfers between devices: 9.4 us -> 31.1 us  [unit_sum(): lax.all_to_all(pieces, 'row', split_axis=0, concat_axis=0, tiled=True)]
    unnamed x11 -> x17, local copies, waits for them, and re-layouts: 4.88 us -> 6.19 us
  transfers between devices with their start and end apart: 8 -> 4, of which waited for: 8 -> 4; matrix products, arithmetic and copies ran while one was open for 17% -> 11% of each run, Pallas kernels for 0% -> 0%
where the time goes in v3:
time: 268 us
  Pallas kernels  98.5 us (37%)
  waiting for transfers between devices  48.6 us (18%)
  blocking collectives  37.8 us (14%)
  matrix products  35.5 us (13%)
  starting transfers between devices  18.7 us (7%)
  between operations  14.1 us (5%)
  local copies, waits for them, and re-layouts  7.95 us (3%)
  other arithmetic  6.62 us (2%)
    pallas_call x1, Pallas kernels, col_reduce_scatter(): pl.pallas_call(functools.partial(_rs_kernel, nx, narr), out_shape=[jax.Sh...  52.6 us
    pallas_call x1, Pallas kernels, col_all_gather(): pl.pallas_call(functools.partial(_ag_kernel, nx, narr), out_shape=[jax.Sh...  46 us
    all_to_all x1, blocking collectives, token_panel_a2a(): lax.all_to_all(copies, 'row', split_axis=0, concat_axis=0, tiled=True)  37.8 us
    all_to_all x2, waiting for transfers between devices, unit_sum(): lax.all_to_all(pieces, 'row', split_axis=0, concat_axis=0, tiled=True)  31.1 us
    all_gather x1, waiting for transfers between devices, token_panel(): return lax.all_gather(local_rows, 'row', axis=0, tiled=True)  12.6 us
    dot_general x2, matrix products, contract_last(): lax.dot_general(left, right, (((1,), (1,)), ((), ())), preferred_element_...  10.2 us
    all_to_all x2, starting transfers between devices, unit_sum(): lax.all_to_all(pieces, 'row', split_axis=0, concat_axis=0, tiled=True)  10.2 us
    all_to_all x1, starting transfers between devices, local(): lax.all_to_all(block_rows, 'col', split_axis=0, concat_axis=1, tiled=True)  8.42 us
  transfers between devices with their start and end apart: 4, of which 4 were waited for; matrix products, arithmetic and copies ran while one was open for 11% of the time, Pallas kernels for 0%

profile of v3, /device:TPU:1, one launch (start us, length us, event | category | flops | bytes accessed | tf_op | source)
XLA Modules:
  0.0 267.8 jit_solution(6403003365305158926)
XLA Ops:
  7.2 0.7 all-gather.2.cloned.1.call-update
  7.9 1.1 broadcast_in_dim.2
  9.0 37.8 %all_to_all.38 = bf16[16,128,512]{2,1,0:T(8,128)(2,1)S(1)} all-to-all(bf16[16,128,512]{2,1,0:T(8,128)(2,1)S(1)} %broadcast_in_dim.2), channel_id=1, replica_groups=mesh['row'=16,'col'=8] {'row'}, dimensions={0} | all-to-all | bytes 4194304 | tf_op jit(solution)/shard_map/all_to_all | solution.py:178
  46.8 1.4 copy-done.2
  48.2 4.3 %convolution_convert_fusion = bf16[2048,1024]{1,0:T(8,128)(2,1)} fusion(bf16[2048,512]{1,0:T(8,128)(2,1)S(1)} %bitcast.25, bf16[1024,512]{1,0:T(8,128)(2,1)S(1)} %copy-done.5), kind=kOutput, calls=%fused_computation.2 | convolution fusion | flops 2149580800 | bytes 7340032 | tf_op jit(solution)/shard_map/dot_general | solution.py:186
  52.5 12.6 %all-gather.2.cloned.1.call-done = bf16[2048,512]{1,0:T(8,128)(2,1)} async-done(((bf16[128,512]{1,0:T(8,128)(2,1)}), bf16[2048,512]{1,0:T(8,128)(2,1)}) %all-gather.2.cloned.1.call-update) | async-done | bytes 2097168 | tf_op jit(solution)/shard_map/all_gather | solution.py:171
  65.1 5.9 %convolution_convert_fusion.1 = bf16[2048,1024]{1,0:T(8,128)(2,1)} fusion(bf16[2048,512]{1,0:T(8,128)(2,1)} %all-gather.2.cloned.1.call-done, bf16[512,1024]{1,0:T(8,128)(2,1)S(1)} %copy-done.6), kind=kOutput, calls=%fused_computation.3 | convolution fusion | flops 2149580800 | bytes 7340032 | tf_op jit(solution)/shard_map/dot_general | solution.py:215
  71.0 52.6 %shard_map.75 = (f32[256,1024]{1,0:T(8,128)}, f32[256,1024]{1,0:T(8,128)}) custom-call(bf16[8,256,1024]{2,1,0:T(8,128)(2,1)} %bitcast.32, bf16[8,256,1024]{2,1,0:T(8,128)(2,1)} %bitcast.31), custom_call_target="tpu_custom_call" | custom-call | tf_op jit(solution)/shard_map/pallas_call | solution.py:83
  123.5 4.7 %fusion.8 = (bf16[256,1024]{1,0:T(8,128)(2,1)}, bf16[256,1024]{1,0:T(8,128)(2,1)}) fusion(f32[256,1024]{1,0:T(8,128)} %get-tuple-element.9, f32[256,1024]{1,0:T(8,128)} %get-tuple-element.8), kind=kLoop, calls=%fused_computation.17 | loop fusion | flops 19660800 | bytes 3145728 | tf_op jit(solution)/shard_map/convert_element_type | solution.py:219
  128.2 46.0 %shard_map.76 = (bf16[8,256,1024]{2,1,0:T(8,128)(2,1)}, bf16[8,256,1024]{2,1,0:T(8,128)(2,1)}) custom-call(bf16[256,1024]{1,0:T(8,128)(2,1)} %get-tuple-element.25.refs_0_, bf16[256,1024]{1,0:T(8,128)(2,1)} %get-tuple-element.24.refs_1_), custom_call_target="tpu_custom_call" | custom-call | tf_op jit(solution)/shard_map/pallas_call | solution.py:147
  174.2 6.2 %convolution_convert_fusion.3 = bf16[2048,512]{1,0:T(8,128)(2,1)} fusion(bf16[2048,1024]{1,0:T(8,128)(2,1)} %bitcast.27, bf16[1024,512]{1,0:T(8,128)(2,1)} %param.6), kind=kOutput, calls=%fused_computation.5 | convolution fusion | flops 2148532224 | bytes 7340032 | tf_op jit(solution)/shard_map/dot_general | solution.py:206
  180.3 4.8 %all-to-all-start.1 = ((bf16[16,128,512]{2,1,0:T(8,128)(2,1)}), bf16[16,128,512]{2,1,0:T(8,128)(2,1)S(1)}, u32[]{:S(2)}, u32[]{:S(2)}) async-start(bf16[16,128,512]{2,1,0:T(8,128)(2,1)} %bitcast.34), calls=%async_computation.1 | async-start | bytes 4194304 | tf_op jit(solution)/shard_map/all_to_all | solution.py:208
  185.2 5.9 %convolution_convert_fusion.2 = bf16[2048,512]{1,0:T(8,128)(2,1)} fusion(bf16[2048,1024]{1,0:T(8,128)(2,1)} %bitcast.29, bf16[512,1024]{1,0:T(8,128)(2,1)S(1)} %copy-done.7), kind=kOutput, calls=%fused_computation.4 | convolution fusion | flops 2148532224 | bytes 7340032 | tf_op jit(solution)/shard_map/dot_general | solution.py:186
  191.1 23.2 %all-to-all-done.1 = bf16[16,128,512]{2,1,0:T(8,128)(2,1)S(1)} async-done(((bf16[16,128,512]{2,1,0:T(8,128)(2,1)}), bf16[16,128,512]{2,1,0:T(8,128)(2,1)S(1)}, u32[]{:S(2)}, u32[]{:S(2)}) %all-to-all-start.1) | async-done | bytes 2097184 | tf_op jit(solution)/shard_map/all_to_all | solution.py:208
  214.3 1.3 copy-done
  215.6 5.4 %all-to-all-start.3 = ((bf16[16,128,512]{2,1,0:T(8,128)(2,1)}), bf16[16,128,512]{2,1,0:T(8,128)(2,1)S(1)}, u32[]{:S(2)}, u32[]{:S(2)}) async-start(bf16[16,128,512]{2,1,0:T(8,128)(2,1)} %bitcast.33), calls=%async_computation.3 | async-start | bytes 4194304 | tf_op jit(solution)/shard_map/all_to_all | solution.py:208
  221.0 6.6 %convolution_bitcast_fusion = f32[512,1024]{0,1:T(8,128)} fusion(bf16[2048,1024]{1,0:T(8,128)(2,1)} %bitcast.30, bf16[2048,512]{1,0:T(8,128)(2,1)} %all-gather.2.cloned.1.call-done), kind=kOutput, calls=%fused_computation.6 | convolution fusion | flops 2147483648 | bytes 8388608 | tf_op jit(solution)/shard_map/dot_general | solution.py:227
  227.6 2.9 %copy.12 = f32[512,1024]{1,0:T(8,128)} copy(f32[512,1024]{0,1:T(8,128)} %convolution_bitcast_fusion) | data formatting | bytes 4194304
  230.4 6.7 %fusion.16 = f32[1024,512]{1,0:T(8,128)} fusion(bf16[2048,1024]{1,0:T(8,128)(2,1)} %bitcast.28, bf16[2048,512]{1,0:T(8,128)(2,1)} %bitcast.26), kind=kOutput, calls=%fused_computation.35 | convolution fusion | flops 2147483648 | bytes 8388608 | tf_op jit(solution)/shard_map/dot_general | solution.py:224
  238.0 0.7 add_convert_fusion.1
  238.7 7.8 %all-to-all-done.3 = bf16[16,128,512]{2,1,0:T(8,128)(2,1)S(1)} async-done(((bf16[16,128,512]{2,1,0:T(8,128)(2,1)}), bf16[16,128,512]{2,1,0:T(8,128)(2,1)S(1)}, u32[]{:S(2)}, u32[]{:S(2)}) %all-to-all-start.3) | async-done | bytes 2097184 | tf_op jit(solution)/shard_map/all_to_all | solution.py:208
  246.6 8.4 %all-to-all-start.2 = ((bf16[8,16,512]{2,1,0:T(8,128)(2,1)}), bf16[8,16,512]{2,1,0:T(8,128)(2,1)S(1)}, u32[]{:S(2)}, u32[]{:S(2)}) async-start(bf16[8,16,512]{2,1,0:T(8,128)(2,1)} %bitcast.5), calls=%async_computation.2 | async-start | bytes 262144 | tf_op jit(solution)/shard_map/all_to_all | solution.py:223
  255.3 0.7 add_convert_fusion
  256.0 4.3 %all-to-all-done.2 = bf16[8,16,512]{2,1,0:T(8,128)(2,1)S(1)} async-done(((bf16[8,16,512]{2,1,0:T(8,128)(2,1)}), bf16[8,16,512]{2,1,0:T(8,128)(2,1)S(1)}, u32[]{:S(2)}, u32[]{:S(2)}) %all-to-all-start.2) | async-done | bytes 131104 | tf_op jit(solution)/shard_map/all_to_all | solution.py:223
  (18 shorter events, 1.9 us)
Async XLA Ops:
  7.2 57.9 %all-gather.2.cloned.1.call-start = ((), (), s32[]{:S(2)}) async-start(), calls=%async_computation.4 | async-start | bytes 2228224 | tf_op jit(solution)/shard_map/all_gather | solution.py:171
  9.0 39.2 %copy-start.5 = (bf16[1024,512]{1,0:T(8,128)(2,1)S(1)}, bf16[1024,512]{1,0:T(8,128)(2,1)}, u32[]{:S(2)}) copy-start(bf16[1024,512]{1,0:T(8,128)(2,1)} %param.6) | copy-start | bytes 3145732
  46.8 1.4 copy-start.2
  48.2 16.9 %copy-start.6 = (bf16[512,1024]{1,0:T(8,128)(2,1)S(1)}, bf16[512,1024]{1,0:T(8,128)(2,1)}, u32[]{:S(2)}) copy-start(bf16[512,1024]{1,0:T(8,128)(2,1)} %param.5) | copy-start | bytes 3145732
  180.3 4.8 %copy-start.7 = (bf16[512,1024]{1,0:T(8,128)(2,1)S(1)}, bf16[512,1024]{1,0:T(8,128)(2,1)}, u32[]{:S(2)}) copy-start(bf16[512,1024]{1,0:T(8,128)(2,1)} %param.5) | copy-start | bytes 3145732
  180.3 33.9 %all-to-all-start.1 = ((bf16[16,128,512]{2,1,0:T(8,128)(2,1)}), bf16[16,128,512]{2,1,0:T(8,128)(2,1)S(1)}, u32[]{:S(2)}, u32[]{:S(2)}) async-start(bf16[16,128,512]{2,1,0:T(8,128)(2,1)} %bitcast.34), calls=%async_computation.1 | async-start | bytes 4194304 | tf_op jit(solution)/shard_map/all_to_all | solution.py:208
  214.3 1.3 copy-start
  215.6 31.0 %all-to-all-start.3 = ((bf16[16,128,512]{2,1,0:T(8,128)(2,1)}), bf16[16,128,512]{2,1,0:T(8,128)(2,1)S(1)}, u32[]{:S(2)}, u32[]{:S(2)}) async-start(bf16[16,128,512]{2,1,0:T(8,128)(2,1)} %bitcast.33), calls=%async_computation.3 | async-start | bytes 4194304 | tf_op jit(solution)/shard_map/all_to_all | solution.py:208
  230.4 6.7 %copy-start.1 = (bf16[16,128,512]{2,1,0:T(8,128)(2,1)S(1)}, bf16[16,128,512]{2,1,0:T(8,128)(2,1)}, u32[]{:S(2)}) copy-start(bf16[16,128,512]{2,1,0:T(8,128)(2,1)} %copy-done) | copy-start | bytes 6291460
  237.1 0.9 copy-start.4
  238.0 17.2 %copy-start.3 = (bf16[128,512]{1,0:T(8,128)(2,1)S(1)}, bf16[128,512]{1,0:T(8,128)(2,1)}, u32[]{:S(2)}) copy-start(bf16[128,512]{1,0:T(8,128)(2,1)} %param.7) | copy-start | bytes 393220
  246.6 13.7 %all-to-all-start.2 = ((bf16[8,16,512]{2,1,0:T(8,128)(2,1)}), bf16[8,16,512]{2,1,0:T(8,128)(2,1)S(1)}, u32[]{:S(2)}, u32[]{:S(2)}) async-start(bf16[8,16,512]{2,1,0:T(8,128)(2,1)} %bitcast.5), calls=%async_computation.2 | async-start | bytes 262144 | tf_op jit(solution)/shard_map/all_to_all | solution.py:223
Sparse Core Ops, SparseCore 0:
  10.1 54.8 all-gather.1

commit v4 on v3

--- a/solution.py
+++ b/solution.py
@@ -210,15 +210,17 @@
 
 
 def local(tokens, w_in, w_out, cotangent):
-    tokens_all = token_panel(tokens)
-    upstream_all = token_panel_a2a(cotangent)
+    tokens_all = token_panel_a2a(tokens)
+    upstream_all = token_panel(cotangent)
     pre_term = jnp.dot(tokens_all, w_in, preferred_element_type=jnp.float32).astype(jnp.bfloat16)
+    (pre_part,) = col_reduce_scatter([pre_term], 1)
+    act = jax.nn.gelu(pre_part, approximate=False).astype(jnp.bfloat16)
+    (act_all,) = col_all_gather([act], 2)
+    mixed = unit_sum(act_all, w_out, False)
     dact_term = contract_last(upstream_all, w_out).astype(jnp.bfloat16)
-    pre_part, dact_part = col_reduce_scatter([pre_term, dact_term], 1)
-    act = jax.nn.gelu(pre_part, approximate=False).astype(jnp.bfloat16)
+    (dact_part,) = col_reduce_scatter([dact_term], 3)
     dpre = (dact_part * gelu_grad(pre_part)).astype(jnp.bfloat16)
-    act_all, dpre_all = col_all_gather([act, dpre], 2)
-    mixed = unit_sum(act_all, w_out, False)
+    (dpre_all,) = col_all_gather([dpre], 4)
     block_rows = (tokens.astype(jnp.float32) + mixed).astype(jnp.bfloat16)
     block_out = lax.all_to_all(block_rows, "col", split_axis=0, concat_axis=1, tiled=True)
     grad_out = lax.dot_general(

time: 268 us -> 268 us (level)
  Pallas kernels: 98.5 us -> 134 us
  waiting for transfers between devices: 48.6 us -> 15.5 us
  local copies, waits for them, and re-layouts: 7.95 us -> 4.67 us
    all_to_all x2, waiting for transfers between devices: 31.1 us -> 10.5 us  [unit_sum(): lax.all_to_all(pieces, 'row', split_axis=0, concat_axis=0, tiled=True)]
    pallas_call x1 -> x2, Pallas kernels: 46 us -> 64.4 us  [col_all_gather(): pl.pallas_call(functools.partial(_ag_kernel, nx, narr), out_shape=[jax.Sh...]
    pallas_call x1 -> x2, Pallas kernels: 52.6 us -> 69.2 us  [col_reduce_scatter(): pl.pallas_call(functools.partial(_rs_kernel, nx, narr), out_shape=[jax.Sh...]
    all_gather x1, waiting for transfers between devices: 12.6 us -> 0.02 us  [token_panel(): return lax.all_gather(local_rows, 'row', axis=0, tiled=True)]
    unnamed x17 -> x9, local copies, waits for them, and re-layouts: 6.19 us -> 2.9 us
  transfers between devices with their start and end apart: 4 -> 4, of which waited for: 4 -> 2; matrix products, arithmetic and copies ran while one was open for 11% -> 12% of each run, Pallas kernels for 0% -> 25%
where the time goes in v4:
time: 268 us; the launch traced here: 267 us
  Pallas kernels  134 us (50%)
  blocking collectives  37.8 us (14%)
  matrix products  35.9 us (13%)
  starting transfers between devices  17.3 us (6%)
  waiting for transfers between devices  15.5 us (6%)
  between operations  14.1 us (5%)
  other arithmetic  8.27 us (3%)
  local copies, waits for them, and re-layouts  4.67 us (2%)
    pallas_call x2, Pallas kernels, col_reduce_scatter(): pl.pallas_call(functools.partial(_rs_kernel, nx, narr), out_shape=[jax.Sh...  69.2 us
    pallas_call x2, Pallas kernels, col_all_gather(): pl.pallas_call(functools.partial(_ag_kernel, nx, narr), out_shape=[jax.Sh...  64.4 us
    all_to_all x1, blocking collectives, token_panel_a2a(): lax.all_to_all(copies, 'row', split_axis=0, concat_axis=0, tiled=True)  37.8 us
    dot_general x2, matrix products, contract_last(): lax.dot_general(left, right, (((1,), (1,)), ((), ())), preferred_element_...  12.4 us
    all_to_all x2, starting transfers between devices, unit_sum(): lax.all_to_all(pieces, 'row', split_axis=0, concat_axis=0, tiled=True)  11.3 us
    all_to_all x2, waiting for transfers between devices, unit_sum(): lax.all_to_all(pieces, 'row', split_axis=0, concat_axis=0, tiled=True)  10.5 us
    dot_general x1, matrix products, local(): lax.dot_general(act_all, upstream_all, (((0,), (0,)), ((), ())), preferre...  6.55 us
    dot_general x1, matrix products, local(): lax.dot_general(tokens_all, dpre_all, (((0,), (0,)), ((), ())), preferred...  6.55 us
  transfers between devices with their start and end apart: 4, of which 2 were waited for; matrix products, arithmetic and copies ran while one was open for 12% of the time, Pallas kernels for 25%

profile of v4, /device:TPU:1, one launch (start us, length us, event | category | flops | bytes accessed | tf_op | source)
XLA Modules:
  0.0 267.1 jit_solution(15973538416832560167)
XLA Ops:
  7.2 0.7 all-gather.2.cloned.1.call-update
  7.9 1.1 broadcast_in_dim.2
  9.0 37.8 %all_to_all.38 = bf16[16,128,512]{2,1,0:T(8,128)(2,1)S(1)} all-to-all(bf16[16,128,512]{2,1,0:T(8,128)(2,1)S(1)} %broadcast_in_dim.2), channel_id=1, replica_groups=mesh['row'=16,'col'=8] {'row'}, dimensions={0} | all-to-all | bytes 4194304 | tf_op jit(solution)/shard_map/all_to_all | solution.py:178
  46.8 4.3 %convolution_convert_fusion.1 = bf16[2048,1024]{1,0:T(8,128)(2,1)} fusion(bf16[2048,512]{1,0:T(8,128)(2,1)S(1)} %bitcast.29, bf16[512,1024]{1,0:T(8,128)(2,1)S(1)} %copy-done.3), kind=kOutput, calls=%fused_computation.3 | convolution fusion | flops 2149580800 | bytes 7340032 | tf_op jit(solution)/shard_map/dot_general | solution.py:215
  51.1 34.6 %shard_map.75 = f32[256,1024]{1,0:T(8,128)} custom-call(bf16[8,256,1024]{2,1,0:T(8,128)(2,1)} %bitcast.31), custom_call_target="tpu_custom_call" | custom-call | tf_op jit(solution)/shard_map/pallas_call | solution.py:83
  85.8 6.2 %convolution_convert_fusion = bf16[2048,1024]{1,0:T(8,128)(2,1)} fusion(bf16[2048,512]{1,0:T(8,128)(2,1)} %all-gather.2.cloned.1.call-done, bf16[1024,512]{1,0:T(8,128)(2,1)} %param.6), kind=kOutput, calls=%fused_computation.2 | convolution fusion | flops 2149580800 | bytes 7340032 | tf_op jit(solution)/shard_map/dot_general | solution.py:186
  91.9 34.6 %shard_map.77 = f32[256,1024]{1,0:T(8,128)} custom-call(bf16[8,256,1024]{2,1,0:T(8,128)(2,1)} %bitcast.32), custom_call_target="tpu_custom_call" | custom-call | tf_op jit(solution)/shard_map/pallas_call | solution.py:83
  126.5 4.7 %fusion.8 = (bf16[256,1024]{1,0:T(8,128)(2,1)}, bf16[256,1024]{1,0:T(8,128)(2,1)}) fusion(f32[256,1024]{1,0:T(8,128)} %shard_map.77, f32[256,1024]{1,0:T(8,128)} %shard_map.75), kind=kLoop, calls=%fused_computation.17 | loop fusion | flops 19660800 | bytes 3145728 | tf_op jit(solution)/shard_map/convert_element_type | solution.py:222
  131.2 33.4 %shard_map.76 = bf16[8,256,1024]{2,1,0:T(8,128)(2,1)} custom-call(bf16[256,1024]{1,0:T(8,128)(2,1)} %get-tuple-element.17.refs_0_), custom_call_target="tpu_custom_call" | custom-call | tf_op jit(solution)/shard_map/pallas_call | solution.py:147
  164.6 6.2 %convolution_convert_fusion.3 = bf16[2048,512]{1,0:T(8,128)(2,1)} fusion(bf16[2048,1024]{1,0:T(8,128)(2,1)} %bitcast.25, bf16[1024,512]{1,0:T(8,128)(2,1)} %param.6), kind=kOutput, calls=%fused_computation.5 | convolution fusion | flops 2148532224 | bytes 7340032 | tf_op jit(solution)/shard_map/dot_general | solution.py:206
  170.8 4.6 %all-to-all-start.1 = ((bf16[16,128,512]{2,1,0:T(8,128)(2,1)}), bf16[16,128,512]{2,1,0:T(8,128)(2,1)}, u32[]{:S(2)}, u32[]{:S(2)}) async-start(bf16[16,128,512]{2,1,0:T(8,128)(2,1)} %bitcast.3), calls=%async_computation.1 | async-start | bytes 4194304 | tf_op jit(solution)/shard_map/all_to_all | solution.py:208
  175.4 30.9 %shard_map.78 = bf16[8,256,1024]{2,1,0:T(8,128)(2,1)} custom-call(bf16[256,1024]{1,0:T(8,128)(2,1)} %get-tuple-element.16.refs_0_), custom_call_target="tpu_custom_call" | custom-call | tf_op jit(solution)/shard_map/pallas_call | solution.py:147
  206.3 6.2 %convolution_convert_fusion.2 = bf16[2048,512]{1,0:T(8,128)(2,1)} fusion(bf16[2048,1024]{1,0:T(8,128)(2,1)} %bitcast.27, bf16[512,1024]{1,0:T(8,128)(2,1)} %param.5), kind=kOutput, calls=%fused_computation.4 | convolution fusion | flops 2148532224 | bytes 7340032 | tf_op jit(solution)/shard_map/dot_general | solution.py:186
  212.5 6.6 %all-to-all-start.3 = ((bf16[16,128,512]{2,1,0:T(8,128)(2,1)}), bf16[16,128,512]{2,1,0:T(8,128)(2,1)S(1)}, u32[]{:S(2)}, u32[]{:S(2)}) async-start(bf16[16,128,512]{2,1,0:T(8,128)(2,1)} %bitcast.33), calls=%async_computation.3 | async-start | bytes 4194304 | tf_op jit(solution)/shard_map/all_to_all | solution.py:208
  219.2 6.5 %convolution_bitcast_fusion = f32[512,1024]{0,1:T(8,128)} fusion(bf16[2048,1024]{1,0:T(8,128)(2,1)} %bitcast.28, bf16[2048,512]{1,0:T(8,128)(2,1)} %bitcast.30), kind=kOutput, calls=%fused_computation.6 | convolution fusion | flops 2147483648 | bytes 8388608 | tf_op jit(solution)/shard_map/dot_general | solution.py:229
  225.7 2.9 %copy.12 = f32[512,1024]{1,0:T(8,128)} copy(f32[512,1024]{0,1:T(8,128)} %convolution_bitcast_fusion) | data formatting | bytes 4194304
  228.6 6.5 %fusion.16 = f32[1024,512]{1,0:T(8,128)} fusion(bf16[2048,1024]{1,0:T(8,128)(2,1)} %bitcast.26, bf16[2048,512]{1,0:T(8,128)(2,1)} %all-gather.2.cloned.1.call-done), kind=kOutput, calls=%fused_computation.35 | convolution fusion | flops 2147483648 | bytes 8388608 | tf_op jit(solution)/shard_map/dot_general | solution.py:226
  235.2 1.9 convert_reduce_fusion.1
  237.1 0.7 add_convert_fusion.1
  237.8 10.5 %all-to-all-done.3 = bf16[16,128,512]{2,1,0:T(8,128)(2,1)S(1)} async-done(((bf16[16,128,512]{2,1,0:T(8,128)(2,1)}), bf16[16,128,512]{2,1,0:T(8,128)(2,1)S(1)}, u32[]{:S(2)}, u32[]{:S(2)}) %all-to-all-start.3) | async-done | bytes 2097184 | tf_op jit(solution)/shard_map/all_to_all | solution.py:208
  248.3 6.0 %all-to-all-start.2 = ((bf16[8,16,512]{2,1,0:T(8,128)(2,1)}), bf16[8,16,512]{2,1,0:T(8,128)(2,1)S(1)}, u32[]{:S(2)}, u32[]{:S(2)}) async-start(bf16[8,16,512]{2,1,0:T(8,128)(2,1)} %bitcast.4), calls=%async_computation.2 | async-start | bytes 262144 | tf_op jit(solution)/shard_map/all_to_all | solution.py:225
  254.6 0.7 add_convert_fusion
  255.3 4.3 %all-to-all-done.2 = bf16[8,16,512]{2,1,0:T(8,128)(2,1)S(1)} async-done(((bf16[8,16,512]{2,1,0:T(8,128)(2,1)}), bf16[8,16,512]{2,1,0:T(8,128)(2,1)S(1)}, u32[]{:S(2)}, u32[]{:S(2)}) %all-to-all-start.2) | async-done | bytes 131104 | tf_op jit(solution)/shard_map/all_to_all | solution.py:225
  259.6 0.7 copy.13
  (12 shorter events, 0.4 us)
Async XLA Ops:
  7.2 78.6 %all-gather.2.cloned.1.call-start = ((), (), s32[]{:S(2)}) async-start(), calls=%async_computation.4 | async-start | bytes 2228224 | tf_op jit(solution)/shard_map/all_gather | solution.py:171
  9.0 37.8 %copy-start.3 = (bf16[512,1024]{1,0:T(8,128)(2,1)S(1)}, bf16[512,1024]{1,0:T(8,128)(2,1)}, u32[]{:S(2)}) copy-start(bf16[512,1024]{1,0:T(8,128)(2,1)} %param.5) | copy-start | bytes 3145732
  46.8 4.3 %copy-start = (bf16[16,128,512]{2,1,0:T(8,128)(2,1)}, bf16[16,128,512]{2,1,0:T(8,128)(2,1)S(1)}, u32[]{:S(2)}) copy-start(bf16[16,128,512]{2,1,0:T(8,128)(2,1)S(1)} %all_to_all.38) | copy-start | bytes 6291460
  170.8 41.8 %all-to-all-start.1 = ((bf16[16,128,512]{2,1,0:T(8,128)(2,1)}), bf16[16,128,512]{2,1,0:T(8,128)(2,1)}, u32[]{:S(2)}, u32[]{:S(2)}) async-start(bf16[16,128,512]{2,1,0:T(8,128)(2,1)} %bitcast.3), calls=%async_computation.1 | async-start | bytes 4194304 | tf_op jit(solution)/shard_map/all_to_all | solution.py:208
  212.5 35.8 %all-to-all-start.3 = ((bf16[16,128,512]{2,1,0:T(8,128)(2,1)}), bf16[16,128,512]{2,1,0:T(8,128)(2,1)S(1)}, u32[]{:S(2)}, u32[]{:S(2)}) async-start(bf16[16,128,512]{2,1,0:T(8,128)(2,1)} %bitcast.33), calls=%async_computation.3 | async-start | bytes 4194304 | tf_op jit(solution)/shard_map/all_to_all | solution.py:208
  235.2 1.9 copy-start.1
  237.1 17.5 %copy-start.2 = (bf16[128,512]{1,0:T(8,128)(2,1)S(1)}, bf16[128,512]{1,0:T(8,128)(2,1)}, u32[]{:S(2)}) copy-start(bf16[128,512]{1,0:T(8,128)(2,1)} %param.7) | copy-start | bytes 393220
  248.3 11.3 %all-to-all-start.2 = ((bf16[8,16,512]{2,1,0:T(8,128)(2,1)}), bf16[8,16,512]{2,1,0:T(8,128)(2,1)S(1)}, u32[]{:S(2)}, u32[]{:S(2)}) async-start(bf16[8,16,512]{2,1,0:T(8,128)(2,1)} %bitcast.4), calls=%async_computation.2 | async-start | bytes 262144 | tf_op jit(solution)/shard_map/all_to_all | solution.py:225
Sparse Core Ops, SparseCore 0:
  10.1 54.8 all-gather.1

commit v5 on v3

--- a/solution.py
+++ b/solution.py
@@ -102,14 +102,21 @@
 
 def _ag_kernel(nx, narr, *refs):
     chunks = refs[:narr]
-    outs = refs[narr:2 * narr]
-    sr, rr, sc, rc = refs[2 * narr:]
+    weights = refs[narr:2 * narr]
+    outs = refs[2 * narr:3 * narr]
+    prods = refs[3 * narr:4 * narr]
+    sr, rr, sc, rc = refs[4 * narr:]
     row = lax.axis_index("row")
     x, k, d, nxt, prv = _col_ids(nx)
     _greet(row, k, x, nxt, prv)
     me = 2 * x + k
     partner = (row, 2 * x + 1 - k)
     nextdev = (row, 2 * nxt + k)
+
+    def product(a, slot):
+        prods[a][slot] = jnp.dot(outs[a][slot], weights[a][...],
+                                 preferred_element_type=jnp.float32).astype(prods[a].dtype)
+
     for a in range(narr):
         outs[a][me] = chunks[a][...]
     ring, core = [], []
@@ -133,22 +140,29 @@
                 device_id=partner, device_id_type=MESH)
             cc.start()
             core.append(cc)
+        for a in range(narr):
+            product(a, 2 * lax.rem(x + 4 * nx - d * step, nx) + k)
     for cp in ring:
         cp.wait_send()
-    for cc in core:
-        cc.wait()
-
-
-def col_all_gather(arrays, cid):
+    for step in range(nx):
+        for a in range(narr):
+            core[step * narr + a].wait()
+        for a in range(narr):
+            product(a, 2 * lax.rem(x + 4 * nx + d * step, nx) + 1 - k)
+
+
+def col_all_gather(arrays, weights, cid):
     n = lax.axis_size("col")
     nx = n // 2
     narr = len(arrays)
     rows, cols = arrays[0].shape
-    outs = pl.pallas_call(
+    width = weights[0].shape[1]
+    res = pl.pallas_call(
         functools.partial(_ag_kernel, nx, narr),
-        out_shape=[jax.ShapeDtypeStruct((n, rows, cols), arrays[0].dtype)] * narr,
-        in_specs=[pl.BlockSpec(memory_space=pltpu.VMEM)] * narr,
-        out_specs=[pl.BlockSpec(memory_space=pltpu.VMEM)] * narr,
+        out_shape=[jax.ShapeDtypeStruct((n, rows, cols), arrays[0].dtype)] * narr
+        + [jax.ShapeDtypeStruct((n, rows, width), jnp.bfloat16)] * narr,
+        in_specs=[pl.BlockSpec(memory_space=pltpu.VMEM)] * (2 * narr),
+        out_specs=[pl.BlockSpec(memory_space=pltpu.VMEM)] * (2 * narr),
         scratch_shapes=[
             pltpu.SemaphoreType.DMA((narr, nx)),
             pltpu.SemaphoreType.DMA((narr, nx)),
@@ -157,8 +171,10 @@
         ],
         compiler_params=pltpu.CompilerParams(collective_id=cid, has_side_effects=True,
                                              vmem_limit_bytes=64 * 1024 * 1024),
-    )(*arrays)
-    return [o.reshape(n * rows, cols) for o in outs]
+    )(*arrays, *weights)
+    gathered = [o.reshape(n * rows, cols) for o in res[:narr]]
+    products = [o.reshape(n * rows, width) for o in res[narr:]]
+    return gathered, products
 
 
 def gelu_grad(value):
@@ -209,6 +225,13 @@
     return jnp.sum(pieces.astype(jnp.float32), axis=0)
 
 
+def row_sum(term):
+    n = lax.axis_size("row")
+    pieces = term.reshape(n, term.shape[0] // n, term.shape[1])
+    pieces = lax.all_to_all(pieces, "row", split_axis=0, concat_axis=0, tiled=True)
+    return jnp.sum(pieces.astype(jnp.float32), axis=0)
+
+
 def local(tokens, w_in, w_out, cotangent):
     tokens_all = token_panel(tokens)
     upstream_all = token_panel_a2a(cotangent)
@@ -217,8 +240,8 @@
     pre_part, dact_part = col_reduce_scatter([pre_term, dact_term], 1)
     act = jax.nn.gelu(pre_part, approximate=False).astype(jnp.bfloat16)
     dpre = (dact_part * gelu_grad(pre_part)).astype(jnp.bfloat16)
-    act_all, dpre_all = col_all_gather([act, dpre], 2)
-    mixed = unit_sum(act_all, w_out, False)
+    (act_all, dpre_all), (mixed_term, back_term) = col_all_gather([act, dpre], [w_out, w_in.T], 2)
+    mixed = row_sum(mixed_term)
     block_rows = (tokens.astype(jnp.float32) + mixed).astype(jnp.bfloat16)
     block_out = lax.all_to_all(block_rows, "col", split_axis=0, concat_axis=1, tiled=True)
     grad_out = lax.dot_general(
@@ -227,7 +250,7 @@
     grad_in = lax.dot_general(
         tokens_all, dpre_all, (((0,), (0,)), ((), ())), preferred_element_type=jnp.float32
     )
-    back = unit_sum(dpre_all, w_in, True)
+    back = row_sum(back_term)
     grad_tokens = (cotangent.astype(jnp.float32) + back).astype(jnp.bfloat16)
     return (block_out, grad_tokens, grad_in, grad_out)
 

time: 268 us -> 266 us (level)
  matrix products: 35.5 us -> 23.7 us
  waiting for transfers between devices: 48.6 us -> 59.1 us
  blocking collectives: 37.8 us -> 30.8 us
  starting transfers between devices: 18.7 us -> 22 us
    all_to_all x1, blocking collectives: 37.8 us -> 30.8 us  [row_sum(): lax.all_to_all(pieces, 'row', split_axis=0, concat_axis=0, tiled=True)]
    all_gather x1, waiting for transfers between devices: 12.6 us -> 18.9 us  [token_panel(): return lax.all_gather(local_rows, 'row', axis=0, tiled=True)]
    dot_general x1 -> x0, matrix products: 6.15 us -> none  [unit_sum(): term = jnp.dot(left_all, right, preferred_element_type=jnp.float32)]
    dot_general x2 -> x1, matrix products: 10.2 us -> 4.34 us  [contract_last(): lax.dot_general(left, right, (((1,), (1,)), ((), ())), preferred_element_...]
    all_to_all x2, waiting for transfers between devices: 31.1 us -> 35.2 us  [the longest x1 27.6 us: token_panel_a2a(): lax.all_to_all(copies, 'row', split_axis=0, concat_axis=0, tiled=True)]
    unnamed x17 -> x12, local copies, waits for them, and re-layouts: 6.19 us -> 5.87 us
  transfers between devices with their start and end apart: 4 -> 4, of which waited for: 4 -> 4; matrix products, arithmetic and copies ran while one was open for 11% -> 10% of each run, Pallas kernels for 0% -> 0%
where the time goes in v5:
time: 266 us
  Pallas kernels  100 us (38%)
  waiting for transfers between devices  59.1 us (22%)
  blocking collectives  30.8 us (12%)
  matrix products  23.7 us (9%)
  starting transfers between devices  22 us (8%)
  between operations  14.1 us (5%)
  local copies, waits for them, and re-layouts  8.96 us (3%)
  other arithmetic  6.62 us (2%)
    pallas_call x1, Pallas kernels, col_reduce_scatter(): pl.pallas_call(functools.partial(_rs_kernel, nx, narr), out_shape=[jax.Sh...  52.6 us
    pallas_call x1, Pallas kernels, col_all_gather(): pl.pallas_call(functools.partial(_ag_kernel, nx, narr), out_shape=[jax.Sh...  47.9 us
    all_to_all x1, blocking collectives, row_sum(): lax.all_to_all(pieces, 'row', split_axis=0, concat_axis=0, tiled=True)  30.8 us
    all_to_all x1, waiting for transfers between devices, token_panel_a2a(): lax.all_to_all(copies, 'row', split_axis=0, concat_axis=0, tiled=True)  27.6 us
    all_gather x1, waiting for transfers between devices, token_panel(): return lax.all_gather(local_rows, 'row', axis=0, tiled=True)  18.9 us
    all_to_all x1, starting transfers between devices, local(): lax.all_to_all(block_rows, 'col', split_axis=0, concat_axis=1, tiled=True)  9.42 us
    all_to_all x1, starting transfers between devices, token_panel_a2a(): lax.all_to_all(copies, 'row', split_axis=0, concat_axis=0, tiled=True)  8.6 us
    all_to_all x1, waiting for transfers between devices, row_sum(): lax.all_to_all(pieces, 'row', split_axis=0, concat_axis=0, tiled=True)  7.58 us
  transfers between devices with their start and end apart: 4, of which 4 were waited for; matrix products, arithmetic and copies ran while one was open for 10% of the time, Pallas kernels for 0%

profile of v5, /device:TPU:1, one launch (start us, length us, event | category | flops | bytes accessed | tf_op | source)
XLA Modules:
  0.0 265.7 jit_solution(8448389595240698027)
XLA Ops:
  7.2 0.7 all-gather.2.cloned.1.call-update
  7.9 2.4 broadcast_in_dim.2
  10.3 8.6 %all-to-all-start = ((bf16[16,128,512]{2,1,0:T(8,128)(2,1)}), bf16[16,128,512]{2,1,0:T(8,128)(2,1)S(1)}, u32[]{:S(2)}, u32[]{:S(2)}) async-start(bf16[16,128,512]{2,1,0:T(8,128)(2,1)} %broadcast_in_dim.2), calls=%async_computation | async-start | bytes 4194304 | tf_op jit(solution)/shard_map/all_to_all | solution.py:194
  18.9 2.4 copy.13
  21.3 27.6 %all-to-all-done = bf16[16,128,512]{2,1,0:T(8,128)(2,1)S(1)} async-done(((bf16[16,128,512]{2,1,0:T(8,128)(2,1)}), bf16[16,128,512]{2,1,0:T(8,128)(2,1)S(1)}, u32[]{:S(2)}, u32[]{:S(2)}) %all-to-all-start) | async-done | bytes 2097184 | tf_op jit(solution)/shard_map/all_to_all | solution.py:194
  48.9 4.3 %convolution_convert_fusion = bf16[2048,1024]{1,0:T(8,128)(2,1)} fusion(bf16[2048,512]{1,0:T(8,128)(2,1)S(1)} %bitcast.22, bf16[1024,512]{1,0:T(8,128)(2,1)S(1)} %copy-done.2), kind=kOutput, calls=%fused_computation.2 | convolution fusion | flops 2149580800 | bytes 7340032 | tf_op jit(solution)/shard_map/dot_general | solution.py:202
  53.3 18.9 %all-gather.2.cloned.1.call-done = bf16[2048,512]{1,0:T(8,128)(2,1)} async-done(((bf16[128,512]{1,0:T(8,128)(2,1)}), bf16[2048,512]{1,0:T(8,128)(2,1)}) %all-gather.2.cloned.1.call-update) | async-done | bytes 2097168 | tf_op jit(solution)/shard_map/all_gather | solution.py:187
  72.2 6.2 %convolution_convert_fusion.1 = bf16[2048,1024]{1,0:T(8,128)(2,1)} fusion(bf16[2048,512]{1,0:T(8,128)(2,1)} %all-gather.2.cloned.1.call-done, bf16[512,1024]{1,0:T(8,128)(2,1)} %param.5), kind=kOutput, calls=%fused_computation.3 | convolution fusion | flops 2149580800 | bytes 7340032 | tf_op jit(solution)/shard_map/dot_general | solution.py:238
  78.3 52.6 %shard_map.75 = (f32[256,1024]{1,0:T(8,128)}, f32[256,1024]{1,0:T(8,128)}) custom-call(bf16[8,256,1024]{2,1,0:T(8,128)(2,1)} %bitcast.28, bf16[8,256,1024]{2,1,0:T(8,128)(2,1)} %bitcast.27), custom_call_target="tpu_custom_call" | custom-call | tf_op jit(solution)/shard_map/pallas_call | solution.py:83
  130.9 4.7 %fusion.8 = (bf16[256,1024]{1,0:T(8,128)(2,1)}, bf16[256,1024]{1,0:T(8,128)(2,1)}) fusion(f32[256,1024]{1,0:T(8,128)} %get-tuple-element.11, f32[256,1024]{1,0:T(8,128)} %get-tuple-element.10), kind=kLoop, calls=%fused_computation.15 | loop fusion | flops 19660800 | bytes 3145728 | tf_op jit(solution)/shard_map/convert_element_type | solution.py:242
  135.6 47.9 %shard_map.76 = (bf16[8,256,1024]{2,1,0:T(8,128)(2,1)}, bf16[8,256,1024]{2,1,0:T(8,128)(2,1)}, bf16[8,256,512]{2,1,0:T(8,128)(2,1)}, bf16[8,256,512]{2,1,0:T(8,128)(2,1)}) custom-call(bf16[256,1024]{1,0:T(8,128)(2,1)} %get-tuple-element.29.refs_0_, bf16[256,1024]{1,0:T(8,128)(2,1)} %get-tuple-element.28.refs_1_, bf16[1024,512]{1,0:T(8,128)(2,1)} %refs_2_.1, ...), custom_call_target="tpu_custom_call" | custom-call | tf_op jit(solution)/shard_map/pallas_call | solution.py:160
  183.5 30.8 %all_to_all.38 = bf16[16,128,512]{2,1,0:T(8,128)(2,1)} all-to-all(bf16[16,128,512]{2,1,0:T(8,128)(2,1)} %bitcast.30), channel_id=1, replica_groups=mesh['row'=16,'col'=8] {'row'}, dimensions={0} | all-to-all | bytes 4194304 | tf_op jit(solution)/shard_map/all_to_all | solution.py:231
  214.3 4.0 %all-to-all-start.3 = ((bf16[16,128,512]{2,1,0:T(8,128)(2,1)}), bf16[16,128,512]{2,1,0:T(8,128)(2,1)S(1)}, u32[]{:S(2)}, u32[]{:S(2)}) async-start(bf16[16,128,512]{2,1,0:T(8,128)(2,1)} %bitcast.29), calls=%async_computation.3 | async-start | bytes 4194304 | tf_op jit(solution)/shard_map/all_to_all | solution.py:231
  218.2 6.5 %convolution_bitcast_fusion = f32[512,1024]{0,1:T(8,128)} fusion(bf16[2048,1024]{1,0:T(8,128)(2,1)} %bitcast.26, bf16[2048,512]{1,0:T(8,128)(2,1)} %all-gather.2.cloned.1.call-done), kind=kOutput, calls=%fused_computation.4 | convolution fusion | flops 2147483648 | bytes 8388608 | tf_op jit(solution)/shard_map/dot_general | solution.py:250
  224.8 2.9 %copy.15 = f32[512,1024]{1,0:T(8,128)} copy(f32[512,1024]{0,1:T(8,128)} %convolution_bitcast_fusion) | data formatting | bytes 4194304
  227.7 6.7 %fusion.16 = f32[1024,512]{1,0:T(8,128)} fusion(bf16[2048,1024]{1,0:T(8,128)(2,1)} %bitcast.25, bf16[2048,512]{1,0:T(8,128)(2,1)} %bitcast.23), kind=kOutput, calls=%fused_computation.33 | convolution fusion | flops 2147483648 | bytes 8388608 | tf_op jit(solution)/shard_map/dot_general | solution.py:247
  234.4 0.3 convert_reduce_fusion.1
  234.6 0.6 copy-done.4
  235.3 0.7 add_convert_fusion.1
  235.9 7.6 %all-to-all-done.3 = bf16[16,128,512]{2,1,0:T(8,128)(2,1)S(1)} async-done(((bf16[16,128,512]{2,1,0:T(8,128)(2,1)}), bf16[16,128,512]{2,1,0:T(8,128)(2,1)S(1)}, u32[]{:S(2)}, u32[]{:S(2)}) %all-to-all-start.3) | async-done | bytes 2097184 | tf_op jit(solution)/shard_map/all_to_all | solution.py:231
  243.5 9.4 %all-to-all-start.2 = ((bf16[8,16,512]{2,1,0:T(8,128)(2,1)}), bf16[8,16,512]{2,1,0:T(8,128)(2,1)S(1)}, u32[]{:S(2)}, u32[]{:S(2)}) async-start(bf16[8,16,512]{2,1,0:T(8,128)(2,1)} %bitcast.5), calls=%async_computation.2 | async-start | bytes 262144 | tf_op jit(solution)/shard_map/all_to_all | solution.py:246
  253.2 0.7 add_convert_fusion
  253.9 4.3 %all-to-all-done.2 = bf16[8,16,512]{2,1,0:T(8,128)(2,1)S(1)} async-done(((bf16[8,16,512]{2,1,0:T(8,128)(2,1)}), bf16[8,16,512]{2,1,0:T(8,128)(2,1)S(1)}, u32[]{:S(2)}, u32[]{:S(2)}) %all-to-all-start.2) | async-done | bytes 131104 | tf_op jit(solution)/shard_map/all_to_all | solution.py:246
  258.2 0.7 copy.16
  (11 shorter events, 0.3 us)
Async XLA Ops:
  7.2 65.0 %all-gather.2.cloned.1.call-start = ((), (), s32[]{:S(2)}) async-start(), calls=%async_computation.4 | async-start | bytes 2228224 | tf_op jit(solution)/shard_map/all_gather | solution.py:187
  10.3 38.6 %all-to-all-start = ((bf16[16,128,512]{2,1,0:T(8,128)(2,1)}), bf16[16,128,512]{2,1,0:T(8,128)(2,1)S(1)}, u32[]{:S(2)}, u32[]{:S(2)}) async-start(bf16[16,128,512]{2,1,0:T(8,128)(2,1)} %broadcast_in_dim.2), calls=%async_computation | async-start | bytes 4194304 | tf_op jit(solution)/shard_map/all_to_all | solution.py:194
  18.9 30.0 %copy-start.2 = (bf16[1024,512]{1,0:T(8,128)(2,1)S(1)}, bf16[1024,512]{1,0:T(8,128)(2,1)}, u32[]{:S(2)}) copy-start(bf16[1024,512]{1,0:T(8,128)(2,1)} %refs_2_.1) | copy-start | bytes 3145732
  48.9 4.4 %copy-start.1 = (bf16[16,128,512]{2,1,0:T(8,128)(2,1)}, bf16[16,128,512]{2,1,0:T(8,128)(2,1)S(1)}, u32[]{:S(2)}) copy-start(bf16[16,128,512]{2,1,0:T(8,128)(2,1)S(1)} %all-to-all-done) | copy-start | bytes 6291460
  214.3 29.2 %all-to-all-start.3 = ((bf16[16,128,512]{2,1,0:T(8,128)(2,1)}), bf16[16,128,512]{2,1,0:T(8,128)(2,1)S(1)}, u32[]{:S(2)}, u32[]{:S(2)}) async-start(bf16[16,128,512]{2,1,0:T(8,128)(2,1)} %bitcast.29), calls=%async_computation.3 | async-start | bytes 4194304 | tf_op jit(solution)/shard_map/all_to_all | solution.py:231
  227.7 6.7 %copy-start = (bf16[16,128,512]{2,1,0:T(8,128)(2,1)S(1)}, bf16[16,128,512]{2,1,0:T(8,128)(2,1)}, u32[]{:S(2)}) copy-start(bf16[16,128,512]{2,1,0:T(8,128)(2,1)} %all_to_all.38) | copy-start | bytes 6291460
  234.4 0.9 copy-start.4
  235.3 18.0 %copy-start.3 = (bf16[128,512]{1,0:T(8,128)(2,1)S(1)}, bf16[128,512]{1,0:T(8,128)(2,1)}, u32[]{:S(2)}) copy-start(bf16[128,512]{1,0:T(8,128)(2,1)} %param.7) | copy-start | bytes 393220
  243.5 14.7 %all-to-all-start.2 = ((bf16[8,16,512]{2,1,0:T(8,128)(2,1)}), bf16[8,16,512]{2,1,0:T(8,128)(2,1)S(1)}, u32[]{:S(2)}, u32[]{:S(2)}) async-start(bf16[8,16,512]{2,1,0:T(8,128)(2,1)} %bitcast.5), calls=%async_computation.2 | async-start | bytes 262144 | tf_op jit(solution)/shard_map/all_to_all | solution.py:246
Sparse Core Ops, SparseCore 0:
  10.1 61.9 all-gather.1

commit v6 on v5

--- a/solution.py
+++ b/solution.py
@@ -104,8 +104,8 @@
     chunks = refs[:narr]
     weights = refs[narr:2 * narr]
     outs = refs[2 * narr:3 * narr]
-    prods = refs[3 * narr:4 * narr]
-    sr, rr, sc, rc = refs[4 * narr:]
+    prods = refs[3 * narr:3 * narr + 1]
+    sr, rr, sc, rc = refs[3 * narr + 1:]
     row = lax.axis_index("row")
     x, k, d, nxt, prv = _col_ids(nx)
     _greet(row, k, x, nxt, prv)
@@ -113,9 +113,12 @@
     partner = (row, 2 * x + 1 - k)
     nextdev = (row, 2 * nxt + k)
 
+    width = weights[0].shape[1]
+
     def product(a, slot):
-        prods[a][slot] = jnp.dot(outs[a][slot], weights[a][...],
-                                 preferred_element_type=jnp.float32).astype(prods[a].dtype)
+        prods[0][slot, :, a * width:(a + 1) * width] = jnp.dot(
+            outs[a][slot], weights[a][...], preferred_element_type=jnp.float32
+        ).astype(prods[0].dtype)
 
     for a in range(narr):
         outs[a][me] = chunks[a][...]
@@ -160,9 +163,9 @@
     res = pl.pallas_call(
         functools.partial(_ag_kernel, nx, narr),
         out_shape=[jax.ShapeDtypeStruct((n, rows, cols), arrays[0].dtype)] * narr
-        + [jax.ShapeDtypeStruct((n, rows, width), jnp.bfloat16)] * narr,
+        + [jax.ShapeDtypeStruct((n, rows, narr * width), jnp.bfloat16)],
         in_specs=[pl.BlockSpec(memory_space=pltpu.VMEM)] * (2 * narr),
-        out_specs=[pl.BlockSpec(memory_space=pltpu.VMEM)] * (2 * narr),
+        out_specs=[pl.BlockSpec(memory_space=pltpu.VMEM)] * (narr + 1),
         scratch_shapes=[
             pltpu.SemaphoreType.DMA((narr, nx)),
             pltpu.SemaphoreType.DMA((narr, nx)),
@@ -173,8 +176,7 @@
                                              vmem_limit_bytes=64 * 1024 * 1024),
     )(*arrays, *weights)
     gathered = [o.reshape(n * rows, cols) for o in res[:narr]]
-    products = [o.reshape(n * rows, width) for o in res[narr:]]
-    return gathered, products
+    return gathered, res[narr].reshape(n * rows, narr * width)
 
 
 def gelu_grad(value):
@@ -240,8 +242,9 @@
     pre_part, dact_part = col_reduce_scatter([pre_term, dact_term], 1)
     act = jax.nn.gelu(pre_part, approximate=False).astype(jnp.bfloat16)
     dpre = (dact_part * gelu_grad(pre_part)).astype(jnp.bfloat16)
-    (act_all, dpre_all), (mixed_term, back_term) = col_all_gather([act, dpre], [w_out, w_in.T], 2)
-    mixed = row_sum(mixed_term)
+    (act_all, dpre_all), both_terms = col_all_gather([act, dpre], [w_out, w_in.T], 2)
+    both_sums = row_sum(both_terms)
+    mixed = both_sums[:, :tokens.shape[1]]
     block_rows = (tokens.astype(jnp.float32) + mixed).astype(jnp.bfloat16)
     block_out = lax.all_to_all(block_rows, "col", split_axis=0, concat_axis=1, tiled=True)
     grad_out = lax.dot_general(
@@ -250,7 +253,7 @@
     grad_in = lax.dot_general(
         tokens_all, dpre_all, (((0,), (0,)), ((), ())), preferred_element_type=jnp.float32
     )
-    back = row_sum(back_term)
+    back = both_sums[:, tokens.shape[1]:]
     grad_tokens = (cotangent.astype(jnp.float32) + back).astype(jnp.bfloat16)
     return (block_out, grad_tokens, grad_in, grad_out)
 

time: 266 us -> 275 us (1.034); the launches traced: 266 us -> 270 us
  waiting for transfers between devices: 59.1 us -> 93 us
  blocking collectives: 30.8 us -> 0 us
  starting transfers between devices: 22 us -> 24.8 us
    all_to_all x1, waiting for transfers between devices: 7.58 us -> 45.8 us  [row_sum(): lax.all_to_all(pieces, 'row', split_axis=0, concat_axis=0, tiled=True)]
    all_to_all x1 -> x0, blocking collectives: 30.8 us -> none  [row_sum(): lax.all_to_all(pieces, 'row', split_axis=0, concat_axis=0, tiled=True)]
    all_to_all x1, waiting for transfers between devices: 4.28 us -> 0.01 us  [local(): lax.all_to_all(block_rows, 'col', split_axis=0, concat_axis=1, tiled=True)]
  transfers between devices with their start and end apart: 4 -> 4, of which waited for: 4 -> 3; matrix products, arithmetic and copies ran while one was open for 10% -> 8% of each run, Pallas kernels for 0% -> 0%
where the time goes in v6:
time: 275 us; the launch traced here: 270 us
  Pallas kernels  101 us (37%)
  waiting for transfers between devices  93 us (34%)
  starting transfers between devices  24.8 us (9%)
  matrix products  21.6 us (8%)
  between operations  14.1 us (5%)
  other arithmetic  8.61 us (3%)
  local copies, waits for them, and re-layouts  7.3 us (3%)
    pallas_call x1, Pallas kernels, col_reduce_scatter(): pl.pallas_call(functools.partial(_rs_kernel, nx, narr), out_shape=[jax.Sh...  52.6 us
    pallas_call x1, Pallas kernels, col_all_gather(): pl.pallas_call(functools.partial(_ag_kernel, nx, narr), out_shape=[jax.Sh...  48 us
    all_to_all x1, waiting for transfers between devices, row_sum(): lax.all_to_all(pieces, 'row', split_axis=0, concat_axis=0, tiled=True)  45.8 us
    all_to_all x1, waiting for transfers between devices, token_panel_a2a(): lax.all_to_all(copies, 'row', split_axis=0, concat_axis=0, tiled=True)  27.6 us
    all_gather x1, waiting for transfers between devices, token_panel(): return lax.all_gather(local_rows, 'row', axis=0, tiled=True)  18.9 us
    all_to_all x1, starting transfers between devices, local(): lax.all_to_all(block_rows, 'col', split_axis=0, concat_axis=1, tiled=True)  11.3 us
    all_to_all x1, starting transfers between devices, token_panel_a2a(): lax.all_to_all(copies, 'row', split_axis=0, concat_axis=0, tiled=True)  8.6 us
    dot_general x1, matrix products, local(): jnp.dot(tokens_all, w_in, preferred_element_type=jnp.float32)  6.15 us
  transfers between devices with their start and end apart: 4, of which 3 were waited for; matrix products, arithmetic and copies ran while one was open for 8% of the time, Pallas kernels for 0%

profile of v6, /device:TPU:1, one launch (start us, length us, event | category | flops | bytes accessed | tf_op | source)
XLA Modules:
  0.0 270.1 jit_solution(198020532192878664)
XLA Ops:
  7.2 0.0 all-gather.2.cloned.1.call-start
  7.2 0.7 all-gather.2.cloned.1.call-update
  7.9 2.4 broadcast_in_dim.2
  10.3 8.6 %all-to-all-start = ((bf16[16,128,512]{2,1,0:T(8,128)(2,1)}), bf16[16,128,512]{2,1,0:T(8,128)(2,1)S(1)}, u32[]{:S(2)}, u32[]{:S(2)}) async-start(bf16[16,128,512]{2,1,0:T(8,128)(2,1)} %broadcast_in_dim.2), calls=%async_computation | async-start | bytes 4194304 | tf_op jit(solution)/shard_map/all_to_all | solution.py:196
  18.9 0.0 copy-start.2
  18.9 2.4 copy.8
  21.3 27.6 %all-to-all-done = bf16[16,128,512]{2,1,0:T(8,128)(2,1)S(1)} async-done(((bf16[16,128,512]{2,1,0:T(8,128)(2,1)}), bf16[16,128,512]{2,1,0:T(8,128)(2,1)S(1)}, u32[]{:S(2)}, u32[]{:S(2)}) %all-to-all-start) | async-done | bytes 2097184 | tf_op jit(solution)/shard_map/all_to_all | solution.py:196
  48.9 4.3 %convolution_convert_fusion = bf16[2048,1024]{1,0:T(8,128)(2,1)} fusion(bf16[2048,512]{1,0:T(8,128)(2,1)S(1)} %bitcast.21, bf16[1024,512]{1,0:T(8,128)(2,1)S(1)} %copy-done.2), kind=kOutput, calls=%fused_computation.1 | convolution fusion | flops 2149580800 | bytes 7340032 | tf_op jit(solution)/shard_map/dot_general | solution.py:204
  53.2 18.9 %all-gather.2.cloned.1.call-done = bf16[2048,512]{1,0:T(8,128)(2,1)} async-done(((bf16[128,512]{1,0:T(8,128)(2,1)}), bf16[2048,512]{1,0:T(8,128)(2,1)}) %all-gather.2.cloned.1.call-update) | async-done | bytes 2097168 | tf_op jit(solution)/shard_map/all_gather | solution.py:189
  72.2 6.2 %convolution_convert_fusion.1 = bf16[2048,1024]{1,0:T(8,128)(2,1)} fusion(bf16[2048,512]{1,0:T(8,128)(2,1)} %all-gather.2.cloned.1.call-done, bf16[512,1024]{1,0:T(8,128)(2,1)} %param.5), kind=kOutput, calls=%fused_computation.2 | convolution fusion | flops 2149580800 | bytes 7340032 | tf_op jit(solution)/shard_map/dot_general | solution.py:240
  78.3 52.6 %shard_map.75 = (f32[256,1024]{1,0:T(8,128)}, f32[256,1024]{1,0:T(8,128)}) custom-call(bf16[8,256,1024]{2,1,0:T(8,128)(2,1)} %bitcast.28, bf16[8,256,1024]{2,1,0:T(8,128)(2,1)} %bitcast.27), custom_call_target="tpu_custom_call" | custom-call | tf_op jit(solution)/shard_map/pallas_call | solution.py:83
  131.0 4.7 %fusion.8 = (bf16[256,1024]{1,0:T(8,128)(2,1)}, bf16[256,1024]{1,0:T(8,128)(2,1)}) fusion(f32[256,1024]{1,0:T(8,128)} %get-tuple-element.10, f32[256,1024]{1,0:T(8,128)} %get-tuple-element.9), kind=kLoop, calls=%fused_computation.14 | loop fusion | flops 19660800 | bytes 3145728 | tf_op jit(solution)/shard_map/convert_element_type | solution.py:244
  135.6 48.0 %shard_map.76 = (bf16[8,256,1024]{2,1,0:T(8,128)(2,1)}, bf16[8,256,1024]{2,1,0:T(8,128)(2,1)}, bf16[8,256,1024]{2,1,0:T(8,128)(2,1)}) custom-call(bf16[256,1024]{1,0:T(8,128)(2,1)} %get-tuple-element.19.refs_0_, bf16[256,1024]{1,0:T(8,128)(2,1)} %get-tuple-element.18.refs_1_, bf16[1024,512]{1,0:T(8,128)(2,1)} %refs_2_.1, bf16[1024,512]{1,0:T(8,128)(2,1)} %bitcast.23), custom_call_target="tpu_custom_call" | custom-call | tf_op jit(solution)/shard_map/pallas_call | solution.py:163
  183.6 0.0 copy-start.1
  183.6 4.9 %all-to-all-start.1 = ((bf16[16,128,1024]{2,1,0:T(8,128)(2,1)}), bf16[16,128,1024]{2,1,0:T(8,128)(2,1)}, u32[]{:S(2)}, u32[]{:S(2)}) async-start(bf16[16,128,1024]{2,1,0:T(8,128)(2,1)} %bitcast.26), calls=%async_computation.1 | async-start | bytes 8388608 | tf_op jit(solution)/shard_map/all_to_all | solution.py:233
  188.5 5.9 %fusion.18 = f32[1024,512]{1,0:T(8,128)} fusion(bf16[2048,1024]{1,0:T(8,128)(2,1)} %bitcast.25, bf16[2048,512]{1,0:T(8,128)(2,1)S(1)} %bitcast.22), kind=kOutput, calls=%fused_computation.34 | convolution fusion | flops 2147483648 | bytes 8388608 | tf_op jit(solution)/shard_map/dot_general | solution.py:250
  194.4 45.8 %all-to-all-done.1 = bf16[16,128,1024]{2,1,0:T(8,128)(2,1)} async-done(((bf16[16,128,1024]{2,1,0:T(8,128)(2,1)}), bf16[16,128,1024]{2,1,0:T(8,128)(2,1)}, u32[]{:S(2)}, u32[]{:S(2)}) %all-to-all-start.1) | async-done | bytes 4194336 | tf_op jit(solution)/shard_map/all_to_all | solution.py:233
  240.2 3.1 %convert_reduce_fusion = f32[128,1024]{1,0:T(8,128)S(1)} fusion(bf16[16,128,1024]{2,1,0:T(8,128)(2,1)} %all-to-all-done.1), kind=kLoop, calls=%fused_computation | loop fusion | flops 4063232 | bytes 4718592 | tf_op jit(solution)/shard_map/reduce_sum | solution.py:234
  243.4 0.8 fusion.16
  244.2 11.3 %all-to-all-start.2 = ((bf16[8,16,512]{2,1,0:T(8,128)(2,1)}), bf16[8,16,512]{2,1,0:T(8,128)(2,1)S(1)}, u32[]{:S(2)}, u32[]{:S(2)}) async-start(bf16[8,16,512]{2,1,0:T(8,128)(2,1)} %bitcast.5), calls=%async_computation.2 | async-start | bytes 262144 | tf_op jit(solution)/shard_map/all_to_all | solution.py:249
  255.5 5.2 %convolution_bitcast_fusion = f32[512,1024]{0,1:T(8,128)S(1)} fusion(bf16[2048,1024]{1,0:T(8,128)(2,1)} %bitcast.24, bf16[2048,512]{1,0:T(8,128)(2,1)} %all-gather.2.cloned.1.call-done), kind=kOutput, calls=%fused_computation.3 | convolution fusion | flops 2147483648 | bytes 8388608 | tf_op jit(solution)/shard_map/dot_general | solution.py:253
  260.7 1.8 copy.10
  262.5 0.0 all-to-all-done.2
  262.5 0.7 copy.11
  (8 shorter events, 0.0 us)
Async XLA Ops:
  7.2 65.0 %all-gather.2.cloned.1.call-start = ((), (), s32[]{:S(2)}) async-start(), calls=%async_computation.3 | async-start | bytes 2228224 | tf_op jit(solution)/shard_map/all_gather | solution.py:189
  10.3 38.6 %all-to-all-start = ((bf16[16,128,512]{2,1,0:T(8,128)(2,1)}), bf16[16,128,512]{2,1,0:T(8,128)(2,1)S(1)}, u32[]{:S(2)}, u32[]{:S(2)}) async-start(bf16[16,128,512]{2,1,0:T(8,128)(2,1)} %broadcast_in_dim.2), calls=%async_computation | async-start | bytes 4194304 | tf_op jit(solution)/shard_map/all_to_all | solution.py:196
  18.9 30.0 %copy-start.2 = (bf16[1024,512]{1,0:T(8,128)(2,1)S(1)}, bf16[1024,512]{1,0:T(8,128)(2,1)}, u32[]{:S(2)}) copy-start(bf16[1024,512]{1,0:T(8,128)(2,1)} %refs_2_.1) | copy-start | bytes 3145732
  48.9 4.3 %copy-start = (bf16[16,128,512]{2,1,0:T(8,128)(2,1)}, bf16[16,128,512]{2,1,0:T(8,128)(2,1)S(1)}, u32[]{:S(2)}) copy-start(bf16[16,128,512]{2,1,0:T(8,128)(2,1)S(1)} %all-to-all-done) | copy-start | bytes 6291460
  183.6 4.9 %copy-start.1 = (bf16[16,128,512]{2,1,0:T(8,128)(2,1)S(1)}, bf16[16,128,512]{2,1,0:T(8,128)(2,1)}, u32[]{:S(2)}) copy-start(bf16[16,128,512]{2,1,0:T(8,128)(2,1)} %copy-done) | copy-start | bytes 6291460
  183.6 56.6 %all-to-all-start.1 = ((bf16[16,128,1024]{2,1,0:T(8,128)(2,1)}), bf16[16,128,1024]{2,1,0:T(8,128)(2,1)}, u32[]{:S(2)}, u32[]{:S(2)}) async-start(bf16[16,128,1024]{2,1,0:T(8,128)(2,1)} %bitcast.26), calls=%async_computation.1 | async-start | bytes 8388608 | tf_op jit(solution)/shard_map/all_to_all | solution.py:233
  194.4 49.0 %copy-start.3 = (bf16[128,512]{1,0:T(8,128)(2,1)S(1)}, bf16[128,512]{1,0:T(8,128)(2,1)}, u32[]{:S(2)}) copy-start(bf16[128,512]{1,0:T(8,128)(2,1)} %param.7) | copy-start | bytes 393220
  194.4 49.0 %copy-start.4 = (bf16[128,512]{1,0:T(8,128)(2,1)S(1)}, bf16[128,512]{1,0:T(8,128)(2,1)}, u32[]{:S(2)}) copy-start(bf16[128,512]{1,0:T(8,128)(2,1)} %param.4) | copy-start | bytes 393220
  244.2 18.4 %all-to-all-start.2 = ((bf16[8,16,512]{2,1,0:T(8,128)(2,1)}), bf16[8,16,512]{2,1,0:T(8,128)(2,1)S(1)}, u32[]{:S(2)}, u32[]{:S(2)}) async-start(bf16[8,16,512]{2,1,0:T(8,128)(2,1)} %bitcast.5), calls=%async_computation.2 | async-start | bytes 262144 | tf_op jit(solution)/shard_map/all_to_all | solution.py:249
Sparse Core Ops, SparseCore 0:
  10.1 61.9 all-gather.1

commit v7 on v5

--- a/solution.py
+++ b/solution.py
@@ -177,6 +177,106 @@
     return gathered, products
 
 
+def _row_ids():
+    me = lax.axis_index("row")
+    y = me // 4
+    z = me % 4
+    k = lax.axis_index("col") % 2
+    d = 1 - 2 * k
+    return y, z, d
+
+
+def _row_ag_kernel(ny, *refs):
+    ins = refs[:2]
+    outs = refs[2:4]
+    sa, sb, rsem = refs[4:]
+    col = lax.axis_index("col")
+    y, z, d = _row_ids()
+    me = y * 4 + z
+    barrier = pltpu.get_barrier_semaphore()
+    peers = (y * 4 + lax.rem(z + 4 + d, 4), y * 4 + lax.rem(z + 4 - d, 4),
+             lax.rem(y + ny + d, ny) * 4 + z, lax.rem(y + ny - d, ny) * 4 + z)
+    for p in peers:
+        pl.semaphore_signal(barrier, inc=1, device_id=(p, col), device_id_type=MESH)
+    pl.semaphore_wait(barrier, 4)
+    geo = []
+    for a in range(2):
+        if a == 0:
+            na, nb = 4, ny
+            pos_a, pos_b = z, y
+            slot_of = lambda pa, pb: pb * 4 + pa
+        else:
+            na, nb = ny, 4
+            pos_a, pos_b = y, z
+            slot_of = lambda pa, pb: pa * 4 + pb
+        geo.append((na, nb, pos_a, pos_b, slot_of))
+        outs[a][me] = ins[a][...]
+
+    def dev(a, pa, pb):
+        return (geo[a][4](pa, pb), col)
+
+    def send(a, src, slot, target, sem):
+        cp = pltpu.make_async_remote_copy(
+            src_ref=src, dst_ref=outs[a].at[slot], send_sem=sem, recv_sem=rsem.at[a, slot],
+            device_id=target, device_id_type=MESH)
+        cp.start()
+        return cp
+
+    def wait_in(a, slot):
+        pltpu.make_async_remote_copy(
+            src_ref=ins[a], dst_ref=outs[a].at[slot], send_sem=sa.at[a, 0], recv_sem=rsem.at[a, slot],
+            device_id=(peers[0], col), device_id_type=MESH).wait_recv()
+
+    sends = []
+    for a in range(2):
+        na, nb, pa, pb, slot_of = geo[a]
+        next_a = dev(a, lax.rem(pa + na + d, na), pb)
+        next_b = dev(a, pa, lax.rem(pb + nb + d, nb))
+        sends.append(send(a, ins[a], me, next_a, sa.at[a, 0]))
+        sends.append(send(a, ins[a], me, next_b, sb.at[a, 0, 0]))
+    for s in range(1, 4):
+        for a in range(2):
+            na, nb, pa, pb, slot_of = geo[a]
+            next_a = dev(a, lax.rem(pa + na + d, na), pb)
+            next_b = dev(a, pa, lax.rem(pb + nb + d, nb))
+            slot = slot_of(lax.rem(pa + 4 * na - d * s, na), pb)
+            wait_in(a, slot)
+            if s < na - 1:
+                sends.append(send(a, outs[a].at[slot], slot, next_a, sa.at[a, s]))
+            sends.append(send(a, outs[a].at[slot], slot, next_b, sb.at[a, 0, s]))
+    for t in range(1, 4):
+        for j in range(4):
+            for a in range(2):
+                na, nb, pa, pb, slot_of = geo[a]
+                next_b = dev(a, pa, lax.rem(pb + nb + d, nb))
+                slot = slot_of(lax.rem(pa + 4 * na - d * j, na), lax.rem(pb + 4 * nb - d * t, nb))
+                wait_in(a, slot)
+                if t < nb - 1:
+                    sends.append(send(a, outs[a].at[slot], slot, next_b, sb.at[a, t, j]))
+    for cp in sends:
+        cp.wait_send()
+
+
+def row_all_gather(first, second, cid):
+    n = lax.axis_size("row")
+    ny = n // 4
+    rows, cols = first.shape
+    outs = pl.pallas_call(
+        functools.partial(_row_ag_kernel, ny),
+        out_shape=[jax.ShapeDtypeStruct((n, rows, cols), first.dtype)] * 2,
+        in_specs=[pl.BlockSpec(memory_space=pltpu.VMEM)] * 2,
+        out_specs=[pl.BlockSpec(memory_space=pltpu.VMEM)] * 2,
+        scratch_shapes=[
+            pltpu.SemaphoreType.DMA((2, 4)),
+            pltpu.SemaphoreType.DMA((2, 4, 4)),
+            pltpu.SemaphoreType.DMA((2, n)),
+        ],
+        compiler_params=pltpu.CompilerParams(collective_id=cid, has_side_effects=True,
+                                             vmem_limit_bytes=64 * 1024 * 1024),
+    )(first, second)
+    return [o.reshape(n * rows, cols) for o in outs]
+
+
 def gelu_grad(value):
     cdf = 0.5 * (1.0 + jax.scipy.special.erf(value * 0.7071067811865476))
     pdf = jnp.exp(-0.5 * value * value) * 0.3989422804014327
@@ -233,8 +333,7 @@
 
 
 def local(tokens, w_in, w_out, cotangent):
-    tokens_all = token_panel(tokens)
-    upstream_all = token_panel_a2a(cotangent)
+    tokens_all, upstream_all = row_all_gather(tokens, cotangent, 3)
     pre_term = jnp.dot(tokens_all, w_in, preferred_element_type=jnp.float32).astype(jnp.bfloat16)
     dact_term = contract_last(upstream_all, w_out).astype(jnp.bfloat16)
     pre_part, dact_part = col_reduce_scatter([pre_term, dact_term], 1)

time: 266 us -> 232 us (0.87)
  waiting for transfers between devices: 59.1 us -> 17.6 us
  Pallas kernels: 100 us -> 138 us
  between operations: 14.1 us -> 0.72 us
  starting transfers between devices: 22 us -> 13.8 us
  local copies, waits for them, and re-layouts: 8.96 us -> 3.58 us
  matrix products: 23.7 us -> 21 us
    pallas_call x0 -> x1, Pallas kernels: none -> 34.7 us  [row_all_gather(): pl.pallas_call(functools.partial(_row_ag_kernel, ny), out_shape=[jax.Shap...]
    all_to_all x1 -> x0, waiting for transfers between devices: 27.6 us -> none  [token_panel_a2a(): lax.all_to_all(copies, 'row', split_axis=0, concat_axis=0, tiled=True)]
    all_gather x1 -> x0, waiting for transfers between devices: 18.9 us -> none  [token_panel(): return lax.all_gather(local_rows, 'row', axis=0, tiled=True)]
    all_to_all x1 -> x0, starting transfers between devices: 8.6 us -> none  [token_panel_a2a(): lax.all_to_all(copies, 'row', split_axis=0, concat_axis=0, tiled=True)]
    all_to_all x1, waiting for transfers between devices: 7.58 us -> 13.3 us  [row_sum(): lax.all_to_all(pieces, 'row', split_axis=0, concat_axis=0, tiled=True)]
    pallas_call x1, Pallas kernels: 52.6 us -> 55.6 us  [col_reduce_scatter(): pl.pallas_call(functools.partial(_rs_kernel, nx, narr), out_shape=[jax.Sh...]
    unnamed x12 -> x15, local copies, waits for them, and re-layouts: 5.87 us -> 2.92 us
    dot_general x1, matrix products: 6.55 us -> 3.67 us  [local(): lax.dot_general(tokens_all, dpre_all, (((0,), (0,)), ((), ())), preferred...]
  transfers between devices with their start and end apart: 4 -> 2, of which waited for: 4 -> 2; matrix products, arithmetic and copies ran while one was open for 10% -> 5% of each run, Pallas kernels for 0% -> 0%
where the time goes in v7:
time: 232 us
  Pallas kernels  138 us (59%)
  blocking collectives  30.3 us (13%)
  matrix products  21 us (9%)
  waiting for transfers between devices  17.6 us (8%)
  starting transfers between devices  13.8 us (6%)
  other arithmetic  6.63 us (3%)
  local copies, waits for them, and re-layouts  3.58 us (2%)
    pallas_call x1, Pallas kernels, col_reduce_scatter(): pl.pallas_call(functools.partial(_rs_kernel, nx, narr), out_shape=[jax.Sh...  55.6 us
    pallas_call x1, Pallas kernels, col_all_gather(): pl.pallas_call(functools.partial(_ag_kernel, nx, narr), out_shape=[jax.Sh...  47.9 us
    pallas_call x1, Pallas kernels, row_all_gather(): pl.pallas_call(functools.partial(_row_ag_kernel, ny), out_shape=[jax.Shap...  34.7 us
    all_to_all x1, blocking collectives, row_sum(): lax.all_to_all(pieces, 'row', split_axis=0, concat_axis=0, tiled=True)  30.3 us
    all_to_all x1, waiting for transfers between devices, row_sum(): lax.all_to_all(pieces, 'row', split_axis=0, concat_axis=0, tiled=True)  13.3 us
    all_to_all x1, starting transfers between devices, local(): lax.all_to_all(block_rows, 'col', split_axis=0, concat_axis=1, tiled=True)  9.2 us
    dot_general x1, matrix products, local(): lax.dot_general(act_all, upstream_all, (((0,), (0,)), ((), ())), preferre...  6.68 us
    dot_general x1, matrix products, local(): jnp.dot(tokens_all, w_in, preferred_element_type=jnp.float32)  6.3 us
  transfers between devices with their start and end apart: 2, of which 2 were waited for; matrix products, arithmetic and copies ran while one was open for 5% of the time, Pallas kernels for 0%

profile of v7, /device:TPU:1, one launch (start us, length us, event | category | flops | bytes accessed | tf_op | source)
XLA Modules:
  0.0 231.9 jit_solution(6563465022690572420)
XLA Ops:
  0.6 2.3 copy.11
  2.9 34.7 %shard_map.75 = (bf16[16,128,512]{2,1,0:T(8,128)(2,1)}, bf16[16,128,512]{2,1,0:T(8,128)(2,1)}) custom-call(bf16[128,512]{1,0:T(8,128)(2,1)} %refs_0_.1, bf16[128,512]{1,0:T(8,128)(2,1)} %refs_1_.1), custom_call_target="tpu_custom_call" | custom-call | tf_op jit(solution)/shard_map/pallas_call | solution.py:264
  37.7 0.0 copy-start.2
  37.7 6.3 %convolution_convert_fusion.1 = bf16[2048,1024]{1,0:T(8,128)(2,1)} fusion(bf16[2048,512]{1,0:T(8,128)(2,1)} %bitcast.32, bf16[512,1024]{1,0:T(8,128)(2,1)} %param.5), kind=kOutput, calls=%fused_computation.3 | convolution fusion | flops 2149580800 | bytes 7340032 | tf_op jit(solution)/shard_map/dot_general | solution.py:337
  44.0 0.0 copy-done.1
  44.0 4.4 %convolution_convert_fusion = bf16[2048,1024]{1,0:T(8,128)(2,1)} fusion(bf16[2048,512]{1,0:T(8,128)(2,1)S(1)} %bitcast.28, bf16[1024,512]{1,0:T(8,128)(2,1)S(1)} %copy-done.2), kind=kOutput, calls=%fused_computation.2 | convolution fusion | flops 2149580800 | bytes 7340032 | tf_op jit(solution)/shard_map/dot_general | solution.py:302
  48.3 55.6 %shard_map.76 = (f32[256,1024]{1,0:T(8,128)}, f32[256,1024]{1,0:T(8,128)}) custom-call(bf16[8,256,1024]{2,1,0:T(8,128)(2,1)} %bitcast.23, bf16[8,256,1024]{2,1,0:T(8,128)(2,1)} %bitcast.24), custom_call_target="tpu_custom_call" | custom-call | tf_op jit(solution)/shard_map/pallas_call | solution.py:83
  103.9 4.7 %fusion.8 = (bf16[256,1024]{1,0:T(8,128)(2,1)}, bf16[256,1024]{1,0:T(8,128)(2,1)}) fusion(f32[256,1024]{1,0:T(8,128)} %get-tuple-element.15, f32[256,1024]{1,0:T(8,128)} %get-tuple-element.14), kind=kLoop, calls=%fused_computation.14 | loop fusion | flops 19660800 | bytes 3145728 | tf_op jit(solution)/shard_map/convert_element_type | solution.py:341
  108.6 47.9 %shard_map.77 = (bf16[8,256,1024]{2,1,0:T(8,128)(2,1)}, bf16[8,256,1024]{2,1,0:T(8,128)(2,1)}, bf16[8,256,512]{2,1,0:T(8,128)(2,1)}, bf16[8,256,512]{2,1,0:T(8,128)(2,1)}) custom-call(bf16[256,1024]{1,0:T(8,128)(2,1)} %get-tuple-element.21.refs_0_, bf16[256,1024]{1,0:T(8,128)(2,1)} %get-tuple-element.20.refs_1_, bf16[1024,512]{1,0:T(8,128)(2,1)} %refs_2_.1, ...), custom_call_target="tpu_custom_call" | custom-call | tf_op jit(solution)/shard_map/pallas_call | solution.py:160
  156.5 30.3 %all_to_all.29 = bf16[16,128,512]{2,1,0:T(8,128)(2,1)} all-to-all(bf16[16,128,512]{2,1,0:T(8,128)(2,1)} %bitcast.26), channel_id=1, replica_groups=mesh['row'=16,'col'=8] {'row'}, dimensions={0} | all-to-all | bytes 4194304 | tf_op jit(solution)/shard_map/all_to_all | solution.py:331
  186.8 4.6 %all-to-all-start.2 = ((bf16[16,128,512]{2,1,0:T(8,128)(2,1)}), bf16[16,128,512]{2,1,0:T(8,128)(2,1)S(1)}, u32[]{:S(2)}, u32[]{:S(2)}) async-start(bf16[16,128,512]{2,1,0:T(8,128)(2,1)} %bitcast.25), calls=%async_computation.2 | async-start | bytes 4194304 | tf_op jit(solution)/shard_map/all_to_all | solution.py:331
  191.4 6.7 %fusion.17 = f32[1024,512]{1,0:T(8,128)} fusion(bf16[2048,1024]{1,0:T(8,128)(2,1)} %bitcast.22, bf16[2048,512]{1,0:T(8,128)(2,1)} %bitcast.27), kind=kOutput, calls=%fused_computation.33 | convolution fusion | flops 2147483648 | bytes 8388608 | tf_op jit(solution)/shard_map/dot_general | solution.py:346
  198.1 0.0 copy-done.5
  198.1 3.7 %fusion.16 = f32[512,1024]{1,0:T(8,128)} fusion(bf16[2048,512]{1,0:T(8,128)(2,1)S(1)} %bitcast.33, bf16[2048,1024]{1,0:T(8,128)(2,1)S(1)} %bitcast.31), kind=kOutput, calls=%fused_computation.32 | convolution fusion | flops 2147483648 | bytes 8388608 | tf_op jit(solution)/shard_map/dot_general | solution.py:349
  201.8 0.0 copy-done
  201.8 0.3 convert_reduce_fusion.1
  202.1 0.6 copy-done.3
  202.7 0.7 add_convert_fusion.1
  203.4 13.3 %all-to-all-done.2 = bf16[16,128,512]{2,1,0:T(8,128)(2,1)S(1)} async-done(((bf16[16,128,512]{2,1,0:T(8,128)(2,1)}), bf16[16,128,512]{2,1,0:T(8,128)(2,1)S(1)}, u32[]{:S(2)}, u32[]{:S(2)}) %all-to-all-start.2) | async-done | bytes 2097184 | tf_op jit(solution)/shard_map/all_to_all | solution.py:331
  216.7 9.2 %all-to-all-start.1 = ((bf16[8,16,512]{2,1,0:T(8,128)(2,1)}), bf16[8,16,512]{2,1,0:T(8,128)(2,1)S(1)}, u32[]{:S(2)}, u32[]{:S(2)}) async-start(bf16[8,16,512]{2,1,0:T(8,128)(2,1)} %bitcast.6), calls=%async_computation.1 | async-start | bytes 262144 | tf_op jit(solution)/shard_map/all_to_all | solution.py:345
  225.9 0.3 convert_reduce_fusion
  226.2 0.7 add_convert_fusion
  226.9 4.3 %all-to-all-done.1 = bf16[8,16,512]{2,1,0:T(8,128)(2,1)S(1)} async-done(((bf16[8,16,512]{2,1,0:T(8,128)(2,1)}), bf16[8,16,512]{2,1,0:T(8,128)(2,1)S(1)}, u32[]{:S(2)}, u32[]{:S(2)}) %all-to-all-start.1) | async-done | bytes 131104 | tf_op jit(solution)/shard_map/all_to_all | solution.py:345
  231.2 0.7 copy.13
  (9 shorter events, 0.0 us)
Async XLA Ops:
  37.6 6.3 %copy-start.1 = (bf16[16,128,512]{2,1,0:T(8,128)(2,1)S(1)}, bf16[16,128,512]{2,1,0:T(8,128)(2,1)}, u32[]{:S(2)}) copy-start(bf16[16,128,512]{2,1,0:T(8,128)(2,1)} %get-tuple-element.13) | copy-start | bytes 6291460
  37.7 6.3 %copy-start.2 = (bf16[1024,512]{1,0:T(8,128)(2,1)S(1)}, bf16[1024,512]{1,0:T(8,128)(2,1)}, u32[]{:S(2)}) copy-start(bf16[1024,512]{1,0:T(8,128)(2,1)} %refs_2_.1) | copy-start | bytes 3145732
  186.8 29.9 %all-to-all-start.2 = ((bf16[16,128,512]{2,1,0:T(8,128)(2,1)}), bf16[16,128,512]{2,1,0:T(8,128)(2,1)S(1)}, u32[]{:S(2)}, u32[]{:S(2)}) async-start(bf16[16,128,512]{2,1,0:T(8,128)(2,1)} %bitcast.25), calls=%async_computation.2 | async-start | bytes 4194304 | tf_op jit(solution)/shard_map/all_to_all | solution.py:331
  191.4 6.7 %copy-start.5 = (bf16[8,256,1024]{2,1,0:T(8,128)(2,1)S(1)}, bf16[8,256,1024]{2,1,0:T(8,128)(2,1)}, u32[]{:S(2)}) copy-start(bf16[8,256,1024]{2,1,0:T(8,128)(2,1)} %get-tuple-element.18) | copy-start | bytes 12582916
  191.4 6.7 %copy-start.6 = (bf16[16,128,512]{2,1,0:T(8,128)(2,1)S(1)}, bf16[16,128,512]{2,1,0:T(8,128)(2,1)}, u32[]{:S(2)}) copy-start(bf16[16,128,512]{2,1,0:T(8,128)(2,1)} %get-tuple-element.12) | copy-start | bytes 6291460
  198.1 3.7 %copy-start = (bf16[16,128,512]{2,1,0:T(8,128)(2,1)S(1)}, bf16[16,128,512]{2,1,0:T(8,128)(2,1)}, u32[]{:S(2)}) copy-start(bf16[16,128,512]{2,1,0:T(8,128)(2,1)} %all_to_all.29) | copy-start | bytes 6291460
  201.8 0.9 copy-start.3
  202.7 23.5 %copy-start.4 = (bf16[128,512]{1,0:T(8,128)(2,1)S(1)}, bf16[128,512]{1,0:T(8,128)(2,1)}, u32[]{:S(2)}) copy-start(bf16[128,512]{1,0:T(8,128)(2,1)} %refs_1_.1) | copy-start | bytes 393220
  216.7 14.5 %all-to-all-start.1 = ((bf16[8,16,512]{2,1,0:T(8,128)(2,1)}), bf16[8,16,512]{2,1,0:T(8,128)(2,1)S(1)}, u32[]{:S(2)}, u32[]{:S(2)}) async-start(bf16[8,16,512]{2,1,0:T(8,128)(2,1)} %bitcast.6), calls=%async_computation.1 | async-start | bytes 262144 | tf_op jit(solution)/shard_map/all_to_all | solution.py:345

commit v8 on v7

--- a/solution.py
+++ b/solution.py
@@ -277,6 +277,99 @@
     return [o.reshape(n * rows, cols) for o in outs]
 
 
+def _row_rs_kernel(ny, *refs):
+    ins = refs[:2]
+    outs = refs[2:4]
+    sb1, rb1, ssum, sb2, rb2, s1, r1, s2, r2 = refs[4:]
+    col = lax.axis_index("col")
+    y, z, d = _row_ids()
+    barrier = pltpu.get_barrier_semaphore()
+    peers = (y * 4 + lax.rem(z + 4 + d, 4), y * 4 + lax.rem(z + 4 - d, 4),
+             lax.rem(y + ny + d, ny) * 4 + z, lax.rem(y + ny - d, ny) * 4 + z)
+    for p in peers:
+        pl.semaphore_signal(barrier, inc=1, device_id=(p, col), device_id_type=MESH)
+    pl.semaphore_wait(barrier, 4)
+    geo = [(4, ny, z, y, lambda pa, pb: pb * 4 + pa), (ny, 4, y, z, lambda pa, pb: pa * 4 + pb)]
+
+    def dev(a, pa, pb):
+        return (geo[a][4](pa, pb), col)
+
+    def send(src, dst, ssem, rsem, target):
+        cp = pltpu.make_async_remote_copy(src_ref=src, dst_ref=dst, send_sem=ssem, recv_sem=rsem,
+                                          device_id=target, device_id_type=MESH)
+        cp.start()
+        return cp
+
+    sends = []
+    first = [[] for _ in range(2)]
+    for s in range(4 - 1):
+        for a in range(2):
+            na, nb, pa, pb, slot_of = geo[a]
+            pos = lax.rem(pa + 4 * na - d * (s + 1), na)
+            for bq in range(nb):
+                own = ins[a][slot_of(pos, bq)]
+                if s == 0:
+                    sb1[a, s, bq] = own
+                else:
+                    sb1[a, s, bq] = (rb1[a, s - 1, bq].astype(jnp.float32) + own.astype(jnp.float32)).astype(sb1.dtype)
+            cp = send(sb1.at[a, s], rb1.at[a, s], s1.at[a, s], r1.at[a, s],
+                      dev(a, lax.rem(pa + na + d, na), pb))
+            sends.append(cp)
+            first[a].append(cp)
+        for a in range(2):
+            first[a][s].wait_recv()
+    for a in range(2):
+        na, nb, pa, pb, slot_of = geo[a]
+        for bq in range(nb):
+            ssum[a, bq] = rb1[a, 2, bq].astype(jnp.float32) + ins[a][slot_of(pa, bq)].astype(jnp.float32)
+    second = [[] for _ in range(2)]
+    for t in range(4 - 1):
+        for a in range(2):
+            na, nb, pa, pb, slot_of = geo[a]
+            pos = lax.rem(pb + 4 * nb - d * (t + 1), nb)
+            if t == 0:
+                sb2[a, t] = ssum[a, pos].astype(sb2.dtype)
+            else:
+                sb2[a, t] = (rb2[a, t - 1].astype(jnp.float32) + ssum[a, pos]).astype(sb2.dtype)
+            cp = send(sb2.at[a, t], rb2.at[a, t], s2.at[a, t], r2.at[a, t],
+                      dev(a, pa, lax.rem(pb + nb + d, nb)))
+            sends.append(cp)
+            second[a].append(cp)
+        for a in range(2):
+            second[a][t].wait_recv()
+    for a in range(2):
+        na, nb, pa, pb, slot_of = geo[a]
+        outs[a][...] = rb2[a, 2].astype(jnp.float32) + ssum[a, pb]
+    for cp in sends:
+        cp.wait_send()
+
+
+def row_reduce_scatter(first, second, cid):
+    n = lax.axis_size("row")
+    ny = n // 4
+    rows, cols = first.shape[0] // n, first.shape[1]
+    ins = [v.reshape(n, rows, cols) for v in (first, second)]
+    return pl.pallas_call(
+        functools.partial(_row_rs_kernel, ny),
+        out_shape=[jax.ShapeDtypeStruct((rows, cols), jnp.float32)] * 2,
+        in_specs=[pl.BlockSpec(memory_space=pltpu.VMEM)] * 2,
+        out_specs=[pl.BlockSpec(memory_space=pltpu.VMEM)] * 2,
+        scratch_shapes=[
+            pltpu.VMEM((2, 3, 4, rows, cols), jnp.bfloat16),
+            pltpu.VMEM((2, 3, 4, rows, cols), jnp.bfloat16),
+            pltpu.VMEM((2, 4, rows, cols), jnp.float32),
+            pltpu.VMEM((2, 3, rows, cols), jnp.bfloat16),
+            pltpu.VMEM((2, 3, rows, cols), jnp.bfloat16),
+            pltpu.SemaphoreType.DMA((2, 3)),
+            pltpu.SemaphoreType.DMA((2, 3)),
+            pltpu.SemaphoreType.DMA((2, 3)),
+            pltpu.SemaphoreType.DMA((2, 3)),
+        ],
+        compiler_params=pltpu.CompilerParams(collective_id=cid, has_side_effects=True,
+                                             vmem_limit_bytes=64 * 1024 * 1024),
+    )(*ins)
+
+
 def gelu_grad(value):
     cdf = 0.5 * (1.0 + jax.scipy.special.erf(value * 0.7071067811865476))
     pdf = jnp.exp(-0.5 * value * value) * 0.3989422804014327
@@ -340,7 +433,7 @@
     act = jax.nn.gelu(pre_part, approximate=False).astype(jnp.bfloat16)
     dpre = (dact_part * gelu_grad(pre_part)).astype(jnp.bfloat16)
     (act_all, dpre_all), (mixed_term, back_term) = col_all_gather([act, dpre], [w_out, w_in.T], 2)
-    mixed = row_sum(mixed_term)
+    mixed, back = row_reduce_scatter(mixed_term, back_term, 4)
     block_rows = (tokens.astype(jnp.float32) + mixed).astype(jnp.bfloat16)
     block_out = lax.all_to_all(block_rows, "col", split_axis=0, concat_axis=1, tiled=True)
     grad_out = lax.dot_general(
@@ -349,7 +442,6 @@
     grad_in = lax.dot_general(
         tokens_all, dpre_all, (((0,), (0,)), ((), ())), preferred_element_type=jnp.float32
     )
-    back = row_sum(back_term)
     grad_tokens = (cotangent.astype(jnp.float32) + back).astype(jnp.bfloat16)
     return (block_out, grad_tokens, grad_in, grad_out)
 

time: 232 us -> 219 us (0.944)
  Pallas kernels: 138 us -> 176 us
  blocking collectives: 30.3 us -> 0 us
  waiting for transfers between devices: 17.6 us -> 0.01 us
  starting transfers between devices: 13.8 us -> 10.8 us
    pallas_call x0 -> x1, Pallas kernels: none -> 38.3 us  [row_reduce_scatter(): pl.pallas_call(functools.partial(_row_rs_kernel, ny), out_shape=[jax.Shap...]
    all_to_all x1 -> x0, blocking collectives: 30.3 us -> none  [row_sum(): lax.all_to_all(pieces, 'row', split_axis=0, concat_axis=0, tiled=True)]
    all_to_all x1 -> x0, waiting for transfers between devices: 13.3 us -> none  [row_sum(): lax.all_to_all(pieces, 'row', split_axis=0, concat_axis=0, tiled=True)]
    all_to_all x1 -> x0, starting transfers between devices: 4.58 us -> none  [row_sum(): lax.all_to_all(pieces, 'row', split_axis=0, concat_axis=0, tiled=True)]
    all_to_all x1, waiting for transfers between devices: 4.28 us -> 0.01 us  [local(): lax.all_to_all(block_rows, 'col', split_axis=0, concat_axis=1, tiled=True)]
  transfers between devices with their start and end apart: 2 -> 1, of which waited for: 2 -> 0; matrix products, arithmetic and copies ran while one was open for 5% -> 5% of each run, Pallas kernels for 0% -> 0%
where the time goes in v8:
time: 219 us
  Pallas kernels  176 us (80%)
  matrix products  21 us (10%)
  starting transfers between devices  10.8 us (5%)
  other arithmetic  7.02 us (3%)
  local copies, waits for them, and re-layouts  2.97 us (1%)
    pallas_call x1, Pallas kernels, col_reduce_scatter(): pl.pallas_call(functools.partial(_rs_kernel, nx, narr), out_shape=[jax.Sh...  55.5 us
    pallas_call x1, Pallas kernels, col_all_gather(): pl.pallas_call(functools.partial(_ag_kernel, nx, narr), out_shape=[jax.Sh...  47.9 us
    pallas_call x1, Pallas kernels, row_reduce_scatter(): pl.pallas_call(functools.partial(_row_rs_kernel, ny), out_shape=[jax.Shap...  38.3 us
    pallas_call x1, Pallas kernels, row_all_gather(): pl.pallas_call(functools.partial(_row_ag_kernel, ny), out_shape=[jax.Shap...  34.7 us
    all_to_all x1, starting transfers between devices, local(): lax.all_to_all(block_rows, 'col', split_axis=0, concat_axis=1, tiled=True)  10.8 us
    dot_general x1, matrix products, local(): lax.dot_general(act_all, upstream_all, (((0,), (0,)), ((), ())), preferre...  6.68 us
    dot_general x1, matrix products, local(): jnp.dot(tokens_all, w_in, preferred_element_type=jnp.float32)  6.3 us
    convert_element_type x1, other arithmetic, local(): dpre = (dact_part * gelu_grad(pre_part)).astype(jnp.bfloat16)  4.67 us
  transfers between devices with their start and end apart: 1, of which 0 were waited for; matrix products, arithmetic and copies ran while one was open for 5% of the time, Pallas kernels for 0%

profile of v8, /device:TPU:1, one launch (start us, length us, event | category | flops | bytes accessed | tf_op | source)
XLA Modules:
  0.0 218.9 jit_solution(2584150924251312252)
XLA Ops:
  0.6 2.3 %copy.8 = bf16[512,1024]{0,1:T(8,128)(2,1)} copy(bf16[512,1024]{1,0:T(8,128)(2,1)} %param.5) | data formatting | bytes 2097152 | tf_op args[1]
  2.9 34.7 %shard_map.75 = (bf16[16,128,512]{2,1,0:T(8,128)(2,1)}, bf16[16,128,512]{2,1,0:T(8,128)(2,1)}) custom-call(bf16[128,512]{1,0:T(8,128)(2,1)} %refs_0_.1, bf16[128,512]{1,0:T(8,128)(2,1)} %refs_1_.1), custom_call_target="tpu_custom_call" | custom-call | tf_op jit(solution)/shard_map/pallas_call | solution.py:264
  37.6 0.0 copy-start
  37.6 0.0 copy-start.1
  37.7 6.3 %convolution_convert_fusion.1 = bf16[2048,1024]{1,0:T(8,128)(2,1)} fusion(bf16[2048,512]{1,0:T(8,128)(2,1)} %bitcast.32, bf16[512,1024]{1,0:T(8,128)(2,1)} %param.5), kind=kOutput, calls=%fused_computation.1 | convolution fusion | flops 2149580800 | bytes 7340032 | tf_op jit(solution)/shard_map/dot_general | solution.py:430
  44.0 0.0 copy-done
  44.0 0.0 copy-done.1
  44.0 4.3 %convolution_convert_fusion = bf16[2048,1024]{1,0:T(8,128)(2,1)} fusion(bf16[2048,512]{1,0:T(8,128)(2,1)S(1)} %bitcast.28, bf16[1024,512]{1,0:T(8,128)(2,1)S(1)} %copy-done.1), kind=kOutput, calls=%fused_computation | convolution fusion | flops 2149580800 | bytes 7340032 | tf_op jit(solution)/shard_map/dot_general | solution.py:395
  48.3 55.5 %shard_map.76 = (f32[256,1024]{1,0:T(8,128)}, f32[256,1024]{1,0:T(8,128)}) custom-call(bf16[8,256,1024]{2,1,0:T(8,128)(2,1)} %bitcast.23, bf16[8,256,1024]{2,1,0:T(8,128)(2,1)} %bitcast.24), custom_call_target="tpu_custom_call" | custom-call | tf_op jit(solution)/shard_map/pallas_call | solution.py:83
  103.8 4.7 %fusion.8 = (bf16[256,1024]{1,0:T(8,128)(2,1)}, bf16[256,1024]{1,0:T(8,128)(2,1)}) fusion(f32[256,1024]{1,0:T(8,128)} %get-tuple-element.17, f32[256,1024]{1,0:T(8,128)} %get-tuple-element.16), kind=kLoop, calls=%fused_computation.12 | loop fusion | flops 19660800 | bytes 3145728 | tf_op jit(solution)/shard_map/convert_element_type | solution.py:434
  108.5 47.9 %shard_map.77 = (bf16[8,256,1024]{2,1,0:T(8,128)(2,1)}, bf16[8,256,1024]{2,1,0:T(8,128)(2,1)}, bf16[8,256,512]{2,1,0:T(8,128)(2,1)}, bf16[8,256,512]{2,1,0:T(8,128)(2,1)}) custom-call(bf16[256,1024]{1,0:T(8,128)(2,1)} %get-tuple-element.25.refs_0_, bf16[256,1024]{1,0:T(8,128)(2,1)} %get-tuple-element.24.refs_1_, bf16[1024,512]{1,0:T(8,128)(2,1)} %refs_2_.1, ...), custom_call_target="tpu_custom_call" | custom-call | tf_op jit(solution)/shard_map/pallas_call | solution.py:160
  156.4 38.3 %shard_map.78 = (f32[128,512]{1,0:T(8,128)}, f32[128,512]{1,0:T(8,128)}) custom-call(bf16[16,128,512]{2,1,0:T(8,128)(2,1)} %bitcast.25, bf16[16,128,512]{2,1,0:T(8,128)(2,1)} %bitcast.26), custom_call_target="tpu_custom_call" | custom-call | tf_op jit(solution)/shard_map/pallas_call | solution.py:352
  194.7 1.7 add_convert_fusion.1
  196.3 10.8 %all-to-all-start = ((bf16[8,16,512]{2,1,0:T(8,128)(2,1)}), bf16[8,16,512]{2,1,0:T(8,128)(2,1)S(1)}, u32[]{:S(2)}, u32[]{:S(2)}) async-start(bf16[8,16,512]{2,1,0:T(8,128)(2,1)} %bitcast.7), calls=%async_computation | async-start | bytes 262144 | tf_op jit(solution)/shard_map/all_to_all | solution.py:438
  207.2 6.7 %fusion.17 = f32[1024,512]{1,0:T(8,128)} fusion(bf16[2048,1024]{1,0:T(8,128)(2,1)} %bitcast.22, bf16[2048,512]{1,0:T(8,128)(2,1)} %bitcast.27), kind=kOutput, calls=%fused_computation.31 | convolution fusion | flops 2147483648 | bytes 8388608 | tf_op jit(solution)/shard_map/dot_general | solution.py:439
  213.8 0.0 copy-done.4
  213.8 0.0 copy-done.5
  213.8 0.0 copy-start.3
  213.9 3.7 %fusion.16 = f32[512,1024]{1,0:T(8,128)} fusion(bf16[2048,512]{1,0:T(8,128)(2,1)S(1)} %bitcast.33, bf16[2048,1024]{1,0:T(8,128)(2,1)S(1)} %bitcast.31), kind=kOutput, calls=%fused_computation.30 | convolution fusion | flops 2147483648 | bytes 8388608 | tf_op jit(solution)/shard_map/dot_general | solution.py:442
  217.5 0.0 copy-done.2
  217.5 0.0 copy-done.3
  217.5 0.7 add_convert_fusion
  218.2 0.0 all-to-all-done
  218.2 0.7 copy.10
  (3 shorter events, 0.0 us)
Async XLA Ops:
  37.6 6.3 %copy-start = (bf16[16,128,512]{2,1,0:T(8,128)(2,1)S(1)}, bf16[16,128,512]{2,1,0:T(8,128)(2,1)}, u32[]{:S(2)}) copy-start(bf16[16,128,512]{2,1,0:T(8,128)(2,1)} %get-tuple-element.15) | copy-start | bytes 6291460
  37.6 6.3 %copy-start.1 = (bf16[1024,512]{1,0:T(8,128)(2,1)S(1)}, bf16[1024,512]{1,0:T(8,128)(2,1)}, u32[]{:S(2)}) copy-start(bf16[1024,512]{1,0:T(8,128)(2,1)} %refs_2_.1) | copy-start | bytes 3145732
  196.3 21.9 %all-to-all-start = ((bf16[8,16,512]{2,1,0:T(8,128)(2,1)}), bf16[8,16,512]{2,1,0:T(8,128)(2,1)S(1)}, u32[]{:S(2)}, u32[]{:S(2)}) async-start(bf16[8,16,512]{2,1,0:T(8,128)(2,1)} %bitcast.7), calls=%async_computation | async-start | bytes 262144 | tf_op jit(solution)/shard_map/all_to_all | solution.py:438
  207.2 6.7 %copy-start.4 = (bf16[8,256,1024]{2,1,0:T(8,128)(2,1)S(1)}, bf16[8,256,1024]{2,1,0:T(8,128)(2,1)}, u32[]{:S(2)}) copy-start(bf16[8,256,1024]{2,1,0:T(8,128)(2,1)} %get-tuple-element.22) | copy-start | bytes 12582916
  207.2 6.7 %copy-start.5 = (bf16[16,128,512]{2,1,0:T(8,128)(2,1)S(1)}, bf16[16,128,512]{2,1,0:T(8,128)(2,1)}, u32[]{:S(2)}) copy-start(bf16[16,128,512]{2,1,0:T(8,128)(2,1)} %get-tuple-element.14) | copy-start | bytes 6291460
  213.8 3.7 %copy-start.2 = (bf16[128,512]{1,0:T(8,128)(2,1)S(1)}, bf16[128,512]{1,0:T(8,128)(2,1)}, u32[]{:S(2)}) copy-start(bf16[128,512]{1,0:T(8,128)(2,1)} %refs_1_.1) | copy-start | bytes 393220
  213.8 3.7 %copy-start.3 = (f32[128,512]{1,0:T(8,128)S(1)}, f32[128,512]{1,0:T(8,128)}, u32[]{:S(2)}) copy-start(f32[128,512]{1,0:T(8,128)} %get-tuple-element.21) | copy-start | bytes 786436

commit v9 on v8

--- a/solution.py
+++ b/solution.py
@@ -188,8 +188,19 @@
 
 def _row_ag_kernel(ny, *refs):
     ins = refs[:2]
-    outs = refs[2:4]
-    sa, sb, rsem = refs[4:]
+    weights = refs[2:4]
+    outs = refs[4:6]
+    terms = refs[6:8]
+    sa, sb, rsem = refs[8:]
+
+    def product(a, slot):
+        if a == 0:
+            value = jnp.dot(outs[a][slot], weights[a][...], preferred_element_type=jnp.float32)
+        else:
+            value = lax.dot_general(outs[a][slot], weights[a][...], (((1,), (1,)), ((), ())),
+                                    preferred_element_type=jnp.float32)
+        terms[a][slot] = value.astype(terms[a].dtype)
+
     col = lax.axis_index("col")
     y, z, d = _row_ids()
     me = y * 4 + z
@@ -234,6 +245,8 @@
         next_b = dev(a, pa, lax.rem(pb + nb + d, nb))
         sends.append(send(a, ins[a], me, next_a, sa.at[a, 0]))
         sends.append(send(a, ins[a], me, next_b, sb.at[a, 0, 0]))
+    for a in range(2):
+        product(a, me)
     for s in range(1, 4):
         for a in range(2):
             na, nb, pa, pb, slot_of = geo[a]
@@ -244,6 +257,7 @@
             if s < na - 1:
                 sends.append(send(a, outs[a].at[slot], slot, next_a, sa.at[a, s]))
             sends.append(send(a, outs[a].at[slot], slot, next_b, sb.at[a, 0, s]))
+            product(a, slot)
     for t in range(1, 4):
         for j in range(4):
             for a in range(2):
@@ -253,19 +267,22 @@
                 wait_in(a, slot)
                 if t < nb - 1:
                     sends.append(send(a, outs[a].at[slot], slot, next_b, sb.at[a, t, j]))
+                product(a, slot)
     for cp in sends:
         cp.wait_send()
 
 
-def row_all_gather(first, second, cid):
+def row_all_gather(first, second, w_first, w_second, cid):
     n = lax.axis_size("row")
     ny = n // 4
     rows, cols = first.shape
+    width = w_first.shape[1]
     outs = pl.pallas_call(
         functools.partial(_row_ag_kernel, ny),
-        out_shape=[jax.ShapeDtypeStruct((n, rows, cols), first.dtype)] * 2,
-        in_specs=[pl.BlockSpec(memory_space=pltpu.VMEM)] * 2,
-        out_specs=[pl.BlockSpec(memory_space=pltpu.VMEM)] * 2,
+        out_shape=[jax.ShapeDtypeStruct((n, rows, cols), first.dtype)] * 2
+        + [jax.ShapeDtypeStruct((n, rows, width), jnp.bfloat16)] * 2,
+        in_specs=[pl.BlockSpec(memory_space=pltpu.VMEM)] * 4,
+        out_specs=[pl.BlockSpec(memory_space=pltpu.VMEM)] * 4,
         scratch_shapes=[
             pltpu.SemaphoreType.DMA((2, 4)),
             pltpu.SemaphoreType.DMA((2, 4, 4)),
@@ -273,8 +290,8 @@
         ],
         compiler_params=pltpu.CompilerParams(collective_id=cid, has_side_effects=True,
                                              vmem_limit_bytes=64 * 1024 * 1024),
-    )(first, second)
-    return [o.reshape(n * rows, cols) for o in outs]
+    )(first, second, w_first, w_second)
+    return [o.reshape(n * rows, o.shape[2]) for o in outs]
 
 
 def _row_rs_kernel(ny, *refs):
@@ -426,9 +443,7 @@
 
 
 def local(tokens, w_in, w_out, cotangent):
-    tokens_all, upstream_all = row_all_gather(tokens, cotangent, 3)
-    pre_term = jnp.dot(tokens_all, w_in, preferred_element_type=jnp.float32).astype(jnp.bfloat16)
-    dact_term = contract_last(upstream_all, w_out).astype(jnp.bfloat16)
+    tokens_all, upstream_all, pre_term, dact_term = row_all_gather(tokens, cotangent, w_in, w_out, 3)
     pre_part, dact_part = col_reduce_scatter([pre_term, dact_term], 1)
     act = jax.nn.gelu(pre_part, approximate=False).astype(jnp.bfloat16)
     dpre = (dact_part * gelu_grad(pre_part)).astype(jnp.bfloat16)

time: 219 us -> 212 us (0.968)
  matrix products: 21 us -> 10.4 us
  Pallas kernels: 176 us -> 180 us
    dot_general x2 -> x0, matrix products: 10.6 us -> none  [the longest x1 6.3 us: local(): jnp.dot(tokens_all, w_in, preferred_element_type=jnp.float32)]
    pallas_call x1, Pallas kernels: 34.7 us -> 38.4 us  [row_all_gather(): pl.pallas_call(functools.partial(_row_ag_kernel, ny), out_shape=[jax.Shap...]
where the time goes in v9:
time: 212 us
  Pallas kernels  180 us (85%)
  starting transfers between devices  10.8 us (5%)
  matrix products  10.4 us (5%)
  other arithmetic  7.02 us (3%)
  local copies, waits for them, and re-layouts  2.96 us (1%)
    pallas_call x1, Pallas kernels, col_reduce_scatter(): pl.pallas_call(functools.partial(_rs_kernel, nx, narr), out_shape=[jax.Sh...  55.6 us
    pallas_call x1, Pallas kernels, col_all_gather(): pl.pallas_call(functools.partial(_ag_kernel, nx, narr), out_shape=[jax.Sh...  47.9 us
    pallas_call x1, Pallas kernels, row_all_gather(): pl.pallas_call(functools.partial(_row_ag_kernel, ny), out_shape=[jax.Shap...  38.4 us
    pallas_call x1, Pallas kernels, row_reduce_scatter(): pl.pallas_call(functools.partial(_row_rs_kernel, ny), out_shape=[jax.Shap...  38.3 us
    all_to_all x1, starting transfers between devices, local(): lax.all_to_all(block_rows, 'col', split_axis=0, concat_axis=1, tiled=True)  10.8 us
    dot_general x1, matrix products, local(): lax.dot_general(act_all, upstream_all, (((0,), (0,)), ((), ())), preferre...  6.69 us
    convert_element_type x1, other arithmetic, local(): dpre = (dact_part * gelu_grad(pre_part)).astype(jnp.bfloat16)  4.67 us
  transfers between devices with their start and end apart: 1, of which 0 were waited for; matrix products, arithmetic and copies ran while one was open for 5% of the time, Pallas kernels for 0%

profile of v9, /device:TPU:1, one launch (start us, length us, event | category | flops | bytes accessed | tf_op | source)
XLA Modules:
  0.0 212.0 jit_solution(5864505294093065233)
XLA Ops:
  0.6 2.3 %copy.8 = bf16[512,1024]{0,1:T(8,128)(2,1)} copy(bf16[512,1024]{1,0:T(8,128)(2,1)} %refs_2_.2) | data formatting | bytes 2097152 | tf_op args[1]
  2.9 38.4 %shard_map.75 = (bf16[16,128,512]{2,1,0:T(8,128)(2,1)}, bf16[16,128,512]{2,1,0:T(8,128)(2,1)}, bf16[16,128,1024]{2,1,0:T(8,128)(2,1)}, bf16[16,128,1024]{2,1,0:T(8,128)(2,1)}) custom-call(bf16[128,512]{1,0:T(8,128)(2,1)} %refs_0_.1, bf16[128,512]{1,0:T(8,128)(2,1)} %refs_1_.1, bf16[512,1024]{1,0:T(8,128)(2,1)} %refs_2_.2, bf16[1024,512]{1,0:T(8,128)(2,1)} %refs_2_.3), custom_call_target="tpu_custom_call" | custom-call | tf_op jit(solution)/shard_map/pallas_call | solution.py:280
  41.3 55.6 %shard_map.76 = (f32[256,1024]{1,0:T(8,128)}, f32[256,1024]{1,0:T(8,128)}) custom-call(bf16[8,256,1024]{2,1,0:T(8,128)(2,1)} %bitcast.19, bf16[8,256,1024]{2,1,0:T(8,128)(2,1)} %bitcast.20), custom_call_target="tpu_custom_call" | custom-call | tf_op jit(solution)/shard_map/pallas_call | solution.py:83
  97.0 4.7 %fusion.8 = (bf16[256,1024]{1,0:T(8,128)(2,1)}, bf16[256,1024]{1,0:T(8,128)(2,1)}) fusion(f32[256,1024]{1,0:T(8,128)} %get-tuple-element.19, f32[256,1024]{1,0:T(8,128)} %get-tuple-element.18), kind=kLoop, calls=%fused_computation.10 | loop fusion | flops 19660800 | bytes 3145728 | tf_op jit(solution)/shard_map/convert_element_type | solution.py:449
  101.6 47.9 %shard_map.77 = (bf16[8,256,1024]{2,1,0:T(8,128)(2,1)}, bf16[8,256,1024]{2,1,0:T(8,128)(2,1)}, bf16[8,256,512]{2,1,0:T(8,128)(2,1)}, bf16[8,256,512]{2,1,0:T(8,128)(2,1)}) custom-call(bf16[256,1024]{1,0:T(8,128)(2,1)} %get-tuple-element.29.refs_0_, bf16[256,1024]{1,0:T(8,128)(2,1)} %get-tuple-element.28.refs_1_, bf16[1024,512]{1,0:T(8,128)(2,1)} %refs_2_.3, ...), custom_call_target="tpu_custom_call" | custom-call | tf_op jit(solution)/shard_map/pallas_call | solution.py:160
  149.5 38.3 %shard_map.78 = (f32[128,512]{1,0:T(8,128)}, f32[128,512]{1,0:T(8,128)}) custom-call(bf16[16,128,512]{2,1,0:T(8,128)(2,1)} %bitcast.21, bf16[16,128,512]{2,1,0:T(8,128)(2,1)} %bitcast.22), custom_call_target="tpu_custom_call" | custom-call | tf_op jit(solution)/shard_map/pallas_call | solution.py:369
  187.8 1.7 add_convert_fusion.1
  189.4 10.8 %all-to-all-start = ((bf16[8,16,512]{2,1,0:T(8,128)(2,1)}), bf16[8,16,512]{2,1,0:T(8,128)(2,1)S(1)}, u32[]{:S(2)}, u32[]{:S(2)}) async-start(bf16[8,16,512]{2,1,0:T(8,128)(2,1)} %bitcast.5), calls=%async_computation | async-start | bytes 262144 | tf_op jit(solution)/shard_map/all_to_all | solution.py:453
  200.3 0.0 copy-start.2
  200.3 0.0 copy-start.3
  200.3 6.7 %fusion.17 = f32[1024,512]{1,0:T(8,128)} fusion(bf16[2048,1024]{1,0:T(8,128)(2,1)} %bitcast.18, bf16[2048,512]{1,0:T(8,128)(2,1)} %bitcast.23), kind=kOutput, calls=%fused_computation.29 | convolution fusion | flops 2147483648 | bytes 8388608 | tf_op jit(solution)/shard_map/dot_general | solution.py:454
  207.0 0.0 copy-done.2
  207.0 0.0 copy-done.3
  207.0 0.0 copy-start
  207.0 0.0 copy-start.1
  207.0 3.7 %fusion.16 = f32[512,1024]{1,0:T(8,128)} fusion(bf16[2048,512]{1,0:T(8,128)(2,1)S(1)} %bitcast.27, bf16[2048,1024]{1,0:T(8,128)(2,1)S(1)} %bitcast.26), kind=kOutput, calls=%fused_computation.28 | convolution fusion | flops 2147483648 | bytes 8388608 | tf_op jit(solution)/shard_map/dot_general | solution.py:457
  210.7 0.0 copy-done
  210.7 0.0 copy-done.1
  210.7 0.7 add_convert_fusion
  211.3 0.0 all-to-all-done
  211.4 0.7 copy.10
Async XLA Ops:
  189.4 21.9 %all-to-all-start = ((bf16[8,16,512]{2,1,0:T(8,128)(2,1)}), bf16[8,16,512]{2,1,0:T(8,128)(2,1)S(1)}, u32[]{:S(2)}, u32[]{:S(2)}) async-start(bf16[8,16,512]{2,1,0:T(8,128)(2,1)} %bitcast.5), calls=%async_computation | async-start | bytes 262144 | tf_op jit(solution)/shard_map/all_to_all | solution.py:453
  200.3 6.7 %copy-start.2 = (bf16[8,256,1024]{2,1,0:T(8,128)(2,1)S(1)}, bf16[8,256,1024]{2,1,0:T(8,128)(2,1)}, u32[]{:S(2)}) copy-start(bf16[8,256,1024]{2,1,0:T(8,128)(2,1)} %get-tuple-element.25) | copy-start | bytes 12582916
  200.3 6.7 %copy-start.3 = (bf16[16,128,512]{2,1,0:T(8,128)(2,1)S(1)}, bf16[16,128,512]{2,1,0:T(8,128)(2,1)}, u32[]{:S(2)}) copy-start(bf16[16,128,512]{2,1,0:T(8,128)(2,1)} %get-tuple-element.24) | copy-start | bytes 6291460
  207.0 3.7 %copy-start = (bf16[128,512]{1,0:T(8,128)(2,1)S(1)}, bf16[128,512]{1,0:T(8,128)(2,1)}, u32[]{:S(2)}) copy-start(bf16[128,512]{1,0:T(8,128)(2,1)} %refs_1_.1) | copy-start | bytes 393220
  207.0 3.7 %copy-start.1 = (f32[128,512]{1,0:T(8,128)S(1)}, f32[128,512]{1,0:T(8,128)}, u32[]{:S(2)}) copy-start(f32[128,512]{1,0:T(8,128)} %get-tuple-element.23) | copy-start | bytes 786436

commit v10 on v9

--- a/solution.py
+++ b/solution.py
@@ -296,8 +296,27 @@
 
 def _row_rs_kernel(ny, *refs):
     ins = refs[:2]
-    outs = refs[2:4]
-    sb1, rb1, ssum, sb2, rb2, s1, r1, s2, r2 = refs[4:]
+    lefts = refs[2:4]
+    rights = refs[4:6]
+    outs = refs[6:8]
+    grads = refs[8:10]
+    sb1, rb1, ssum, sb2, rb2, s1, r1, s2, r2 = refs[10:]
+    span = 256
+    pending = [(g, c) for c in range(lefts[0].shape[0] // span) for g in range(2)]
+
+    def grad_work(count):
+        for _ in range(count):
+            if not pending:
+                return
+            g, c = pending.pop(0)
+            rows = pl.ds(c * span, span)
+            value = lax.dot_general(lefts[g][rows, :], rights[g][rows, :], (((0,), (0,)), ((), ())),
+                                    preferred_element_type=jnp.float32)
+            if c == 0:
+                grads[g][...] = value
+            else:
+                grads[g][...] += value
+
     col = lax.axis_index("col")
     y, z, d = _row_ids()
     barrier = pltpu.get_barrier_semaphore()
@@ -333,6 +352,7 @@
                       dev(a, lax.rem(pa + na + d, na), pb))
             sends.append(cp)
             first[a].append(cp)
+        grad_work(3)
         for a in range(2):
             first[a][s].wait_recv()
     for a in range(2):
@@ -352,25 +372,28 @@
                       dev(a, pa, lax.rem(pb + nb + d, nb)))
             sends.append(cp)
             second[a].append(cp)
+        grad_work(3)
         for a in range(2):
             second[a][t].wait_recv()
     for a in range(2):
         na, nb, pa, pb, slot_of = geo[a]
         outs[a][...] = rb2[a, 2].astype(jnp.float32) + ssum[a, pb]
+    grad_work(len(pending))
     for cp in sends:
         cp.wait_send()
 
 
-def row_reduce_scatter(first, second, cid):
+def row_reduce_scatter(first, second, lefts, rights, cid):
     n = lax.axis_size("row")
     ny = n // 4
     rows, cols = first.shape[0] // n, first.shape[1]
     ins = [v.reshape(n, rows, cols) for v in (first, second)]
+    grad_shapes = [jax.ShapeDtypeStruct((l.shape[1], r.shape[1]), jnp.float32) for l, r in zip(lefts, rights)]
     return pl.pallas_call(
         functools.partial(_row_rs_kernel, ny),
-        out_shape=[jax.ShapeDtypeStruct((rows, cols), jnp.float32)] * 2,
-        in_specs=[pl.BlockSpec(memory_space=pltpu.VMEM)] * 2,
-        out_specs=[pl.BlockSpec(memory_space=pltpu.VMEM)] * 2,
+        out_shape=[jax.ShapeDtypeStruct((rows, cols), jnp.float32)] * 2 + grad_shapes,
+        in_specs=[pl.BlockSpec(memory_space=pltpu.VMEM)] * 6,
+        out_specs=[pl.BlockSpec(memory_space=pltpu.VMEM)] * 4,
         scratch_shapes=[
             pltpu.VMEM((2, 3, 4, rows, cols), jnp.bfloat16),
             pltpu.VMEM((2, 3, 4, rows, cols), jnp.bfloat16),
@@ -384,7 +407,7 @@
         ],
         compiler_params=pltpu.CompilerParams(collective_id=cid, has_side_effects=True,
                                              vmem_limit_bytes=64 * 1024 * 1024),
-    )(*ins)
+    )(*ins, *lefts, *rights)
 
 
 def gelu_grad(value):
@@ -448,15 +471,10 @@
     act = jax.nn.gelu(pre_part, approximate=False).astype(jnp.bfloat16)
     dpre = (dact_part * gelu_grad(pre_part)).astype(jnp.bfloat16)
     (act_all, dpre_all), (mixed_term, back_term) = col_all_gather([act, dpre], [w_out, w_in.T], 2)
-    mixed, back = row_reduce_scatter(mixed_term, back_term, 4)
+    mixed, back, grad_out, grad_in = row_reduce_scatter(
+        mixed_term, back_term, [act_all, tokens_all], [upstream_all, dpre_all], 4)
     block_rows = (tokens.astype(jnp.float32) + mixed).astype(jnp.bfloat16)
     block_out = lax.all_to_all(block_rows, "col", split_axis=0, concat_axis=1, tiled=True)
-    grad_out = lax.dot_general(
-        act_all, upstream_all, (((0,), (0,)), ((), ())), preferred_element_type=jnp.float32
-    )
-    grad_in = lax.dot_general(
-        tokens_all, dpre_all, (((0,), (0,)), ((), ())), preferred_element_type=jnp.float32
-    )
     grad_tokens = (cotangent.astype(jnp.float32) + back).astype(jnp.bfloat16)
     return (block_out, grad_tokens, grad_in, grad_out)
 

time: 212 us -> 216 us (1.019)
  matrix products: 10.4 us -> 0 us
  Pallas kernels: 180 us -> 185 us
  local copies, waits for them, and re-layouts: 2.96 us -> 7.57 us
  waiting for transfers between devices: 0.01 us -> 3.63 us
    dot_general x2 -> x0, matrix products: 10.4 us -> none  [the longest x1 6.69 us: local(): lax.dot_general(act_all, upstream_all, (((0,), (0,)), ((), ())), preferre...]
    pallas_call x1, Pallas kernels: 38.3 us -> 43.4 us  [row_reduce_scatter(): pl.pallas_call(functools.partial(_row_rs_kernel, ny), out_shape=[jax.Shap...]
    unnamed x9 -> x5, local copies, waits for them, and re-layouts: 2.29 us -> 6.91 us
    all_to_all x1, waiting for transfers between devices: 0.01 us -> 3.63 us  [local(): lax.all_to_all(block_rows, 'col', split_axis=0, concat_axis=1, tiled=True)]
  transfers between devices with their start and end apart: 1 -> 1, of which waited for: 0 -> 1; matrix products, arithmetic and copies ran while one was open for 5% -> 1% of each run, Pallas kernels for 0% -> 0%
where the time goes in v10:
time: 216 us
  Pallas kernels  185 us (86%)
  starting transfers between devices  10.8 us (5%)
  other arithmetic  8 us (4%)
  local copies, waits for them, and re-layouts  7.57 us (4%)
  waiting for transfers between devices  3.63 us (2%)
    pallas_call x1, Pallas kernels, col_reduce_scatter(): pl.pallas_call(functools.partial(_rs_kernel, nx, narr), out_shape=[jax.Sh...  55.6 us
    pallas_call x1, Pallas kernels, col_all_gather(): pl.pallas_call(functools.partial(_ag_kernel, nx, narr), out_shape=[jax.Sh...  47.9 us
    pallas_call x1, Pallas kernels, row_reduce_scatter(): pl.pallas_call(functools.partial(_row_rs_kernel, ny), out_shape=[jax.Shap...  43.4 us
    pallas_call x1, Pallas kernels, row_all_gather(): pl.pallas_call(functools.partial(_row_ag_kernel, ny), out_shape=[jax.Shap...  38.4 us
    all_to_all x1, starting transfers between devices, local(): lax.all_to_all(block_rows, 'col', split_axis=0, concat_axis=1, tiled=True)  10.8 us
    unnamed x5, local copies, waits for them, and re-layouts  6.91 us
    convert_element_type x1, other arithmetic, local(): dpre = (dact_part * gelu_grad(pre_part)).astype(jnp.bfloat16)  4.67 us
  transfers between devices with their start and end apart: 1, of which 1 were waited for; matrix products, arithmetic and copies ran while one was open for 1% of the time, Pallas kernels for 0%

profile of v10, /device:TPU:1, one launch (start us, length us, event | category | flops | bytes accessed | tf_op | source)
XLA Modules:
  0.0 216.0 jit_solution(17309424494074476604)
XLA Ops:
  0.6 2.3 %copy.8 = bf16[512,1024]{0,1:T(8,128)(2,1)} copy(bf16[512,1024]{1,0:T(8,128)(2,1)} %refs_2_.2) | data formatting | bytes 2097152 | tf_op args[1]
  2.9 38.4 %shard_map.75 = (bf16[16,128,512]{2,1,0:T(8,128)(2,1)}, bf16[16,128,512]{2,1,0:T(8,128)(2,1)}, bf16[16,128,1024]{2,1,0:T(8,128)(2,1)}, bf16[16,128,1024]{2,1,0:T(8,128)(2,1)}) custom-call(bf16[128,512]{1,0:T(8,128)(2,1)} %refs_0_.1, bf16[128,512]{1,0:T(8,128)(2,1)} %refs_1_.1, bf16[512,1024]{1,0:T(8,128)(2,1)} %refs_2_.2, bf16[1024,512]{1,0:T(8,128)(2,1)} %refs_2_.3), custom_call_target="tpu_custom_call" | custom-call | tf_op jit(solution)/shard_map/pallas_call | solution.py:280
  41.4 55.6 %shard_map.76 = (f32[256,1024]{1,0:T(8,128)}, f32[256,1024]{1,0:T(8,128)}) custom-call(bf16[8,256,1024]{2,1,0:T(8,128)(2,1)} %bitcast.14, bf16[8,256,1024]{2,1,0:T(8,128)(2,1)} %bitcast.15), custom_call_target="tpu_custom_call" | custom-call | tf_op jit(solution)/shard_map/pallas_call | solution.py:83
  97.0 4.7 %fusion.8 = (bf16[256,1024]{1,0:T(8,128)(2,1)}, bf16[256,1024]{1,0:T(8,128)(2,1)}) fusion(f32[256,1024]{1,0:T(8,128)} %get-tuple-element.21, f32[256,1024]{1,0:T(8,128)} %get-tuple-element.20), kind=kLoop, calls=%fused_computation.10 | loop fusion | flops 19660800 | bytes 3145728 | tf_op jit(solution)/shard_map/convert_element_type | solution.py:472
  101.7 47.9 %shard_map.77 = (bf16[8,256,1024]{2,1,0:T(8,128)(2,1)}, bf16[8,256,1024]{2,1,0:T(8,128)(2,1)}, bf16[8,256,512]{2,1,0:T(8,128)(2,1)}, bf16[8,256,512]{2,1,0:T(8,128)(2,1)}) custom-call(bf16[256,1024]{1,0:T(8,128)(2,1)} %get-tuple-element.33.refs_0_, bf16[256,1024]{1,0:T(8,128)(2,1)} %get-tuple-element.32.refs_1_, bf16[1024,512]{1,0:T(8,128)(2,1)} %refs_2_.3, ...), custom_call_target="tpu_custom_call" | custom-call | tf_op jit(solution)/shard_map/pallas_call | solution.py:160
  149.5 43.4 %shard_map.78 = (f32[128,512]{1,0:T(8,128)}, f32[128,512]{1,0:T(8,128)}, f32[1024,512]{1,0:T(8,128)}, f32[512,1024]{1,0:T(8,128)}) custom-call(bf16[16,128,512]{2,1,0:T(8,128)(2,1)} %bitcast.20, bf16[16,128,512]{2,1,0:T(8,128)(2,1)} %bitcast.21, bf16[2048,1024]{1,0:T(8,128)(2,1)} %bitcast.16, bf16[2048,512]{1,0:T(8,128)(2,1)} %bitcast.18, ...), custom_call_target="tpu_custom_call" | custom-call | tf_op jit(solution)/shard_map/pallas_call | solution.py:392
  193.0 1.7 add_convert_fusion.1
  194.6 10.8 %all-to-all-start = ((bf16[8,16,512]{2,1,0:T(8,128)(2,1)}), bf16[8,16,512]{2,1,0:T(8,128)(2,1)S(1)}, u32[]{:S(2)}, u32[]{:S(2)}) async-start(bf16[8,16,512]{2,1,0:T(8,128)(2,1)} %bitcast.9), calls=%async_computation | async-start | bytes 262144 | tf_op jit(solution)/shard_map/all_to_all | solution.py:477
  205.4 1.7 add_convert_fusion
  207.1 3.6 %all-to-all-done = bf16[8,16,512]{2,1,0:T(8,128)(2,1)S(1)} async-done(((bf16[8,16,512]{2,1,0:T(8,128)(2,1)}), bf16[8,16,512]{2,1,0:T(8,128)(2,1)S(1)}, u32[]{:S(2)}, u32[]{:S(2)}) %all-to-all-start) | async-done | bytes 131104 | tf_op jit(solution)/shard_map/all_to_all | solution.py:477
  210.7 0.7 copy.10
  211.4 0.0 copy-start
  211.4 3.3 %copy.13 = f32[512,1024]{1,0:T(8,128)} copy(f32[512,1024]{1,0:T(8,128)} %get-tuple-element.40) | data formatting | bytes 4194304
  214.7 0.0 copy-done
  214.7 1.3 copy.14
Async XLA Ops:
  194.6 16.1 %all-to-all-start = ((bf16[8,16,512]{2,1,0:T(8,128)(2,1)}), bf16[8,16,512]{2,1,0:T(8,128)(2,1)S(1)}, u32[]{:S(2)}, u32[]{:S(2)}) async-start(bf16[8,16,512]{2,1,0:T(8,128)(2,1)} %bitcast.9), calls=%async_computation | async-start | bytes 262144 | tf_op jit(solution)/shard_map/all_to_all | solution.py:477
  211.4 3.3 %copy-start = (f32[1024,512]{1,0:T(8,128)S(1)}, f32[1024,512]{1,0:T(8,128)}, u32[]{:S(2)}) copy-start(f32[1024,512]{1,0:T(8,128)} %get-tuple-element.41) | copy-start | bytes 6291460

commit v11 on v9

--- a/solution.py
+++ b/solution.py
@@ -29,36 +29,42 @@
 def _rs_kernel(nx, narr, *refs):
     parts = refs[:narr]
     outs = refs[narr:2 * narr]
-    recv1, vsum, sendbuf, recv2, s1, r1, s2, r2 = refs[2 * narr:]
+    recv1, sendbuf, recv2, s1, r1, s2, r2 = refs[2 * narr:]
     row = lax.axis_index("row")
     x, k, d, nxt, prv = _col_ids(nx)
     _greet(row, k, x, nxt, prv)
     partner = (row, 2 * x + 1 - k)
     nextdev = (row, 2 * nxt + k)
+
+    def order(j, sign):
+        if j == nx - 1:
+            return x
+        return lax.rem(x + 4 * nx + sign * d * (j + 1), nx)
+
     first = []
-    for a in range(narr):
-        for i in range(nx):
+    for j in range(nx):
+        for a in range(narr):
             cp = pltpu.make_async_remote_copy(
-                src_ref=parts[a].at[2 * i + 1 - k], dst_ref=recv1.at[a, i],
-                send_sem=s1.at[a, i], recv_sem=r1.at[a, i],
+                src_ref=parts[a].at[2 * order(j, 1) + 1 - k], dst_ref=recv1.at[a, j],
+                send_sem=s1.at[a, j], recv_sem=r1.at[a, j],
                 device_id=partner, device_id_type=MESH)
             cp.start()
             first.append(cp)
-    for cp in first:
-        cp.wait()
-    for a in range(narr):
-        for i in range(nx):
-            vsum[a, i] = parts[a][2 * i + k].astype(jnp.float32) + recv1[a, i].astype(jnp.float32)
+
+    def chip_sum(a, j):
+        first[j * narr + a].wait_recv()
+        own = parts[a][2 * order(j, -1) + k].astype(jnp.float32)
+        return own + recv1[a, j].astype(jnp.float32)
+
     ring = []
     for step in range(nx - 1):
         for a in range(narr):
-            src_idx = lax.rem(x + 4 * nx - d * (step + 1), nx)
+            value = chip_sum(a, step)
             if step == 0:
-                sendbuf[a, step] = vsum[a, src_idx].astype(sendbuf.dtype)
+                sendbuf[a, step] = value.astype(sendbuf.dtype)
             else:
-                prevcp = ring[(step - 1) * narr + a]
-                prevcp.wait_recv()
-                sendbuf[a, step] = (recv2[a, step - 1].astype(jnp.float32) + vsum[a, src_idx]).astype(sendbuf.dtype)
+                ring[(step - 1) * narr + a].wait_recv()
+                sendbuf[a, step] = (recv2[a, step - 1].astype(jnp.float32) + value).astype(sendbuf.dtype)
             cp = pltpu.make_async_remote_copy(
                 src_ref=sendbuf.at[a, step], dst_ref=recv2.at[a, step],
                 send_sem=s2.at[a, step], recv_sem=r2.at[a, step],
@@ -66,9 +72,11 @@
             cp.start()
             ring.append(cp)
     for a in range(narr):
-        last = ring[(nx - 2) * narr + a]
-        last.wait_recv()
-        outs[a][...] = recv2[a, nx - 2].astype(jnp.float32) + vsum[a, x]
+        value = chip_sum(a, nx - 1)
+        ring[(nx - 2) * narr + a].wait_recv()
+        outs[a][...] = recv2[a, nx - 2].astype(jnp.float32) + value
+    for cp in first:
+        cp.wait_send()
     for cp in ring:
         cp.wait_send()
 
@@ -87,7 +95,6 @@
         out_specs=[pl.BlockSpec(memory_space=pltpu.VMEM)] * narr,
         scratch_shapes=[
             pltpu.VMEM((narr, nx, rows, cols), jnp.bfloat16),
-            pltpu.VMEM((narr, nx, rows, cols), jnp.float32),
             pltpu.VMEM((narr, nx - 1, rows, cols), jnp.bfloat16),
             pltpu.VMEM((narr, nx - 1, rows, cols), jnp.bfloat16),
             pltpu.SemaphoreType.DMA((narr, nx)),

time: 212 us -> 205 us (0.967)
  Pallas kernels: 180 us -> 173 us
    pallas_call x1, Pallas kernels: 55.6 us -> 49 us  [col_reduce_scatter(): pl.pallas_call(functools.partial(_rs_kernel, nx, narr), out_shape=[jax.Sh...]
where the time goes in v11:
time: 205 us
  Pallas kernels  173 us (84%)
  starting transfers between devices  10.8 us (5%)
  matrix products  10.3 us (5%)
  other arithmetic  7.02 us (3%)
  local copies, waits for them, and re-layouts  2.96 us (1%)
    pallas_call x1, Pallas kernels, col_reduce_scatter(): pl.pallas_call(functools.partial(_rs_kernel, nx, narr), out_shape=[jax.Sh...  49 us
    pallas_call x1, Pallas kernels, col_all_gather(): pl.pallas_call(functools.partial(_ag_kernel, nx, narr), out_shape=[jax.Sh...  47.4 us
    pallas_call x1, Pallas kernels, row_all_gather(): pl.pallas_call(functools.partial(_row_ag_kernel, ny), out_shape=[jax.Shap...  38.4 us
    pallas_call x1, Pallas kernels, row_reduce_scatter(): pl.pallas_call(functools.partial(_row_rs_kernel, ny), out_shape=[jax.Shap...  38.3 us
    all_to_all x1, starting transfers between devices, local(): lax.all_to_all(block_rows, 'col', split_axis=0, concat_axis=1, tiled=True)  10.8 us
    dot_general x1, matrix products, local(): lax.dot_general(act_all, upstream_all, (((0,), (0,)), ((), ())), preferre...  6.68 us
    convert_element_type x1, other arithmetic, local(): dpre = (dact_part * gelu_grad(pre_part)).astype(jnp.bfloat16)  4.67 us
  transfers between devices with their start and end apart: 1, of which 0 were waited for; matrix products, arithmetic and copies ran while one was open for 5% of the time, Pallas kernels for 0%

profile of v11, /device:TPU:1, one launch (start us, length us, event | category | flops | bytes accessed | tf_op | source)
XLA Modules:
  0.0 205.0 jit_solution(18199168218156383689)
XLA Ops:
  0.6 2.3 %copy.8 = bf16[512,1024]{0,1:T(8,128)(2,1)} copy(bf16[512,1024]{1,0:T(8,128)(2,1)} %refs_2_.2) | data formatting | bytes 2097152 | tf_op args[1]
  2.9 38.4 %shard_map.75 = (bf16[16,128,512]{2,1,0:T(8,128)(2,1)}, bf16[16,128,512]{2,1,0:T(8,128)(2,1)}, bf16[16,128,1024]{2,1,0:T(8,128)(2,1)}, bf16[16,128,1024]{2,1,0:T(8,128)(2,1)}) custom-call(bf16[128,512]{1,0:T(8,128)(2,1)} %refs_0_.1, bf16[128,512]{1,0:T(8,128)(2,1)} %refs_1_.1, bf16[512,1024]{1,0:T(8,128)(2,1)} %refs_2_.2, bf16[1024,512]{1,0:T(8,128)(2,1)} %refs_2_.3), custom_call_target="tpu_custom_call" | custom-call | tf_op jit(solution)/shard_map/pallas_call | solution.py:287
  41.3 49.0 %shard_map.76 = (f32[256,1024]{1,0:T(8,128)}, f32[256,1024]{1,0:T(8,128)}) custom-call(bf16[8,256,1024]{2,1,0:T(8,128)(2,1)} %bitcast.19, bf16[8,256,1024]{2,1,0:T(8,128)(2,1)} %bitcast.20), custom_call_target="tpu_custom_call" | custom-call | tf_op jit(solution)/shard_map/pallas_call | solution.py:91
  90.4 4.7 %fusion.8 = (bf16[256,1024]{1,0:T(8,128)(2,1)}, bf16[256,1024]{1,0:T(8,128)(2,1)}) fusion(f32[256,1024]{1,0:T(8,128)} %get-tuple-element.19, f32[256,1024]{1,0:T(8,128)} %get-tuple-element.18), kind=kLoop, calls=%fused_computation.10 | loop fusion | flops 19660800 | bytes 3145728 | tf_op jit(solution)/shard_map/convert_element_type | solution.py:456
  95.1 47.4 %shard_map.77 = (bf16[8,256,1024]{2,1,0:T(8,128)(2,1)}, bf16[8,256,1024]{2,1,0:T(8,128)(2,1)}, bf16[8,256,512]{2,1,0:T(8,128)(2,1)}, bf16[8,256,512]{2,1,0:T(8,128)(2,1)}) custom-call(bf16[256,1024]{1,0:T(8,128)(2,1)} %get-tuple-element.29.refs_0_, bf16[256,1024]{1,0:T(8,128)(2,1)} %get-tuple-element.28.refs_1_, bf16[1024,512]{1,0:T(8,128)(2,1)} %refs_2_.3, ...), custom_call_target="tpu_custom_call" | custom-call | tf_op jit(solution)/shard_map/pallas_call | solution.py:167
  142.5 38.3 %shard_map.78 = (f32[128,512]{1,0:T(8,128)}, f32[128,512]{1,0:T(8,128)}) custom-call(bf16[16,128,512]{2,1,0:T(8,128)(2,1)} %bitcast.21, bf16[16,128,512]{2,1,0:T(8,128)(2,1)} %bitcast.22), custom_call_target="tpu_custom_call" | custom-call | tf_op jit(solution)/shard_map/pallas_call | solution.py:376
  180.7 1.7 add_convert_fusion.1
  182.4 10.8 %all-to-all-start = ((bf16[8,16,512]{2,1,0:T(8,128)(2,1)}), bf16[8,16,512]{2,1,0:T(8,128)(2,1)S(1)}, u32[]{:S(2)}, u32[]{:S(2)}) async-start(bf16[8,16,512]{2,1,0:T(8,128)(2,1)} %bitcast.5), calls=%async_computation | async-start | bytes 262144 | tf_op jit(solution)/shard_map/all_to_all | solution.py:460
  193.3 0.0 copy-start.2
  193.3 0.0 copy-start.3
  193.3 6.7 %fusion.17 = f32[1024,512]{1,0:T(8,128)} fusion(bf16[2048,1024]{1,0:T(8,128)(2,1)} %bitcast.18, bf16[2048,512]{1,0:T(8,128)(2,1)} %bitcast.23), kind=kOutput, calls=%fused_computation.29 | convolution fusion | flops 2147483648 | bytes 8388608 | tf_op jit(solution)/shard_map/dot_general | solution.py:461
  199.9 0.0 copy-done.2
  199.9 0.0 copy-done.3
  199.9 0.0 copy-start
  199.9 0.0 copy-start.1
  200.0 3.7 %fusion.16 = f32[512,1024]{1,0:T(8,128)} fusion(bf16[2048,512]{1,0:T(8,128)(2,1)S(1)} %bitcast.27, bf16[2048,1024]{1,0:T(8,128)(2,1)S(1)} %bitcast.26), kind=kOutput, calls=%fused_computation.28 | convolution fusion | flops 2147483648 | bytes 8388608 | tf_op jit(solution)/shard_map/dot_general | solution.py:464
  203.6 0.0 copy-done
  203.6 0.0 copy-done.1
  203.6 0.7 add_convert_fusion
  204.3 0.0 all-to-all-done
  204.3 0.7 copy.10
Async XLA Ops:
  182.4 21.9 %all-to-all-start = ((bf16[8,16,512]{2,1,0:T(8,128)(2,1)}), bf16[8,16,512]{2,1,0:T(8,128)(2,1)S(1)}, u32[]{:S(2)}, u32[]{:S(2)}) async-start(bf16[8,16,512]{2,1,0:T(8,128)(2,1)} %bitcast.5), calls=%async_computation | async-start | bytes 262144 | tf_op jit(solution)/shard_map/all_to_all | solution.py:460
  193.3 6.7 %copy-start.2 = (bf16[8,256,1024]{2,1,0:T(8,128)(2,1)S(1)}, bf16[8,256,1024]{2,1,0:T(8,128)(2,1)}, u32[]{:S(2)}) copy-start(bf16[8,256,1024]{2,1,0:T(8,128)(2,1)} %get-tuple-element.25) | copy-start | bytes 12582916
  193.3 6.7 %copy-start.3 = (bf16[16,128,512]{2,1,0:T(8,128)(2,1)S(1)}, bf16[16,128,512]{2,1,0:T(8,128)(2,1)}, u32[]{:S(2)}) copy-start(bf16[16,128,512]{2,1,0:T(8,128)(2,1)} %get-tuple-element.24) | copy-start | bytes 6291460
  199.9 3.7 %copy-start = (bf16[128,512]{1,0:T(8,128)(2,1)S(1)}, bf16[128,512]{1,0:T(8,128)(2,1)}, u32[]{:S(2)}) copy-start(bf16[128,512]{1,0:T(8,128)(2,1)} %refs_1_.1) | copy-start | bytes 393220
  199.9 3.7 %copy-start.1 = (f32[128,512]{1,0:T(8,128)S(1)}, f32[128,512]{1,0:T(8,128)}, u32[]{:S(2)}) copy-start(f32[128,512]{1,0:T(8,128)} %get-tuple-element.23) | copy-start | bytes 786436

commit v12 on v11

--- a/solution.py
+++ b/solution.py
@@ -149,13 +149,17 @@
             core.append(cc)
         for a in range(narr):
             product(a, 2 * lax.rem(x + 4 * nx - d * step, nx) + k)
+        if step > 0:
+            for a in range(narr):
+                core[(step - 1) * narr + a].wait()
+            for a in range(narr):
+                product(a, 2 * lax.rem(x + 4 * nx + d * (step - 1), nx) + 1 - k)
     for cp in ring:
         cp.wait_send()
-    for step in range(nx):
-        for a in range(narr):
-            core[step * narr + a].wait()
-        for a in range(narr):
-            product(a, 2 * lax.rem(x + 4 * nx + d * step, nx) + 1 - k)
+    for a in range(narr):
+        core[(nx - 1) * narr + a].wait()
+    for a in range(narr):
+        product(a, 2 * lax.rem(x + 4 * nx + d * (nx - 1), nx) + 1 - k)
 
 
 def col_all_gather(arrays, weights, cid):

time: 205 us -> 204 us (level)
  no operation moved by 1% of the time
where the time goes in v12:
time: 204 us
  Pallas kernels  173 us (85%)
  matrix products  10.3 us (5%)
  starting transfers between devices  9.23 us (5%)
  other arithmetic  7.02 us (3%)
  local copies, waits for them, and re-layouts  2.96 us (1%)
    pallas_call x1, Pallas kernels, col_reduce_scatter(): pl.pallas_call(functools.partial(_rs_kernel, nx, narr), out_shape=[jax.Sh...  49 us
    pallas_call x1, Pallas kernels, col_all_gather(): pl.pallas_call(functools.partial(_ag_kernel, nx, narr), out_shape=[jax.Sh...  47.4 us
    pallas_call x1, Pallas kernels, row_reduce_scatter(): pl.pallas_call(functools.partial(_row_rs_kernel, ny), out_shape=[jax.Shap...  38.5 us
    pallas_call x1, Pallas kernels, row_all_gather(): pl.pallas_call(functools.partial(_row_ag_kernel, ny), out_shape=[jax.Shap...  38.4 us
    all_to_all x1, starting transfers between devices, local(): lax.all_to_all(block_rows, 'col', split_axis=0, concat_axis=1, tiled=True)  9.23 us
    dot_general x1, matrix products, local(): lax.dot_general(act_all, upstream_all, (((0,), (0,)), ((), ())), preferre...  6.68 us
    convert_element_type x1, other arithmetic, local(): dpre = (dact_part * gelu_grad(pre_part)).astype(jnp.bfloat16)  4.67 us
  transfers between devices with their start and end apart: 1, of which 0 were waited for; matrix products, arithmetic and copies ran while one was open for 5% of the time, Pallas kernels for 0%

profile of v12, /device:TPU:1, one launch (start us, length us, event | category | flops | bytes accessed | tf_op | source)
XLA Modules:
  0.0 203.7 jit_solution(8692409845754939156)
XLA Ops:
  0.6 2.3 %copy.8 = bf16[512,1024]{0,1:T(8,128)(2,1)} copy(bf16[512,1024]{1,0:T(8,128)(2,1)} %refs_2_.2) | data formatting | bytes 2097152 | tf_op args[1]
  2.9 38.4 %shard_map.75 = (bf16[16,128,512]{2,1,0:T(8,128)(2,1)}, bf16[16,128,512]{2,1,0:T(8,128)(2,1)}, bf16[16,128,1024]{2,1,0:T(8,128)(2,1)}, bf16[16,128,1024]{2,1,0:T(8,128)(2,1)}) custom-call(bf16[128,512]{1,0:T(8,128)(2,1)} %refs_0_.1, bf16[128,512]{1,0:T(8,128)(2,1)} %refs_1_.1, bf16[512,1024]{1,0:T(8,128)(2,1)} %refs_2_.2, bf16[1024,512]{1,0:T(8,128)(2,1)} %refs_2_.3), custom_call_target="tpu_custom_call" | custom-call | tf_op jit(solution)/shard_map/pallas_call | solution.py:291
  41.3 49.0 %shard_map.76 = (f32[256,1024]{1,0:T(8,128)}, f32[256,1024]{1,0:T(8,128)}) custom-call(bf16[8,256,1024]{2,1,0:T(8,128)(2,1)} %bitcast.19, bf16[8,256,1024]{2,1,0:T(8,128)(2,1)} %bitcast.20), custom_call_target="tpu_custom_call" | custom-call | tf_op jit(solution)/shard_map/pallas_call | solution.py:91
  90.4 4.7 %fusion.8 = (bf16[256,1024]{1,0:T(8,128)(2,1)}, bf16[256,1024]{1,0:T(8,128)(2,1)}) fusion(f32[256,1024]{1,0:T(8,128)} %get-tuple-element.19, f32[256,1024]{1,0:T(8,128)} %get-tuple-element.18), kind=kLoop, calls=%fused_computation.10 | loop fusion | flops 19660800 | bytes 3145728 | tf_op jit(solution)/shard_map/convert_element_type | solution.py:460
  95.1 47.4 %shard_map.77 = (bf16[8,256,1024]{2,1,0:T(8,128)(2,1)}, bf16[8,256,1024]{2,1,0:T(8,128)(2,1)}, bf16[8,256,512]{2,1,0:T(8,128)(2,1)}, bf16[8,256,512]{2,1,0:T(8,128)(2,1)}) custom-call(bf16[256,1024]{1,0:T(8,128)(2,1)} %get-tuple-element.29.refs_0_, bf16[256,1024]{1,0:T(8,128)(2,1)} %get-tuple-element.28.refs_1_, bf16[1024,512]{1,0:T(8,128)(2,1)} %refs_2_.3, ...), custom_call_target="tpu_custom_call" | custom-call | tf_op jit(solution)/shard_map/pallas_call | solution.py:171
  142.5 38.5 %shard_map.78 = (f32[128,512]{1,0:T(8,128)}, f32[128,512]{1,0:T(8,128)}) custom-call(bf16[16,128,512]{2,1,0:T(8,128)(2,1)} %bitcast.21, bf16[16,128,512]{2,1,0:T(8,128)(2,1)} %bitcast.22), custom_call_target="tpu_custom_call" | custom-call | tf_op jit(solution)/shard_map/pallas_call | solution.py:380
  181.0 1.7 add_convert_fusion.1
  182.7 9.2 %all-to-all-start = ((bf16[8,16,512]{2,1,0:T(8,128)(2,1)}), bf16[8,16,512]{2,1,0:T(8,128)(2,1)S(1)}, u32[]{:S(2)}, u32[]{:S(2)}) async-start(bf16[8,16,512]{2,1,0:T(8,128)(2,1)} %bitcast.5), calls=%async_computation | async-start | bytes 262144 | tf_op jit(solution)/shard_map/all_to_all | solution.py:464
  191.9 0.0 copy-start.2
  191.9 0.0 copy-start.3
  191.9 6.7 %fusion.17 = f32[1024,512]{1,0:T(8,128)} fusion(bf16[2048,1024]{1,0:T(8,128)(2,1)} %bitcast.18, bf16[2048,512]{1,0:T(8,128)(2,1)} %bitcast.23), kind=kOutput, calls=%fused_computation.29 | convolution fusion | flops 2147483648 | bytes 8388608 | tf_op jit(solution)/shard_map/dot_general | solution.py:465
  198.6 0.0 copy-done.2
  198.6 0.0 copy-done.3
  198.6 0.0 copy-start
  198.6 0.0 copy-start.1
  198.6 3.7 %fusion.16 = f32[512,1024]{1,0:T(8,128)} fusion(bf16[2048,512]{1,0:T(8,128)(2,1)S(1)} %bitcast.27, bf16[2048,1024]{1,0:T(8,128)(2,1)S(1)} %bitcast.26), kind=kOutput, calls=%fused_computation.28 | convolution fusion | flops 2147483648 | bytes 8388608 | tf_op jit(solution)/shard_map/dot_general | solution.py:468
  202.3 0.0 copy-done
  202.3 0.0 copy-done.1
  202.3 0.7 add_convert_fusion
  203.0 0.0 all-to-all-done
  203.0 0.7 copy.10
Async XLA Ops:
  182.7 20.3 %all-to-all-start = ((bf16[8,16,512]{2,1,0:T(8,128)(2,1)}), bf16[8,16,512]{2,1,0:T(8,128)(2,1)S(1)}, u32[]{:S(2)}, u32[]{:S(2)}) async-start(bf16[8,16,512]{2,1,0:T(8,128)(2,1)} %bitcast.5), calls=%async_computation | async-start | bytes 262144 | tf_op jit(solution)/shard_map/all_to_all | solution.py:464
  191.9 6.7 %copy-start.2 = (bf16[8,256,1024]{2,1,0:T(8,128)(2,1)S(1)}, bf16[8,256,1024]{2,1,0:T(8,128)(2,1)}, u32[]{:S(2)}) copy-start(bf16[8,256,1024]{2,1,0:T(8,128)(2,1)} %get-tuple-element.25) | copy-start | bytes 12582916
  191.9 6.7 %copy-start.3 = (bf16[16,128,512]{2,1,0:T(8,128)(2,1)S(1)}, bf16[16,128,512]{2,1,0:T(8,128)(2,1)}, u32[]{:S(2)}) copy-start(bf16[16,128,512]{2,1,0:T(8,128)(2,1)} %get-tuple-element.24) | copy-start | bytes 6291460
  198.6 3.7 %copy-start = (bf16[128,512]{1,0:T(8,128)(2,1)S(1)}, bf16[128,512]{1,0:T(8,128)(2,1)}, u32[]{:S(2)}) copy-start(bf16[128,512]{1,0:T(8,128)(2,1)} %refs_1_.1) | copy-start | bytes 393220
  198.6 3.7 %copy-start.1 = (f32[128,512]{1,0:T(8,128)S(1)}, f32[128,512]{1,0:T(8,128)}, u32[]{:S(2)}) copy-start(f32[128,512]{1,0:T(8,128)} %get-tuple-element.23) | copy-start | bytes 786436

commit v13 on v12

--- a/solution.py
+++ b/solution.py
@@ -329,26 +329,27 @@
         return cp
 
     sends = []
-    first = [[] for _ in range(2)]
+    first = {}
     for s in range(4 - 1):
+        for bq in range(4):
+            for a in range(2):
+                na, nb, pa, pb, slot_of = geo[a]
+                slot = slot_of(lax.rem(pa + 4 * na - d * (s + 1), na), bq)
+                if s == 0:
+                    src = ins[a].at[slot]
+                else:
+                    first[(a, s - 1, bq)].wait_recv()
+                    sb1[a, s, bq] = (rb1[a, s - 1, bq].astype(jnp.float32)
+                                     + ins[a][slot].astype(jnp.float32)).astype(sb1.dtype)
+                    src = sb1.at[a, s, bq]
+                cp = send(src, rb1.at[a, s, bq], s1.at[a, s, bq], r1.at[a, s, bq],
+                          dev(a, lax.rem(pa + na + d, na), pb))
+                sends.append(cp)
+                first[(a, s, bq)] = cp
+    for bq in range(4):
         for a in range(2):
             na, nb, pa, pb, slot_of = geo[a]
-            pos = lax.rem(pa + 4 * na - d * (s + 1), na)
-            for bq in range(nb):
-                own = ins[a][slot_of(pos, bq)]
-                if s == 0:
-                    sb1[a, s, bq] = own
-                else:
-                    sb1[a, s, bq] = (rb1[a, s - 1, bq].astype(jnp.float32) + own.astype(jnp.float32)).astype(sb1.dtype)
-            cp = send(sb1.at[a, s], rb1.at[a, s], s1.at[a, s], r1.at[a, s],
-                      dev(a, lax.rem(pa + na + d, na), pb))
-            sends.append(cp)
-            first[a].append(cp)
-        for a in range(2):
-            first[a][s].wait_recv()
-    for a in range(2):
-        na, nb, pa, pb, slot_of = geo[a]
-        for bq in range(nb):
+            first[(a, 2, bq)].wait_recv()
             ssum[a, bq] = rb1[a, 2, bq].astype(jnp.float32) + ins[a][slot_of(pa, bq)].astype(jnp.float32)
     second = [[] for _ in range(2)]
     for t in range(4 - 1):
@@ -388,8 +389,8 @@
             pltpu.VMEM((2, 4, rows, cols), jnp.float32),
             pltpu.VMEM((2, 3, rows, cols), jnp.bfloat16),
             pltpu.VMEM((2, 3, rows, cols), jnp.bfloat16),
-            pltpu.SemaphoreType.DMA((2, 3)),
-            pltpu.SemaphoreType.DMA((2, 3)),
+            pltpu.SemaphoreType.DMA((2, 3, 4)),
+            pltpu.SemaphoreType.DMA((2, 3, 4)),
             pltpu.SemaphoreType.DMA((2, 3)),
             pltpu.SemaphoreType.DMA((2, 3)),
         ],

time: 204 us -> 198 us (0.971)
  Pallas kernels: 173 us -> 169 us
  starting transfers between devices: 9.23 us -> 7.18 us
    pallas_call x1, Pallas kernels: 38.5 us -> 34.5 us  [row_reduce_scatter(): pl.pallas_call(functools.partial(_row_rs_kernel, ny), out_shape=[jax.Shap...]
    all_to_all x1, starting transfers between devices: 9.23 us -> 7.18 us  [local(): lax.all_to_all(block_rows, 'col', split_axis=0, concat_axis=1, tiled=True)]
  transfers between devices with their start and end apart: 1 -> 1, of which waited for: 0 -> 0; matrix products, arithmetic and copies ran while one was open for 5% -> 6% of each run, Pallas kernels for 0% -> 0%
where the time goes in v13:
time: 198 us
  Pallas kernels  169 us (85%)
  matrix products  10.3 us (5%)
  starting transfers between devices  7.18 us (4%)
  other arithmetic  7.02 us (4%)
  local copies, waits for them, and re-layouts  2.96 us (1%)
    pallas_call x1, Pallas kernels, col_reduce_scatter(): pl.pallas_call(functools.partial(_rs_kernel, nx, narr), out_shape=[jax.Sh...  49 us
    pallas_call x1, Pallas kernels, col_all_gather(): pl.pallas_call(functools.partial(_ag_kernel, nx, narr), out_shape=[jax.Sh...  47.4 us
    pallas_call x1, Pallas kernels, row_all_gather(): pl.pallas_call(functools.partial(_row_ag_kernel, ny), out_shape=[jax.Shap...  38.4 us
    pallas_call x1, Pallas kernels, row_reduce_scatter(): pl.pallas_call(functools.partial(_row_rs_kernel, ny), out_shape=[jax.Shap...  34.5 us
    all_to_all x1, starting transfers between devices, local(): lax.all_to_all(block_rows, 'col', split_axis=0, concat_axis=1, tiled=True)  7.18 us
    dot_general x1, matrix products, local(): lax.dot_general(act_all, upstream_all, (((0,), (0,)), ((), ())), preferre...  6.68 us
    convert_element_type x1, other arithmetic, local(): dpre = (dact_part * gelu_grad(pre_part)).astype(jnp.bfloat16)  4.67 us
  transfers between devices with their start and end apart: 1, of which 0 were waited for; matrix products, arithmetic and copies ran while one was open for 6% of the time, Pallas kernels for 0%

profile of v13, /device:TPU:1, one launch (start us, length us, event | category | flops | bytes accessed | tf_op | source)
XLA Modules:
  0.0 197.6 jit_solution(2419034352529350168)
XLA Ops:
  0.6 2.3 %copy.8 = bf16[512,1024]{0,1:T(8,128)(2,1)} copy(bf16[512,1024]{1,0:T(8,128)(2,1)} %refs_2_.2) | data formatting | bytes 2097152 | tf_op args[1]
  2.9 38.4 %shard_map.75 = (bf16[16,128,512]{2,1,0:T(8,128)(2,1)}, bf16[16,128,512]{2,1,0:T(8,128)(2,1)}, bf16[16,128,1024]{2,1,0:T(8,128)(2,1)}, bf16[16,128,1024]{2,1,0:T(8,128)(2,1)}) custom-call(bf16[128,512]{1,0:T(8,128)(2,1)} %refs_0_.1, bf16[128,512]{1,0:T(8,128)(2,1)} %refs_1_.1, bf16[512,1024]{1,0:T(8,128)(2,1)} %refs_2_.2, bf16[1024,512]{1,0:T(8,128)(2,1)} %refs_2_.3), custom_call_target="tpu_custom_call" | custom-call | tf_op jit(solution)/shard_map/pallas_call | solution.py:291
  41.3 49.0 %shard_map.76 = (f32[256,1024]{1,0:T(8,128)}, f32[256,1024]{1,0:T(8,128)}) custom-call(bf16[8,256,1024]{2,1,0:T(8,128)(2,1)} %bitcast.19, bf16[8,256,1024]{2,1,0:T(8,128)(2,1)} %bitcast.20), custom_call_target="tpu_custom_call" | custom-call | tf_op jit(solution)/shard_map/pallas_call | solution.py:91
  90.4 4.7 %fusion.8 = (bf16[256,1024]{1,0:T(8,128)(2,1)}, bf16[256,1024]{1,0:T(8,128)(2,1)}) fusion(f32[256,1024]{1,0:T(8,128)} %get-tuple-element.19, f32[256,1024]{1,0:T(8,128)} %get-tuple-element.18), kind=kLoop, calls=%fused_computation.10 | loop fusion | flops 19660800 | bytes 3145728 | tf_op jit(solution)/shard_map/convert_element_type | solution.py:461
  95.1 47.4 %shard_map.77 = (bf16[8,256,1024]{2,1,0:T(8,128)(2,1)}, bf16[8,256,1024]{2,1,0:T(8,128)(2,1)}, bf16[8,256,512]{2,1,0:T(8,128)(2,1)}, bf16[8,256,512]{2,1,0:T(8,128)(2,1)}) custom-call(bf16[256,1024]{1,0:T(8,128)(2,1)} %get-tuple-element.29.refs_0_, bf16[256,1024]{1,0:T(8,128)(2,1)} %get-tuple-element.28.refs_1_, bf16[1024,512]{1,0:T(8,128)(2,1)} %refs_2_.3, ...), custom_call_target="tpu_custom_call" | custom-call | tf_op jit(solution)/shard_map/pallas_call | solution.py:171
  142.5 34.5 %shard_map.78 = (f32[128,512]{1,0:T(8,128)}, f32[128,512]{1,0:T(8,128)}) custom-call(bf16[16,128,512]{2,1,0:T(8,128)(2,1)} %bitcast.21, bf16[16,128,512]{2,1,0:T(8,128)(2,1)} %bitcast.22), custom_call_target="tpu_custom_call" | custom-call | tf_op jit(solution)/shard_map/pallas_call | solution.py:381
  177.0 1.7 add_convert_fusion.1
  178.7 7.2 %all-to-all-start = ((bf16[8,16,512]{2,1,0:T(8,128)(2,1)}), bf16[8,16,512]{2,1,0:T(8,128)(2,1)S(1)}, u32[]{:S(2)}, u32[]{:S(2)}) async-start(bf16[8,16,512]{2,1,0:T(8,128)(2,1)} %bitcast.5), calls=%async_computation | async-start | bytes 262144 | tf_op jit(solution)/shard_map/all_to_all | solution.py:465
  185.8 0.0 copy-start.2
  185.8 0.0 copy-start.3
  185.8 6.7 %fusion.17 = f32[1024,512]{1,0:T(8,128)} fusion(bf16[2048,1024]{1,0:T(8,128)(2,1)} %bitcast.18, bf16[2048,512]{1,0:T(8,128)(2,1)} %bitcast.23), kind=kOutput, calls=%fused_computation.29 | convolution fusion | flops 2147483648 | bytes 8388608 | tf_op jit(solution)/shard_map/dot_general | solution.py:466
  192.5 0.0 copy-done.2
  192.5 0.0 copy-done.3
  192.5 0.0 copy-start
  192.5 0.0 copy-start.1
  192.5 3.7 %fusion.16 = f32[512,1024]{1,0:T(8,128)} fusion(bf16[2048,512]{1,0:T(8,128)(2,1)S(1)} %bitcast.27, bf16[2048,1024]{1,0:T(8,128)(2,1)S(1)} %bitcast.26), kind=kOutput, calls=%fused_computation.28 | convolution fusion | flops 2147483648 | bytes 8388608 | tf_op jit(solution)/shard_map/dot_general | solution.py:469
  196.2 0.0 copy-done
  196.2 0.0 copy-done.1
  196.2 0.7 add_convert_fusion
  196.9 0.0 all-to-all-done
  196.9 0.7 copy.10
Async XLA Ops:
  178.7 18.2 %all-to-all-start = ((bf16[8,16,512]{2,1,0:T(8,128)(2,1)}), bf16[8,16,512]{2,1,0:T(8,128)(2,1)S(1)}, u32[]{:S(2)}, u32[]{:S(2)}) async-start(bf16[8,16,512]{2,1,0:T(8,128)(2,1)} %bitcast.5), calls=%async_computation | async-start | bytes 262144 | tf_op jit(solution)/shard_map/all_to_all | solution.py:465
  185.8 6.7 %copy-start.2 = (bf16[8,256,1024]{2,1,0:T(8,128)(2,1)S(1)}, bf16[8,256,1024]{2,1,0:T(8,128)(2,1)}, u32[]{:S(2)}) copy-start(bf16[8,256,1024]{2,1,0:T(8,128)(2,1)} %get-tuple-element.25) | copy-start | bytes 12582916
  185.8 6.7 %copy-start.3 = (bf16[16,128,512]{2,1,0:T(8,128)(2,1)S(1)}, bf16[16,128,512]{2,1,0:T(8,128)(2,1)}, u32[]{:S(2)}) copy-start(bf16[16,128,512]{2,1,0:T(8,128)(2,1)} %get-tuple-element.24) | copy-start | bytes 6291460
  192.5 3.7 %copy-start = (bf16[128,512]{1,0:T(8,128)(2,1)S(1)}, bf16[128,512]{1,0:T(8,128)(2,1)}, u32[]{:S(2)}) copy-start(bf16[128,512]{1,0:T(8,128)(2,1)} %refs_1_.1) | copy-start | bytes 393220
  192.5 3.7 %copy-start.1 = (f32[128,512]{1,0:T(8,128)S(1)}, f32[128,512]{1,0:T(8,128)}, u32[]{:S(2)}) copy-start(f32[128,512]{1,0:T(8,128)} %get-tuple-element.23) | copy-start | bytes 786436

commit v14 on v13

--- a/solution.py
+++ b/solution.py
@@ -56,28 +56,41 @@
         own = parts[a][2 * order(j, -1) + k].astype(jnp.float32)
         return own + recv1[a, j].astype(jnp.float32)
 
-    ring = []
+    pieces = 4
+    span = outs[0].shape[0] // pieces
+    ring = {}
     for step in range(nx - 1):
         for a in range(narr):
-            value = chip_sum(a, step)
-            if step == 0:
-                sendbuf[a, step] = value.astype(sendbuf.dtype)
-            else:
-                ring[(step - 1) * narr + a].wait_recv()
-                sendbuf[a, step] = (recv2[a, step - 1].astype(jnp.float32) + value).astype(sendbuf.dtype)
-            cp = pltpu.make_async_remote_copy(
-                src_ref=sendbuf.at[a, step], dst_ref=recv2.at[a, step],
-                send_sem=s2.at[a, step], recv_sem=r2.at[a, step],
-                device_id=nextdev, device_id_type=MESH)
-            cp.start()
-            ring.append(cp)
+            first[step * narr + a].wait_recv()
+        for q in range(pieces):
+            rows = pl.ds(q * span, span)
+            for a in range(narr):
+                value = (parts[a][2 * order(step, -1) + k, rows, :].astype(jnp.float32)
+                         + recv1[a, step, rows, :].astype(jnp.float32))
+                if step == 0:
+                    sendbuf[a, step, rows, :] = value.astype(sendbuf.dtype)
+                else:
+                    ring[(a, step - 1, q)].wait_recv()
+                    sendbuf[a, step, rows, :] = (recv2[a, step - 1, rows, :].astype(jnp.float32)
+                                                 + value).astype(sendbuf.dtype)
+                cp = pltpu.make_async_remote_copy(
+                    src_ref=sendbuf.at[a, step, rows], dst_ref=recv2.at[a, step, rows],
+                    send_sem=s2.at[a, step, q], recv_sem=r2.at[a, step, q],
+                    device_id=nextdev, device_id_type=MESH)
+                cp.start()
+                ring[(a, step, q)] = cp
     for a in range(narr):
-        value = chip_sum(a, nx - 1)
-        ring[(nx - 2) * narr + a].wait_recv()
-        outs[a][...] = recv2[a, nx - 2].astype(jnp.float32) + value
+        first[(nx - 1) * narr + a].wait_recv()
+    for q in range(pieces):
+        rows = pl.ds(q * span, span)
+        for a in range(narr):
+            value = (parts[a][2 * x + k, rows, :].astype(jnp.float32)
+                     + recv1[a, nx - 1, rows, :].astype(jnp.float32))
+            ring[(a, nx - 2, q)].wait_recv()
+            outs[a][rows, :] = recv2[a, nx - 2, rows, :].astype(jnp.float32) + value
     for cp in first:
         cp.wait_send()
-    for cp in ring:
+    for cp in ring.values():
         cp.wait_send()
 
 
@@ -99,8 +112,8 @@
             pltpu.VMEM((narr, nx - 1, rows, cols), jnp.bfloat16),
             pltpu.SemaphoreType.DMA((narr, nx)),
             pltpu.SemaphoreType.DMA((narr, nx)),
-            pltpu.SemaphoreType.DMA((narr, nx - 1)),
-            pltpu.SemaphoreType.DMA((narr, nx - 1)),
+            pltpu.SemaphoreType.DMA((narr, nx - 1, 4)),
+            pltpu.SemaphoreType.DMA((narr, nx - 1, 4)),
         ],
         compiler_params=pltpu.CompilerParams(collective_id=cid, has_side_effects=True,
                                              vmem_limit_bytes=64 * 1024 * 1024),

time: 198 us -> 199 us (level)
  no operation moved by 1% of the time
where the time goes in v14:
time: 199 us
  Pallas kernels  170 us (85%)
  matrix products  10.3 us (5%)
  starting transfers between devices  7.18 us (4%)
  other arithmetic  7.02 us (4%)
  local copies, waits for them, and re-layouts  2.96 us (1%)
    pallas_call x1, Pallas kernels, col_reduce_scatter(): pl.pallas_call(functools.partial(_rs_kernel, nx, narr), out_shape=[jax.Sh...  50 us
    pallas_call x1, Pallas kernels, col_all_gather(): pl.pallas_call(functools.partial(_ag_kernel, nx, narr), out_shape=[jax.Sh...  47.4 us
    pallas_call x1, Pallas kernels, row_all_gather(): pl.pallas_call(functools.partial(_row_ag_kernel, ny), out_shape=[jax.Shap...  38.4 us
    pallas_call x1, Pallas kernels, row_reduce_scatter(): pl.pallas_call(functools.partial(_row_rs_kernel, ny), out_shape=[jax.Shap...  34.5 us
    all_to_all x1, starting transfers between devices, local(): lax.all_to_all(block_rows, 'col', split_axis=0, concat_axis=1, tiled=True)  7.18 us
    dot_general x1, matrix products, local(): lax.dot_general(act_all, upstream_all, (((0,), (0,)), ((), ())), preferre...  6.68 us
    convert_element_type x1, other arithmetic, local(): dpre = (dact_part * gelu_grad(pre_part)).astype(jnp.bfloat16)  4.67 us
  transfers between devices with their start and end apart: 1, of which 0 were waited for; matrix products, arithmetic and copies ran while one was open for 6% of the time, Pallas kernels for 0%

profile of v14, /device:TPU:1, one launch (start us, length us, event | category | flops | bytes accessed | tf_op | source)
XLA Modules:
  0.0 198.5 jit_solution(2284384483911635500)
XLA Ops:
  0.6 2.3 %copy.8 = bf16[512,1024]{0,1:T(8,128)(2,1)} copy(bf16[512,1024]{1,0:T(8,128)(2,1)} %refs_2_.2) | data formatting | bytes 2097152 | tf_op args[1]
  2.9 38.4 %shard_map.75 = (bf16[16,128,512]{2,1,0:T(8,128)(2,1)}, bf16[16,128,512]{2,1,0:T(8,128)(2,1)}, bf16[16,128,1024]{2,1,0:T(8,128)(2,1)}, bf16[16,128,1024]{2,1,0:T(8,128)(2,1)}) custom-call(bf16[128,512]{1,0:T(8,128)(2,1)} %refs_0_.1, bf16[128,512]{1,0:T(8,128)(2,1)} %refs_1_.1, bf16[512,1024]{1,0:T(8,128)(2,1)} %refs_2_.2, bf16[1024,512]{1,0:T(8,128)(2,1)} %refs_2_.3), custom_call_target="tpu_custom_call" | custom-call | tf_op jit(solution)/shard_map/pallas_call | solution.py:304
  41.3 50.0 %shard_map.76 = (f32[256,1024]{1,0:T(8,128)}, f32[256,1024]{1,0:T(8,128)}) custom-call(bf16[8,256,1024]{2,1,0:T(8,128)(2,1)} %bitcast.19, bf16[8,256,1024]{2,1,0:T(8,128)(2,1)} %bitcast.20), custom_call_target="tpu_custom_call" | custom-call | tf_op jit(solution)/shard_map/pallas_call | solution.py:104
  91.3 4.7 %fusion.8 = (bf16[256,1024]{1,0:T(8,128)(2,1)}, bf16[256,1024]{1,0:T(8,128)(2,1)}) fusion(f32[256,1024]{1,0:T(8,128)} %get-tuple-element.19, f32[256,1024]{1,0:T(8,128)} %get-tuple-element.18), kind=kLoop, calls=%fused_computation.10 | loop fusion | flops 19660800 | bytes 3145728 | tf_op jit(solution)/shard_map/convert_element_type | solution.py:474
  96.0 47.4 %shard_map.77 = (bf16[8,256,1024]{2,1,0:T(8,128)(2,1)}, bf16[8,256,1024]{2,1,0:T(8,128)(2,1)}, bf16[8,256,512]{2,1,0:T(8,128)(2,1)}, bf16[8,256,512]{2,1,0:T(8,128)(2,1)}) custom-call(bf16[256,1024]{1,0:T(8,128)(2,1)} %get-tuple-element.29.refs_0_, bf16[256,1024]{1,0:T(8,128)(2,1)} %get-tuple-element.28.refs_1_, bf16[1024,512]{1,0:T(8,128)(2,1)} %refs_2_.3, ...), custom_call_target="tpu_custom_call" | custom-call | tf_op jit(solution)/shard_map/pallas_call | solution.py:184
  143.4 34.5 %shard_map.78 = (f32[128,512]{1,0:T(8,128)}, f32[128,512]{1,0:T(8,128)}) custom-call(bf16[16,128,512]{2,1,0:T(8,128)(2,1)} %bitcast.21, bf16[16,128,512]{2,1,0:T(8,128)(2,1)} %bitcast.22), custom_call_target="tpu_custom_call" | custom-call | tf_op jit(solution)/shard_map/pallas_call | solution.py:394
  177.9 1.7 add_convert_fusion.1
  179.6 7.2 %all-to-all-start = ((bf16[8,16,512]{2,1,0:T(8,128)(2,1)}), bf16[8,16,512]{2,1,0:T(8,128)(2,1)S(1)}, u32[]{:S(2)}, u32[]{:S(2)}) async-start(bf16[8,16,512]{2,1,0:T(8,128)(2,1)} %bitcast.5), calls=%async_computation | async-start | bytes 262144 | tf_op jit(solution)/shard_map/all_to_all | solution.py:478
  186.8 0.0 copy-start.2
  186.8 0.0 copy-start.3
  186.8 6.7 %fusion.17 = f32[1024,512]{1,0:T(8,128)} fusion(bf16[2048,1024]{1,0:T(8,128)(2,1)} %bitcast.18, bf16[2048,512]{1,0:T(8,128)(2,1)} %bitcast.23), kind=kOutput, calls=%fused_computation.29 | convolution fusion | flops 2147483648 | bytes 8388608 | tf_op jit(solution)/shard_map/dot_general | solution.py:479
  193.5 0.0 copy-done.2
  193.5 0.0 copy-done.3
  193.5 0.0 copy-start
  193.5 0.0 copy-start.1
  193.5 3.7 %fusion.16 = f32[512,1024]{1,0:T(8,128)} fusion(bf16[2048,512]{1,0:T(8,128)(2,1)S(1)} %bitcast.27, bf16[2048,1024]{1,0:T(8,128)(2,1)S(1)} %bitcast.26), kind=kOutput, calls=%fused_computation.28 | convolution fusion | flops 2147483648 | bytes 8388608 | tf_op jit(solution)/shard_map/dot_general | solution.py:482
  197.2 0.0 copy-done
  197.2 0.0 copy-done.1
  197.2 0.7 add_convert_fusion
  197.9 0.0 all-to-all-done
  197.9 0.7 copy.10
Async XLA Ops:
  179.6 18.2 %all-to-all-start = ((bf16[8,16,512]{2,1,0:T(8,128)(2,1)}), bf16[8,16,512]{2,1,0:T(8,128)(2,1)S(1)}, u32[]{:S(2)}, u32[]{:S(2)}) async-start(bf16[8,16,512]{2,1,0:T(8,128)(2,1)} %bitcast.5), calls=%async_computation | async-start | bytes 262144 | tf_op jit(solution)/shard_map/all_to_all | solution.py:478
  186.8 6.7 %copy-start.2 = (bf16[8,256,1024]{2,1,0:T(8,128)(2,1)S(1)}, bf16[8,256,1024]{2,1,0:T(8,128)(2,1)}, u32[]{:S(2)}) copy-start(bf16[8,256,1024]{2,1,0:T(8,128)(2,1)} %get-tuple-element.25) | copy-start | bytes 12582916
  186.8 6.7 %copy-start.3 = (bf16[16,128,512]{2,1,0:T(8,128)(2,1)S(1)}, bf16[16,128,512]{2,1,0:T(8,128)(2,1)}, u32[]{:S(2)}) copy-start(bf16[16,128,512]{2,1,0:T(8,128)(2,1)} %get-tuple-element.24) | copy-start | bytes 6291460
  193.5 3.7 %copy-start = (bf16[128,512]{1,0:T(8,128)(2,1)S(1)}, bf16[128,512]{1,0:T(8,128)(2,1)}, u32[]{:S(2)}) copy-start(bf16[128,512]{1,0:T(8,128)(2,1)} %refs_1_.1) | copy-start | bytes 393220
  193.5 3.7 %copy-start.1 = (f32[128,512]{1,0:T(8,128)S(1)}, f32[128,512]{1,0:T(8,128)}, u32[]{:S(2)}) copy-start(f32[128,512]{1,0:T(8,128)} %get-tuple-element.23) | copy-start | bytes 786436

commit v15 on v14

--- a/solution.py
+++ b/solution.py
@@ -83,11 +83,16 @@
         first[(nx - 1) * narr + a].wait_recv()
     for q in range(pieces):
         rows = pl.ds(q * span, span)
+        sums = []
         for a in range(narr):
             value = (parts[a][2 * x + k, rows, :].astype(jnp.float32)
                      + recv1[a, nx - 1, rows, :].astype(jnp.float32))
             ring[(a, nx - 2, q)].wait_recv()
-            outs[a][rows, :] = recv2[a, nx - 2, rows, :].astype(jnp.float32) + value
+            sums.append(recv2[a, nx - 2, rows, :].astype(jnp.float32) + value)
+        pre, dact = sums
+        cdf = 0.5 * (1.0 + jax.scipy.special.erf(pre * 0.7071067811865476))
+        outs[0][rows, :] = (pre * cdf).astype(outs[0].dtype)
+        outs[1][rows, :] = (dact * gelu_grad(pre)).astype(outs[1].dtype)
     for cp in first:
         cp.wait_send()
     for cp in ring.values():
@@ -103,7 +108,7 @@
     parts = [a.reshape(n, rows, cols) for a in arrays]
     return pl.pallas_call(
         functools.partial(_rs_kernel, nx, narr),
-        out_shape=[jax.ShapeDtypeStruct((rows, cols), jnp.float32)] * narr,
+        out_shape=[jax.ShapeDtypeStruct((rows, cols), jnp.bfloat16)] * narr,
         in_specs=[pl.BlockSpec(memory_space=pltpu.VMEM)] * narr,
         out_specs=[pl.BlockSpec(memory_space=pltpu.VMEM)] * narr,
         scratch_shapes=[
@@ -469,9 +474,7 @@
 
 def local(tokens, w_in, w_out, cotangent):
     tokens_all, upstream_all, pre_term, dact_term = row_all_gather(tokens, cotangent, w_in, w_out, 3)
-    pre_part, dact_part = col_reduce_scatter([pre_term, dact_term], 1)
-    act = jax.nn.gelu(pre_part, approximate=False).astype(jnp.bfloat16)
-    dpre = (dact_part * gelu_grad(pre_part)).astype(jnp.bfloat16)
+    act, dpre = col_reduce_scatter([pre_term, dact_term], 1)
     (act_all, dpre_all), (mixed_term, back_term) = col_all_gather([act, dpre], [w_out, w_in.T], 2)
     mixed, back = row_reduce_scatter(mixed_term, back_term, 4)
     block_rows = (tokens.astype(jnp.float32) + mixed).astype(jnp.bfloat16)

time: 199 us -> 194 us (0.975)
  other arithmetic: 7.02 us -> 2.35 us
    convert_element_type x1 -> x0, other arithmetic: 4.67 us -> none  [local(): dpre = (dact_part * gelu_grad(pre_part)).astype(jnp.bfloat16)]
where the time goes in v15:
time: 194 us
  Pallas kernels  170 us (88%)
  matrix products  10.3 us (5%)
  starting transfers between devices  7.18 us (4%)
  local copies, waits for them, and re-layouts  2.96 us (2%)
  other arithmetic  2.35 us (1%)
    pallas_call x1, Pallas kernels, col_reduce_scatter(): pl.pallas_call(functools.partial(_rs_kernel, nx, narr), out_shape=[jax.Sh...  49.8 us
    pallas_call x1, Pallas kernels, col_all_gather(): pl.pallas_call(functools.partial(_ag_kernel, nx, narr), out_shape=[jax.Sh...  47.5 us
    pallas_call x1, Pallas kernels, row_all_gather(): pl.pallas_call(functools.partial(_row_ag_kernel, ny), out_shape=[jax.Shap...  38.4 us
    pallas_call x1, Pallas kernels, row_reduce_scatter(): pl.pallas_call(functools.partial(_row_rs_kernel, ny), out_shape=[jax.Shap...  34.5 us
    all_to_all x1, starting transfers between devices, local(): lax.all_to_all(block_rows, 'col', split_axis=0, concat_axis=1, tiled=True)  7.18 us
    dot_general x1, matrix products, local(): lax.dot_general(act_all, upstream_all, (((0,), (0,)), ((), ())), preferre...  6.68 us
  transfers between devices with their start and end apart: 1, of which 0 were waited for; matrix products, arithmetic and copies ran while one was open for 6% of the time, Pallas kernels for 0%

profile of v15, /device:TPU:1, one launch (start us, length us, event | category | flops | bytes accessed | tf_op | source)
XLA Modules:
  0.0 193.7 jit_solution(4355425010479512901)
XLA Ops:
  0.6 2.3 %copy.8 = bf16[512,1024]{0,1:T(8,128)(2,1)} copy(bf16[512,1024]{1,0:T(8,128)(2,1)} %refs_2_.2) | data formatting | bytes 2097152 | tf_op args[1]
  2.9 38.4 %shard_map.75 = (bf16[16,128,512]{2,1,0:T(8,128)(2,1)}, bf16[16,128,512]{2,1,0:T(8,128)(2,1)}, bf16[16,128,1024]{2,1,0:T(8,128)(2,1)}, bf16[16,128,1024]{2,1,0:T(8,128)(2,1)}) custom-call(bf16[128,512]{1,0:T(8,128)(2,1)} %refs_0_.1, bf16[128,512]{1,0:T(8,128)(2,1)} %refs_1_.1, bf16[512,1024]{1,0:T(8,128)(2,1)} %refs_2_.2, bf16[1024,512]{1,0:T(8,128)(2,1)} %refs_2_.3), custom_call_target="tpu_custom_call" | custom-call | tf_op jit(solution)/shard_map/pallas_call | solution.py:309
  41.3 49.8 %shard_map.76 = (bf16[256,1024]{1,0:T(8,128)(2,1)}, bf16[256,1024]{1,0:T(8,128)(2,1)}) custom-call(bf16[8,256,1024]{2,1,0:T(8,128)(2,1)} %bitcast.19, bf16[8,256,1024]{2,1,0:T(8,128)(2,1)} %bitcast.20), custom_call_target="tpu_custom_call" | custom-call | tf_op jit(solution)/shard_map/pallas_call | solution.py:109
  91.1 47.5 %shard_map.77 = (bf16[8,256,1024]{2,1,0:T(8,128)(2,1)}, bf16[8,256,1024]{2,1,0:T(8,128)(2,1)}, bf16[8,256,512]{2,1,0:T(8,128)(2,1)}, bf16[8,256,512]{2,1,0:T(8,128)(2,1)}) custom-call(bf16[256,1024]{1,0:T(8,128)(2,1)} %get-tuple-element.18.refs_0_, bf16[256,1024]{1,0:T(8,128)(2,1)} %get-tuple-element.19.refs_1_, bf16[1024,512]{1,0:T(8,128)(2,1)} %refs_2_.3, ...), custom_call_target="tpu_custom_call" | custom-call | tf_op jit(solution)/shard_map/pallas_call | solution.py:189
  138.6 34.5 %shard_map.78 = (f32[128,512]{1,0:T(8,128)}, f32[128,512]{1,0:T(8,128)}) custom-call(bf16[16,128,512]{2,1,0:T(8,128)(2,1)} %bitcast.21, bf16[16,128,512]{2,1,0:T(8,128)(2,1)} %bitcast.22), custom_call_target="tpu_custom_call" | custom-call | tf_op jit(solution)/shard_map/pallas_call | solution.py:399
  173.1 1.7 add_convert_fusion.1
  174.8 7.2 %all-to-all-start = ((bf16[8,16,512]{2,1,0:T(8,128)(2,1)}), bf16[8,16,512]{2,1,0:T(8,128)(2,1)S(1)}, u32[]{:S(2)}, u32[]{:S(2)}) async-start(bf16[8,16,512]{2,1,0:T(8,128)(2,1)} %bitcast.5), calls=%async_computation | async-start | bytes 262144 | tf_op jit(solution)/shard_map/all_to_all | solution.py:481
  182.0 0.0 copy-start.2
  182.0 0.0 copy-start.3
  182.0 6.7 %fusion.1 = f32[1024,512]{1,0:T(8,128)} fusion(bf16[2048,1024]{1,0:T(8,128)(2,1)} %bitcast.18, bf16[2048,512]{1,0:T(8,128)(2,1)} %bitcast.23), kind=kOutput, calls=%fused_computation.3 | convolution fusion | flops 2147483648 | bytes 8388608 | tf_op jit(solution)/shard_map/dot_general | solution.py:482
  188.7 0.0 copy-done.2
  188.7 0.0 copy-done.3
  188.7 0.0 copy-start
  188.7 0.0 copy-start.1
  188.7 3.7 %fusion = f32[512,1024]{1,0:T(8,128)} fusion(bf16[2048,512]{1,0:T(8,128)(2,1)S(1)} %bitcast.27, bf16[2048,1024]{1,0:T(8,128)(2,1)S(1)} %bitcast.26), kind=kOutput, calls=%fused_computation.2 | convolution fusion | flops 2147483648 | bytes 8388608 | tf_op jit(solution)/shard_map/dot_general | solution.py:485
  192.3 0.0 copy-done
  192.3 0.0 copy-done.1
  192.4 0.7 add_convert_fusion
  193.0 0.0 all-to-all-done
  193.0 0.7 copy.10
Async XLA Ops:
  174.8 18.2 %all-to-all-start = ((bf16[8,16,512]{2,1,0:T(8,128)(2,1)}), bf16[8,16,512]{2,1,0:T(8,128)(2,1)S(1)}, u32[]{:S(2)}, u32[]{:S(2)}) async-start(bf16[8,16,512]{2,1,0:T(8,128)(2,1)} %bitcast.5), calls=%async_computation | async-start | bytes 262144 | tf_op jit(solution)/shard_map/all_to_all | solution.py:481
  182.0 6.7 %copy-start.2 = (bf16[8,256,1024]{2,1,0:T(8,128)(2,1)S(1)}, bf16[8,256,1024]{2,1,0:T(8,128)(2,1)}, u32[]{:S(2)}) copy-start(bf16[8,256,1024]{2,1,0:T(8,128)(2,1)} %get-tuple-element.25) | copy-start | bytes 12582916
  182.0 6.7 %copy-start.3 = (bf16[16,128,512]{2,1,0:T(8,128)(2,1)S(1)}, bf16[16,128,512]{2,1,0:T(8,128)(2,1)}, u32[]{:S(2)}) copy-start(bf16[16,128,512]{2,1,0:T(8,128)(2,1)} %get-tuple-element.24) | copy-start | bytes 6291460
  188.7 3.7 %copy-start = (bf16[128,512]{1,0:T(8,128)(2,1)S(1)}, bf16[128,512]{1,0:T(8,128)(2,1)}, u32[]{:S(2)}) copy-start(bf16[128,512]{1,0:T(8,128)(2,1)} %refs_1_.1) | copy-start | bytes 393220
  188.7 3.7 %copy-start.1 = (f32[128,512]{1,0:T(8,128)S(1)}, f32[128,512]{1,0:T(8,128)}, u32[]{:S(2)}) copy-start(f32[128,512]{1,0:T(8,128)} %get-tuple-element.23) | copy-start | bytes 786436

commit v16 on v15

--- a/solution.py
+++ b/solution.py
@@ -139,8 +139,12 @@
     nextdev = (row, 2 * nxt + k)
 
     def product(a, slot):
-        prods[a][slot] = jnp.dot(outs[a][slot], weights[a][...],
-                                 preferred_element_type=jnp.float32).astype(prods[a].dtype)
+        if a == 0:
+            value = jnp.dot(outs[a][slot], weights[a][...], preferred_element_type=jnp.float32)
+        else:
+            value = lax.dot_general(outs[a][slot], weights[a][...], (((1,), (1,)), ((), ())),
+                                    preferred_element_type=jnp.float32)
+        prods[a][slot] = value.astype(prods[a].dtype)
 
     for a in range(narr):
         outs[a][me] = chunks[a][...]
@@ -475,7 +479,7 @@
 def local(tokens, w_in, w_out, cotangent):
     tokens_all, upstream_all, pre_term, dact_term = row_all_gather(tokens, cotangent, w_in, w_out, 3)
     act, dpre = col_reduce_scatter([pre_term, dact_term], 1)
-    (act_all, dpre_all), (mixed_term, back_term) = col_all_gather([act, dpre], [w_out, w_in.T], 2)
+    (act_all, dpre_all), (mixed_term, back_term) = col_all_gather([act, dpre], [w_out, w_in], 2)
     mixed, back = row_reduce_scatter(mixed_term, back_term, 4)
     block_rows = (tokens.astype(jnp.float32) + mixed).astype(jnp.bfloat16)
     block_out = lax.all_to_all(block_rows, "col", split_axis=0, concat_axis=1, tiled=True)

time: 194 us -> 192 us (0.990)
  local copies, waits for them, and re-layouts: 2.96 us -> 0.68 us
    unnamed x9 -> x8, local copies, waits for them, and re-layouts: 2.29 us -> 0.02 us
where the time goes in v16:
time: 192 us
  Pallas kernels  170 us (89%)
  matrix products  10.3 us (5%)
  starting transfers between devices  7.19 us (4%)
  other arithmetic  2.35 us (1%)
    pallas_call x1, Pallas kernels, col_reduce_scatter(): pl.pallas_call(functools.partial(_rs_kernel, nx, narr), out_shape=[jax.Sh...  49.8 us
    pallas_call x1, Pallas kernels, col_all_gather(): pl.pallas_call(functools.partial(_ag_kernel, nx, narr), out_shape=[jax.Sh...  47.5 us
    pallas_call x1, Pallas kernels, row_all_gather(): pl.pallas_call(functools.partial(_row_ag_kernel, ny), out_shape=[jax.Shap...  38.5 us
    pallas_call x1, Pallas kernels, row_reduce_scatter(): pl.pallas_call(functools.partial(_row_rs_kernel, ny), out_shape=[jax.Shap...  34.5 us
    all_to_all x1, starting transfers between devices, local(): lax.all_to_all(block_rows, 'col', split_axis=0, concat_axis=1, tiled=True)  7.19 us
    dot_general x1, matrix products, local(): lax.dot_general(act_all, upstream_all, (((0,), (0,)), ((), ())), preferre...  6.68 us
  transfers between devices with their start and end apart: 1, of which 0 were waited for; matrix products, arithmetic and copies ran while one was open for 6% of the time, Pallas kernels for 0%

profile of v16, /device:TPU:1, one launch (start us, length us, event | category | flops | bytes accessed | tf_op | source)
XLA Modules:
  0.0 191.5 jit_solution(840114149046029968)
XLA Ops:
  0.6 38.5 %shard_map.75 = (bf16[16,128,512]{2,1,0:T(8,128)(2,1)}, bf16[16,128,512]{2,1,0:T(8,128)(2,1)}, bf16[16,128,1024]{2,1,0:T(8,128)(2,1)}, bf16[16,128,1024]{2,1,0:T(8,128)(2,1)}) custom-call(bf16[128,512]{1,0:T(8,128)(2,1)} %refs_0_.1, bf16[128,512]{1,0:T(8,128)(2,1)} %refs_1_.1, bf16[512,1024]{1,0:T(8,128)(2,1)} %refs_3_.3, bf16[1024,512]{1,0:T(8,128)(2,1)} %refs_2_.3), custom_call_target="tpu_custom_call" | custom-call | tf_op jit(solution)/shard_map/pallas_call | solution.py:313
  39.1 49.8 %shard_map.76 = (bf16[256,1024]{1,0:T(8,128)(2,1)}, bf16[256,1024]{1,0:T(8,128)(2,1)}) custom-call(bf16[8,256,1024]{2,1,0:T(8,128)(2,1)} %bitcast.17, bf16[8,256,1024]{2,1,0:T(8,128)(2,1)} %bitcast.18), custom_call_target="tpu_custom_call" | custom-call | tf_op jit(solution)/shard_map/pallas_call | solution.py:109
  88.9 47.5 %shard_map.77 = (bf16[8,256,1024]{2,1,0:T(8,128)(2,1)}, bf16[8,256,1024]{2,1,0:T(8,128)(2,1)}, bf16[8,256,512]{2,1,0:T(8,128)(2,1)}, bf16[8,256,512]{2,1,0:T(8,128)(2,1)}) custom-call(bf16[256,1024]{1,0:T(8,128)(2,1)} %get-tuple-element.18.refs_0_, bf16[256,1024]{1,0:T(8,128)(2,1)} %get-tuple-element.19.refs_1_, bf16[1024,512]{1,0:T(8,128)(2,1)} %refs_2_.3, ...), custom_call_target="tpu_custom_call" | custom-call | tf_op jit(solution)/shard_map/pallas_call | solution.py:193
  136.4 34.5 %shard_map.78 = (f32[128,512]{1,0:T(8,128)}, f32[128,512]{1,0:T(8,128)}) custom-call(bf16[16,128,512]{2,1,0:T(8,128)(2,1)} %bitcast.19, bf16[16,128,512]{2,1,0:T(8,128)(2,1)} %bitcast.20), custom_call_target="tpu_custom_call" | custom-call | tf_op jit(solution)/shard_map/pallas_call | solution.py:403
  170.9 1.7 add_convert_fusion.1
  172.6 7.2 %all-to-all-start = ((bf16[8,16,512]{2,1,0:T(8,128)(2,1)}), bf16[8,16,512]{2,1,0:T(8,128)(2,1)S(1)}, u32[]{:S(2)}, u32[]{:S(2)}) async-start(bf16[8,16,512]{2,1,0:T(8,128)(2,1)} %bitcast.4), calls=%async_computation | async-start | bytes 262144 | tf_op jit(solution)/shard_map/all_to_all | solution.py:485
  179.8 0.0 copy-start.2
  179.8 0.0 copy-start.3
  179.8 6.7 %fusion.1 = f32[1024,512]{1,0:T(8,128)} fusion(bf16[2048,1024]{1,0:T(8,128)(2,1)} %bitcast.16, bf16[2048,512]{1,0:T(8,128)(2,1)} %bitcast.21), kind=kOutput, calls=%fused_computation.3 | convolution fusion | flops 2147483648 | bytes 8388608 | tf_op jit(solution)/shard_map/dot_general | solution.py:486
  186.5 0.0 copy-done.2
  186.5 0.0 copy-done.3
  186.5 0.0 copy-start
  186.5 0.0 copy-start.1
  186.5 3.7 %fusion = f32[512,1024]{1,0:T(8,128)} fusion(bf16[2048,512]{1,0:T(8,128)(2,1)S(1)} %bitcast.25, bf16[2048,1024]{1,0:T(8,128)(2,1)S(1)} %bitcast.24), kind=kOutput, calls=%fused_computation.2 | convolution fusion | flops 2147483648 | bytes 8388608 | tf_op jit(solution)/shard_map/dot_general | solution.py:489
  190.1 0.0 copy-done
  190.2 0.0 copy-done.1
  190.2 0.7 add_convert_fusion
  190.8 0.0 all-to-all-done
  190.8 0.7 copy.9
Async XLA Ops:
  172.6 18.3 %all-to-all-start = ((bf16[8,16,512]{2,1,0:T(8,128)(2,1)}), bf16[8,16,512]{2,1,0:T(8,128)(2,1)S(1)}, u32[]{:S(2)}, u32[]{:S(2)}) async-start(bf16[8,16,512]{2,1,0:T(8,128)(2,1)} %bitcast.4), calls=%async_computation | async-start | bytes 262144 | tf_op jit(solution)/shard_map/all_to_all | solution.py:485
  179.8 6.7 %copy-start.2 = (bf16[8,256,1024]{2,1,0:T(8,128)(2,1)S(1)}, bf16[8,256,1024]{2,1,0:T(8,128)(2,1)}, u32[]{:S(2)}) copy-start(bf16[8,256,1024]{2,1,0:T(8,128)(2,1)} %get-tuple-element.25) | copy-start | bytes 12582916
  179.8 6.7 %copy-start.3 = (bf16[16,128,512]{2,1,0:T(8,128)(2,1)S(1)}, bf16[16,128,512]{2,1,0:T(8,128)(2,1)}, u32[]{:S(2)}) copy-start(bf16[16,128,512]{2,1,0:T(8,128)(2,1)} %get-tuple-element.24) | copy-start | bytes 6291460
  186.5 3.7 %copy-start = (bf16[128,512]{1,0:T(8,128)(2,1)S(1)}, bf16[128,512]{1,0:T(8,128)(2,1)}, u32[]{:S(2)}) copy-start(bf16[128,512]{1,0:T(8,128)(2,1)} %refs_1_.1) | copy-start | bytes 393220
  186.5 3.7 %copy-start.1 = (f32[128,512]{1,0:T(8,128)S(1)}, f32[128,512]{1,0:T(8,128)}, u32[]{:S(2)}) copy-start(f32[128,512]{1,0:T(8,128)} %get-tuple-element.23) | copy-start | bytes 786436

commit v17 on v16

--- a/solution.py
+++ b/solution.py
@@ -26,13 +26,9 @@
     pl.semaphore_wait(barrier, 3)
 
 
-def _rs_kernel(nx, narr, *refs):
-    parts = refs[:narr]
-    outs = refs[narr:2 * narr]
-    recv1, sendbuf, recv2, s1, r1, s2, r2 = refs[2 * narr:]
+def _rs_body(nx, narr, parts, outs, recv1, sendbuf, recv2, s1, r1, s2, r2):
     row = lax.axis_index("row")
     x, k, d, nxt, prv = _col_ids(nx)
-    _greet(row, k, x, nxt, prv)
     partner = (row, 2 * x + 1 - k)
     nextdev = (row, 2 * nxt + k)
 
@@ -99,18 +95,34 @@
         cp.wait_send()
 
 
-def col_reduce_scatter(arrays, cid):
+def _col_kernel(nx, narr, *refs):
+    parts = refs[:narr]
+    weights = refs[narr:2 * narr]
+    outs = refs[2 * narr:3 * narr]
+    prods = refs[3 * narr:4 * narr]
+    scratch = refs[4 * narr:]
+    row = lax.axis_index("row")
+    x, k, d, nxt, prv = _col_ids(nx)
+    _greet(row, k, x, nxt, prv)
+    own = [o.at[2 * x + k] for o in outs]
+    _rs_body(nx, narr, parts, own, *scratch[:7])
+    _ag_body(nx, narr, own, weights, outs, prods, *scratch[7:])
+
+
+def col_exchange(arrays, weights, cid):
     n = lax.axis_size("col")
     nx = n // 2
     narr = len(arrays)
     rows = arrays[0].shape[0] // n
     cols = arrays[0].shape[1]
+    width = weights[0].shape[1]
     parts = [a.reshape(n, rows, cols) for a in arrays]
-    return pl.pallas_call(
-        functools.partial(_rs_kernel, nx, narr),
-        out_shape=[jax.ShapeDtypeStruct((rows, cols), jnp.bfloat16)] * narr,
-        in_specs=[pl.BlockSpec(memory_space=pltpu.VMEM)] * narr,
-        out_specs=[pl.BlockSpec(memory_space=pltpu.VMEM)] * narr,
+    res = pl.pallas_call(
+        functools.partial(_col_kernel, nx, narr),
+        out_shape=[jax.ShapeDtypeStruct((n, rows, cols), jnp.bfloat16)] * narr
+        + [jax.ShapeDtypeStruct((n, rows, width), jnp.bfloat16)] * narr,
+        in_specs=[pl.BlockSpec(memory_space=pltpu.VMEM)] * (2 * narr),
+        out_specs=[pl.BlockSpec(memory_space=pltpu.VMEM)] * (2 * narr),
         scratch_shapes=[
             pltpu.VMEM((narr, nx, rows, cols), jnp.bfloat16),
             pltpu.VMEM((narr, nx - 1, rows, cols), jnp.bfloat16),
@@ -119,21 +131,22 @@
             pltpu.SemaphoreType.DMA((narr, nx)),
             pltpu.SemaphoreType.DMA((narr, nx - 1, 4)),
             pltpu.SemaphoreType.DMA((narr, nx - 1, 4)),
+            pltpu.SemaphoreType.DMA((narr, nx)),
+            pltpu.SemaphoreType.DMA((narr, nx)),
+            pltpu.SemaphoreType.DMA((narr, nx)),
+            pltpu.SemaphoreType.DMA((narr, nx)),
         ],
         compiler_params=pltpu.CompilerParams(collective_id=cid, has_side_effects=True,
                                              vmem_limit_bytes=64 * 1024 * 1024),
-    )(*parts)
-
-
-def _ag_kernel(nx, narr, *refs):
-    chunks = refs[:narr]
-    weights = refs[narr:2 * narr]
-    outs = refs[2 * narr:3 * narr]
-    prods = refs[3 * narr:4 * narr]
-    sr, rr, sc, rc = refs[4 * narr:]
+    )(*parts, *weights)
+    gathered = [o.reshape(n * rows, cols) for o in res[:narr]]
+    products = [o.reshape(n * rows, width) for o in res[narr:]]
+    return gathered, products
+
+
+def _ag_body(nx, narr, chunks, weights, outs, prods, sr, rr, sc, rc):
     row = lax.axis_index("row")
     x, k, d, nxt, prv = _col_ids(nx)
-    _greet(row, k, x, nxt, prv)
     me = 2 * x + k
     partner = (row, 2 * x + 1 - k)
     nextdev = (row, 2 * nxt + k)
@@ -146,8 +159,6 @@
                                     preferred_element_type=jnp.float32)
         prods[a][slot] = value.astype(prods[a].dtype)
 
-    for a in range(narr):
-        outs[a][me] = chunks[a][...]
     ring, core = [], []
     for step in range(nx):
         for a in range(narr):
@@ -182,32 +193,6 @@
         core[(nx - 1) * narr + a].wait()
     for a in range(narr):
         product(a, 2 * lax.rem(x + 4 * nx + d * (nx - 1), nx) + 1 - k)
-
-
-def col_all_gather(arrays, weights, cid):
-    n = lax.axis_size("col")
-    nx = n // 2
-    narr = len(arrays)
-    rows, cols = arrays[0].shape
-    width = weights[0].shape[1]
-    res = pl.pallas_call(
-        functools.partial(_ag_kernel, nx, narr),
-        out_shape=[jax.ShapeDtypeStruct((n, rows, cols), arrays[0].dtype)] * narr
-        + [jax.ShapeDtypeStruct((n, rows, width), jnp.bfloat16)] * narr,
-        in_specs=[pl.BlockSpec(memory_space=pltpu.VMEM)] * (2 * narr),
-        out_specs=[pl.BlockSpec(memory_space=pltpu.VMEM)] * (2 * narr),
-        scratch_shapes=[
-            pltpu.SemaphoreType.DMA((narr, nx)),
-            pltpu.SemaphoreType.DMA((narr, nx)),
-            pltpu.SemaphoreType.DMA((narr, nx)),
-            pltpu.SemaphoreType.DMA((narr, nx)),
-        ],
-        compiler_params=pltpu.CompilerParams(collective_id=cid, has_side_effects=True,
-                                             vmem_limit_bytes=64 * 1024 * 1024),
-    )(*arrays, *weights)
-    gathered = [o.reshape(n * rows, cols) for o in res[:narr]]
-    products = [o.reshape(n * rows, width) for o in res[narr:]]
-    return gathered, products
 
 
 def _row_ids():
@@ -478,8 +463,7 @@
 
 def local(tokens, w_in, w_out, cotangent):
     tokens_all, upstream_all, pre_term, dact_term = row_all_gather(tokens, cotangent, w_in, w_out, 3)
-    act, dpre = col_reduce_scatter([pre_term, dact_term], 1)
-    (act_all, dpre_all), (mixed_term, back_term) = col_all_gather([act, dpre], [w_out, w_in], 2)
+    (act_all, dpre_all), (mixed_term, back_term) = col_exchange([pre_term, dact_term], [w_out, w_in], 1)
     mixed, back = row_reduce_scatter(mixed_term, back_term, 4)
     block_rows = (tokens.astype(jnp.float32) + mixed).astype(jnp.bfloat16)
     block_out = lax.all_to_all(block_rows, "col", split_axis=0, concat_axis=1, tiled=True)

time: 192 us -> 187 us (0.974)
  Pallas kernels: 170 us -> 165 us
    pallas_call x2 -> x1, Pallas kernels: 97.3 us -> 92.4 us  [col_exchange(): pl.pallas_call(functools.partial(_col_kernel, nx, narr), out_shape=[jax.S...]
where the time goes in v17:
time: 187 us
  Pallas kernels  165 us (88%)
  matrix products  10.4 us (6%)
  starting transfers between devices  7.25 us (4%)
  other arithmetic  2.35 us (1%)
    pallas_call x1, Pallas kernels, col_exchange(): pl.pallas_call(functools.partial(_col_kernel, nx, narr), out_shape=[jax.S...  92.4 us
    pallas_call x1, Pallas kernels, row_all_gather(): pl.pallas_call(functools.partial(_row_ag_kernel, ny), out_shape=[jax.Shap...  38.5 us
    pallas_call x1, Pallas kernels, row_reduce_scatter(): pl.pallas_call(functools.partial(_row_rs_kernel, ny), out_shape=[jax.Shap...  34.5 us
    all_to_all x1, starting transfers between devices, local(): lax.all_to_all(block_rows, 'col', split_axis=0, concat_axis=1, tiled=True)  7.25 us
    dot_general x1, matrix products, local(): lax.dot_general(act_all, upstream_all, (((0,), (0,)), ((), ())), preferre...  6.69 us
  transfers between devices with their start and end apart: 1, of which 0 were waited for; matrix products, arithmetic and copies ran while one was open for 6% of the time, Pallas kernels for 0%

profile of v17, /device:TPU:1, one launch (start us, length us, event | category | flops | bytes accessed | tf_op | source)
XLA Modules:
  0.0 186.8 jit_solution(10592807728475644864)
XLA Ops:
  0.6 38.5 %shard_map.75 = (bf16[16,128,512]{2,1,0:T(8,128)(2,1)}, bf16[16,128,512]{2,1,0:T(8,128)(2,1)}, bf16[16,128,1024]{2,1,0:T(8,128)(2,1)}, bf16[16,128,1024]{2,1,0:T(8,128)(2,1)}) custom-call(bf16[128,512]{1,0:T(8,128)(2,1)} %refs_0_.1, bf16[128,512]{1,0:T(8,128)(2,1)} %refs_1_.1, bf16[512,1024]{1,0:T(8,128)(2,1)} %refs_3_.3, bf16[1024,512]{1,0:T(8,128)(2,1)} %refs_2_.3), custom_call_target="tpu_custom_call" | custom-call | tf_op jit(solution)/shard_map/pallas_call | solution.py:298
  39.1 92.4 %shard_map.76 = (bf16[8,256,1024]{2,1,0:T(8,128)(2,1)}, bf16[8,256,1024]{2,1,0:T(8,128)(2,1)}, bf16[8,256,512]{2,1,0:T(8,128)(2,1)}, bf16[8,256,512]{2,1,0:T(8,128)(2,1)}) custom-call(bf16[8,256,1024]{2,1,0:T(8,128)(2,1)} %bitcast.17, bf16[8,256,1024]{2,1,0:T(8,128)(2,1)} %bitcast.18, bf16[1024,512]{1,0:T(8,128)(2,1)} %refs_2_.3, bf16[512,1024]{1,0:T(8,128)(2,1)} %refs_3_.3), custom_call_target="tpu_custom_call" | custom-call | tf_op jit(solution)/shard_map/pallas_call | solution.py:120
  131.6 34.5 %shard_map.77 = (f32[128,512]{1,0:T(8,128)}, f32[128,512]{1,0:T(8,128)}) custom-call(bf16[16,128,512]{2,1,0:T(8,128)(2,1)} %bitcast.19, bf16[16,128,512]{2,1,0:T(8,128)(2,1)} %bitcast.20), custom_call_target="tpu_custom_call" | custom-call | tf_op jit(solution)/shard_map/pallas_call | solution.py:388
  166.1 1.7 add_convert_fusion.1
  167.8 7.2 %all-to-all-start = ((bf16[8,16,512]{2,1,0:T(8,128)(2,1)}), bf16[8,16,512]{2,1,0:T(8,128)(2,1)S(1)}, u32[]{:S(2)}, u32[]{:S(2)}) async-start(bf16[8,16,512]{2,1,0:T(8,128)(2,1)} %bitcast.4), calls=%async_computation | async-start | bytes 262144 | tf_op jit(solution)/shard_map/all_to_all | solution.py:469
  175.1 0.0 copy-start.2
  175.1 0.0 copy-start.3
  175.1 6.7 %fusion.1 = f32[1024,512]{1,0:T(8,128)} fusion(bf16[2048,1024]{1,0:T(8,128)(2,1)} %bitcast.16, bf16[2048,512]{1,0:T(8,128)(2,1)} %bitcast.21), kind=kOutput, calls=%fused_computation.3 | convolution fusion | flops 2147483648 | bytes 8388608 | tf_op jit(solution)/shard_map/dot_general | solution.py:470
  181.7 0.0 copy-done.2
  181.7 0.0 copy-done.3
  181.7 0.0 copy-start
  181.8 0.0 copy-start.1
  181.8 3.7 %fusion = f32[512,1024]{1,0:T(8,128)} fusion(bf16[2048,512]{1,0:T(8,128)(2,1)S(1)} %bitcast.25, bf16[2048,1024]{1,0:T(8,128)(2,1)S(1)} %bitcast.24), kind=kOutput, calls=%fused_computation.2 | convolution fusion | flops 2147483648 | bytes 8388608 | tf_op jit(solution)/shard_map/dot_general | solution.py:473
  185.4 0.0 copy-done
  185.4 0.0 copy-done.1
  185.4 0.7 add_convert_fusion
  186.1 0.0 all-to-all-done
  186.1 0.7 copy.9
Async XLA Ops:
  167.8 18.3 %all-to-all-start = ((bf16[8,16,512]{2,1,0:T(8,128)(2,1)}), bf16[8,16,512]{2,1,0:T(8,128)(2,1)S(1)}, u32[]{:S(2)}, u32[]{:S(2)}) async-start(bf16[8,16,512]{2,1,0:T(8,128)(2,1)} %bitcast.4), calls=%async_computation | async-start | bytes 262144 | tf_op jit(solution)/shard_map/all_to_all | solution.py:469
  175.1 6.7 %copy-start.2 = (bf16[8,256,1024]{2,1,0:T(8,128)(2,1)S(1)}, bf16[8,256,1024]{2,1,0:T(8,128)(2,1)}, u32[]{:S(2)}) copy-start(bf16[8,256,1024]{2,1,0:T(8,128)(2,1)} %get-tuple-element.21) | copy-start | bytes 12582916
  175.1 6.7 %copy-start.3 = (bf16[16,128,512]{2,1,0:T(8,128)(2,1)S(1)}, bf16[16,128,512]{2,1,0:T(8,128)(2,1)}, u32[]{:S(2)}) copy-start(bf16[16,128,512]{2,1,0:T(8,128)(2,1)} %get-tuple-element.20) | copy-start | bytes 6291460
  181.7 3.7 %copy-start = (bf16[128,512]{1,0:T(8,128)(2,1)S(1)}, bf16[128,512]{1,0:T(8,128)(2,1)}, u32[]{:S(2)}) copy-start(bf16[128,512]{1,0:T(8,128)(2,1)} %refs_1_.1) | copy-start | bytes 393220
  181.8 3.7 %copy-start.1 = (f32[128,512]{1,0:T(8,128)S(1)}, f32[128,512]{1,0:T(8,128)}, u32[]{:S(2)}) copy-start(f32[128,512]{1,0:T(8,128)} %get-tuple-element.19) | copy-start | bytes 786436

commit v18 on v17

--- a/solution.py
+++ b/solution.py
@@ -95,18 +95,27 @@
         cp.wait_send()
 
 
-def _col_kernel(nx, narr, *refs):
+def _col_kernel(nx, ny, narr, *refs):
     parts = refs[:narr]
     weights = refs[narr:2 * narr]
     outs = refs[2 * narr:3 * narr]
-    prods = refs[3 * narr:4 * narr]
-    scratch = refs[4 * narr:]
+    sums = refs[3 * narr:4 * narr]
+    prods = refs[4 * narr:5 * narr]
+    scratch = refs[5 * narr:]
     row = lax.axis_index("row")
     x, k, d, nxt, prv = _col_ids(nx)
-    _greet(row, k, x, nxt, prv)
+    barrier = pltpu.get_barrier_semaphore()
+    for peer in (2 * x + 1 - k, 2 * nxt + k, 2 * prv + k):
+        pl.semaphore_signal(barrier, inc=1, device_id=(row, peer), device_id_type=MESH)
+    y, z, dr = _row_ids()
+    for p in (y * 4 + lax.rem(z + 4 + dr, 4), y * 4 + lax.rem(z + 4 - dr, 4),
+              lax.rem(y + ny + dr, ny) * 4 + z, lax.rem(y + ny - dr, ny) * 4 + z):
+        pl.semaphore_signal(barrier, inc=1, device_id=(p, 2 * x + k), device_id_type=MESH)
+    pl.semaphore_wait(barrier, 7)
     own = [o.at[2 * x + k] for o in outs]
     _rs_body(nx, narr, parts, own, *scratch[:7])
-    _ag_body(nx, narr, own, weights, outs, prods, *scratch[7:])
+    _ag_body(nx, narr, own, weights, outs, prods, *scratch[7:11])
+    _row_rs_body(ny, prods, sums, *scratch[11:])
 
 
 def col_exchange(arrays, weights, cid):
@@ -117,13 +126,16 @@
     cols = arrays[0].shape[1]
     width = weights[0].shape[1]
     parts = [a.reshape(n, rows, cols) for a in arrays]
+    nr = lax.axis_size("row")
+    ny = nr // 4
+    piece = n * rows // nr
     res = pl.pallas_call(
-        functools.partial(_col_kernel, nx, narr),
+        functools.partial(_col_kernel, nx, ny, narr),
         out_shape=[jax.ShapeDtypeStruct((n, rows, cols), jnp.bfloat16)] * narr
-        + [jax.ShapeDtypeStruct((n, rows, width), jnp.bfloat16)] * narr,
+        + [jax.ShapeDtypeStruct((piece, width), jnp.float32)] * narr,
         in_specs=[pl.BlockSpec(memory_space=pltpu.VMEM)] * (2 * narr),
         out_specs=[pl.BlockSpec(memory_space=pltpu.VMEM)] * (2 * narr),
-        scratch_shapes=[
+        scratch_shapes=[pltpu.VMEM((n, rows, width), jnp.bfloat16)] * narr + [
             pltpu.VMEM((narr, nx, rows, cols), jnp.bfloat16),
             pltpu.VMEM((narr, nx - 1, rows, cols), jnp.bfloat16),
             pltpu.VMEM((narr, nx - 1, rows, cols), jnp.bfloat16),
@@ -135,13 +147,21 @@
             pltpu.SemaphoreType.DMA((narr, nx)),
             pltpu.SemaphoreType.DMA((narr, nx)),
             pltpu.SemaphoreType.DMA((narr, nx)),
+            pltpu.VMEM((2, 3, 4, piece, width), jnp.bfloat16),
+            pltpu.VMEM((2, 3, 4, piece, width), jnp.bfloat16),
+            pltpu.VMEM((2, 4, piece, width), jnp.float32),
+            pltpu.VMEM((2, 3, piece, width), jnp.bfloat16),
+            pltpu.VMEM((2, 3, piece, width), jnp.bfloat16),
+            pltpu.SemaphoreType.DMA((2, 3, 4)),
+            pltpu.SemaphoreType.DMA((2, 3, 4)),
+            pltpu.SemaphoreType.DMA((2, 3)),
+            pltpu.SemaphoreType.DMA((2, 3)),
         ],
         compiler_params=pltpu.CompilerParams(collective_id=cid, has_side_effects=True,
                                              vmem_limit_bytes=64 * 1024 * 1024),
     )(*parts, *weights)
     gathered = [o.reshape(n * rows, cols) for o in res[:narr]]
-    products = [o.reshape(n * rows, width) for o in res[narr:]]
-    return gathered, products
+    return gathered, res[narr:]
 
 
 def _ag_body(nx, narr, chunks, weights, outs, prods, sr, rr, sc, rc):
@@ -312,18 +332,14 @@
     return [o.reshape(n * rows, o.shape[2]) for o in outs]
 
 
-def _row_rs_kernel(ny, *refs):
-    ins = refs[:2]
-    outs = refs[2:4]
-    sb1, rb1, ssum, sb2, rb2, s1, r1, s2, r2 = refs[4:]
+def _piece(ref, slot):
+    half = ref.shape[1] // 2
+    return ref.at[slot // 2, pl.ds(pl.multiple_of((slot % 2) * half, half), half)]
+
+
+def _row_rs_body(ny, ins, outs, sb1, rb1, ssum, sb2, rb2, s1, r1, s2, r2):
     col = lax.axis_index("col")
     y, z, d = _row_ids()
-    barrier = pltpu.get_barrier_semaphore()
-    peers = (y * 4 + lax.rem(z + 4 + d, 4), y * 4 + lax.rem(z + 4 - d, 4),
-             lax.rem(y + ny + d, ny) * 4 + z, lax.rem(y + ny - d, ny) * 4 + z)
-    for p in peers:
-        pl.semaphore_signal(barrier, inc=1, device_id=(p, col), device_id_type=MESH)
-    pl.semaphore_wait(barrier, 4)
     geo = [(4, ny, z, y, lambda pa, pb: pb * 4 + pa), (ny, 4, y, z, lambda pa, pb: pa * 4 + pb)]
 
     def dev(a, pa, pb):
@@ -343,11 +359,11 @@
                 na, nb, pa, pb, slot_of = geo[a]
                 slot = slot_of(lax.rem(pa + 4 * na - d * (s + 1), na), bq)
                 if s == 0:
-                    src = ins[a].at[slot]
+                    src = _piece(ins[a], slot)
                 else:
                     first[(a, s - 1, bq)].wait_recv()
                     sb1[a, s, bq] = (rb1[a, s - 1, bq].astype(jnp.float32)
-                                     + ins[a][slot].astype(jnp.float32)).astype(sb1.dtype)
+                                     + _piece(ins[a], slot)[...].astype(jnp.float32)).astype(sb1.dtype)
                     src = sb1.at[a, s, bq]
                 cp = send(src, rb1.at[a, s, bq], s1.at[a, s, bq], r1.at[a, s, bq],
                           dev(a, lax.rem(pa + na + d, na), pb))
@@ -357,7 +373,7 @@
         for a in range(2):
             na, nb, pa, pb, slot_of = geo[a]
             first[(a, 2, bq)].wait_recv()
-            ssum[a, bq] = rb1[a, 2, bq].astype(jnp.float32) + ins[a][slot_of(pa, bq)].astype(jnp.float32)
+            ssum[a, bq] = rb1[a, 2, bq].astype(jnp.float32) + _piece(ins[a], slot_of(pa, bq))[...].astype(jnp.float32)
     second = [[] for _ in range(2)]
     for t in range(4 - 1):
         for a in range(2):
@@ -380,32 +396,6 @@
         cp.wait_send()
 
 
-def row_reduce_scatter(first, second, cid):
-    n = lax.axis_size("row")
-    ny = n // 4
-    rows, cols = first.shape[0] // n, first.shape[1]
-    ins = [v.reshape(n, rows, cols) for v in (first, second)]
-    return pl.pallas_call(
-        functools.partial(_row_rs_kernel, ny),
-        out_shape=[jax.ShapeDtypeStruct((rows, cols), jnp.float32)] * 2,
-        in_specs=[pl.BlockSpec(memory_space=pltpu.VMEM)] * 2,
-        out_specs=[pl.BlockSpec(memory_space=pltpu.VMEM)] * 2,
-        scratch_shapes=[
-            pltpu.VMEM((2, 3, 4, rows, cols), jnp.bfloat16),
-            pltpu.VMEM((2, 3, 4, rows, cols), jnp.bfloat16),
-            pltpu.VMEM((2, 4, rows, cols), jnp.float32),
-            pltpu.VMEM((2, 3, rows, cols), jnp.bfloat16),
-            pltpu.VMEM((2, 3, rows, cols), jnp.bfloat16),
-            pltpu.SemaphoreType.DMA((2, 3, 4)),
-            pltpu.SemaphoreType.DMA((2, 3, 4)),
-            pltpu.SemaphoreType.DMA((2, 3)),
-            pltpu.SemaphoreType.DMA((2, 3)),
-        ],
-        compiler_params=pltpu.CompilerParams(collective_id=cid, has_side_effects=True,
-                                             vmem_limit_bytes=64 * 1024 * 1024),
-    )(*ins)
-
-
 def gelu_grad(value):
     cdf = 0.5 * (1.0 + jax.scipy.special.erf(value * 0.7071067811865476))
     pdf = jnp.exp(-0.5 * value * value) * 0.3989422804014327
@@ -463,8 +453,7 @@
 
 def local(tokens, w_in, w_out, cotangent):
     tokens_all, upstream_all, pre_term, dact_term = row_all_gather(tokens, cotangent, w_in, w_out, 3)
-    (act_all, dpre_all), (mixed_term, back_term) = col_exchange([pre_term, dact_term], [w_out, w_in], 1)
-    mixed, back = row_reduce_scatter(mixed_term, back_term, 4)
+    (act_all, dpre_all), (mixed, back) = col_exchange([pre_term, dact_term], [w_out, w_in], 1)
     block_rows = (tokens.astype(jnp.float32) + mixed).astype(jnp.bfloat16)
     block_out = lax.all_to_all(block_rows, "col", split_axis=0, concat_axis=1, tiled=True)
     grad_out = lax.dot_general(

time: 187 us -> 181 us (0.968)
  Pallas kernels: 165 us -> 160 us
    pallas_call x2 -> x1, Pallas kernels: 127 us -> 122 us  [col_exchange(): pl.pallas_call(functools.partial(_col_kernel, nx, ny, narr), out_shape=[j...]
where the time goes in v18:
time: 181 us
  Pallas kernels  160 us (88%)
  matrix products  10.4 us (6%)
  starting transfers between devices  6.58 us (4%)
  other arithmetic  2.35 us (1%)
    pallas_call x1, Pallas kernels, col_exchange(): pl.pallas_call(functools.partial(_col_kernel, nx, ny, narr), out_shape=[j...  122 us
    pallas_call x1, Pallas kernels, row_all_gather(): pl.pallas_call(functools.partial(_row_ag_kernel, ny), out_shape=[jax.Shap...  38.5 us
    dot_general x1, matrix products, local(): lax.dot_general(act_all, upstream_all, (((0,), (0,)), ((), ())), preferre...  6.69 us
    all_to_all x1, starting transfers between devices, local(): lax.all_to_all(block_rows, 'col', split_axis=0, concat_axis=1, tiled=True)  6.58 us
    dot_general x1, matrix products, local(): lax.dot_general(tokens_all, dpre_all, (((0,), (0,)), ((), ())), preferred...  3.67 us
  transfers between devices with their start and end apart: 1, of which 0 were waited for; matrix products, arithmetic and copies ran while one was open for 6% of the time, Pallas kernels for 0%

profile of v18, /device:TPU:1, one launch (start us, length us, event | category | flops | bytes accessed | tf_op | source)
XLA Modules:
  0.0 180.8 jit_solution(11345251618712941190)
XLA Ops:
  0.6 38.5 %shard_map.75 = (bf16[16,128,512]{2,1,0:T(8,128)(2,1)}, bf16[16,128,512]{2,1,0:T(8,128)(2,1)}, bf16[16,128,1024]{2,1,0:T(8,128)(2,1)}, bf16[16,128,1024]{2,1,0:T(8,128)(2,1)}) custom-call(bf16[128,512]{1,0:T(8,128)(2,1)} %refs_0_.1, bf16[128,512]{1,0:T(8,128)(2,1)} %refs_1_.1, bf16[512,1024]{1,0:T(8,128)(2,1)} %refs_3_.3, bf16[1024,512]{1,0:T(8,128)(2,1)} %refs_2_.3), custom_call_target="tpu_custom_call" | custom-call | tf_op jit(solution)/shard_map/pallas_call | solution.py:318
  39.1 121.6 %shard_map.76 = (bf16[8,256,1024]{2,1,0:T(8,128)(2,1)}, bf16[8,256,1024]{2,1,0:T(8,128)(2,1)}, f32[128,512]{1,0:T(8,128)}, f32[128,512]{1,0:T(8,128)}) custom-call(bf16[8,256,1024]{2,1,0:T(8,128)(2,1)} %bitcast.15, bf16[8,256,1024]{2,1,0:T(8,128)(2,1)} %bitcast.16, bf16[1024,512]{1,0:T(8,128)(2,1)} %refs_2_.3, bf16[512,1024]{1,0:T(8,128)(2,1)} %refs_3_.3), custom_call_target="tpu_custom_call" | custom-call | tf_op jit(solution)/shard_map/pallas_call | solution.py:132
  160.8 1.7 add_convert_fusion.1
  162.4 6.6 %all-to-all-start = ((bf16[8,16,512]{2,1,0:T(8,128)(2,1)}), bf16[8,16,512]{2,1,0:T(8,128)(2,1)S(1)}, u32[]{:S(2)}, u32[]{:S(2)}) async-start(bf16[8,16,512]{2,1,0:T(8,128)(2,1)} %bitcast.2), calls=%async_computation | async-start | bytes 262144 | tf_op jit(solution)/shard_map/all_to_all | solution.py:458
  169.0 0.0 copy-start.2
  169.0 0.0 copy-start.3
  169.0 6.7 %fusion.1 = f32[1024,512]{1,0:T(8,128)} fusion(bf16[2048,1024]{1,0:T(8,128)(2,1)} %bitcast.14, bf16[2048,512]{1,0:T(8,128)(2,1)} %bitcast.17), kind=kOutput, calls=%fused_computation.3 | convolution fusion | flops 2147483648 | bytes 8388608 | tf_op jit(solution)/shard_map/dot_general | solution.py:459
  175.7 0.0 copy-done.2
  175.7 0.0 copy-done.3
  175.7 0.0 copy-start
  175.7 0.0 copy-start.1
  175.7 3.7 %fusion = f32[512,1024]{1,0:T(8,128)} fusion(bf16[2048,512]{1,0:T(8,128)(2,1)S(1)} %bitcast.21, bf16[2048,1024]{1,0:T(8,128)(2,1)S(1)} %bitcast.20), kind=kOutput, calls=%fused_computation.2 | convolution fusion | flops 2147483648 | bytes 8388608 | tf_op jit(solution)/shard_map/dot_general | solution.py:462
  179.4 0.0 copy-done
  179.4 0.0 copy-done.1
  179.4 0.7 add_convert_fusion
  180.1 0.0 all-to-all-done
  180.1 0.7 copy.9
Async XLA Ops:
  162.4 17.7 %all-to-all-start = ((bf16[8,16,512]{2,1,0:T(8,128)(2,1)}), bf16[8,16,512]{2,1,0:T(8,128)(2,1)S(1)}, u32[]{:S(2)}, u32[]{:S(2)}) async-start(bf16[8,16,512]{2,1,0:T(8,128)(2,1)} %bitcast.2), calls=%async_computation | async-start | bytes 262144 | tf_op jit(solution)/shard_map/all_to_all | solution.py:458
  169.0 6.7 %copy-start.2 = (bf16[8,256,1024]{2,1,0:T(8,128)(2,1)S(1)}, bf16[8,256,1024]{2,1,0:T(8,128)(2,1)}, u32[]{:S(2)}) copy-start(bf16[8,256,1024]{2,1,0:T(8,128)(2,1)} %get-tuple-element.17) | copy-start | bytes 12582916
  169.0 6.7 %copy-start.3 = (bf16[16,128,512]{2,1,0:T(8,128)(2,1)S(1)}, bf16[16,128,512]{2,1,0:T(8,128)(2,1)}, u32[]{:S(2)}) copy-start(bf16[16,128,512]{2,1,0:T(8,128)(2,1)} %get-tuple-element.16) | copy-start | bytes 6291460
  175.7 3.7 %copy-start = (bf16[128,512]{1,0:T(8,128)(2,1)S(1)}, bf16[128,512]{1,0:T(8,128)(2,1)}, u32[]{:S(2)}) copy-start(bf16[128,512]{1,0:T(8,128)(2,1)} %refs_1_.1) | copy-start | bytes 393220
  175.7 3.7 %copy-start.1 = (f32[128,512]{1,0:T(8,128)S(1)}, f32[128,512]{1,0:T(8,128)}, u32[]{:S(2)}) copy-start(f32[128,512]{1,0:T(8,128)} %get-tuple-element.15) | copy-start | bytes 786436

commit v19 on v18

--- a/solution.py
+++ b/solution.py
@@ -96,12 +96,14 @@
 
 
 def _col_kernel(nx, ny, narr, *refs):
-    parts = refs[:narr]
-    weights = refs[narr:2 * narr]
-    outs = refs[2 * narr:3 * narr]
-    sums = refs[3 * narr:4 * narr]
-    prods = refs[4 * narr:5 * narr]
-    scratch = refs[5 * narr:]
+    tokens, cot, w_in, w_out = refs[:4]
+    panels = refs[4:6]
+    outs = refs[6:8]
+    sums = refs[8:10]
+    parts = refs[10:12]
+    prods = refs[12:14]
+    scratch = refs[14:]
+    weights = [w_out, w_in]
     row = lax.axis_index("row")
     x, k, d, nxt, prv = _col_ids(nx)
     barrier = pltpu.get_barrier_semaphore()
@@ -112,30 +114,33 @@
               lax.rem(y + ny + dr, ny) * 4 + z, lax.rem(y + ny - dr, ny) * 4 + z):
         pl.semaphore_signal(barrier, inc=1, device_id=(p, 2 * x + k), device_id_type=MESH)
     pl.semaphore_wait(barrier, 7)
+    _row_ag_body(ny, [tokens, cot], [w_in, w_out], panels, parts, *scratch[20:23])
     own = [o.at[2 * x + k] for o in outs]
     _rs_body(nx, narr, parts, own, *scratch[:7])
     _ag_body(nx, narr, own, weights, outs, prods, *scratch[7:11])
-    _row_rs_body(ny, prods, sums, *scratch[11:])
-
-
-def col_exchange(arrays, weights, cid):
+    _row_rs_body(ny, prods, sums, *scratch[11:20])
+
+
+def fused_block(tokens, cotangent, w_in, w_out, cid):
     n = lax.axis_size("col")
     nx = n // 2
-    narr = len(arrays)
-    rows = arrays[0].shape[0] // n
-    cols = arrays[0].shape[1]
-    width = weights[0].shape[1]
-    parts = [a.reshape(n, rows, cols) for a in arrays]
+    narr = 2
     nr = lax.axis_size("row")
     ny = nr // 4
-    piece = n * rows // nr
+    piece, model = tokens.shape
+    hidden = w_in.shape[1]
+    rows = piece * nr // n
+    cols = hidden
+    width = model
     res = pl.pallas_call(
         functools.partial(_col_kernel, nx, ny, narr),
-        out_shape=[jax.ShapeDtypeStruct((n, rows, cols), jnp.bfloat16)] * narr
+        out_shape=[jax.ShapeDtypeStruct((nr, piece, model), jnp.bfloat16)] * 2
+        + [jax.ShapeDtypeStruct((n, rows, cols), jnp.bfloat16)] * narr
         + [jax.ShapeDtypeStruct((piece, width), jnp.float32)] * narr,
-        in_specs=[pl.BlockSpec(memory_space=pltpu.VMEM)] * (2 * narr),
-        out_specs=[pl.BlockSpec(memory_space=pltpu.VMEM)] * (2 * narr),
-        scratch_shapes=[pltpu.VMEM((n, rows, width), jnp.bfloat16)] * narr + [
+        in_specs=[pl.BlockSpec(memory_space=pltpu.VMEM)] * 4,
+        out_specs=[pl.BlockSpec(memory_space=pltpu.VMEM)] * 6,
+        scratch_shapes=[pltpu.VMEM((n, rows, cols), jnp.bfloat16)] * narr
+        + [pltpu.VMEM((n, rows, width), jnp.bfloat16)] * narr + [
             pltpu.VMEM((narr, nx, rows, cols), jnp.bfloat16),
             pltpu.VMEM((narr, nx - 1, rows, cols), jnp.bfloat16),
             pltpu.VMEM((narr, nx - 1, rows, cols), jnp.bfloat16),
@@ -156,12 +161,15 @@
             pltpu.SemaphoreType.DMA((2, 3, 4)),
             pltpu.SemaphoreType.DMA((2, 3)),
             pltpu.SemaphoreType.DMA((2, 3)),
+            pltpu.SemaphoreType.DMA((2, 4)),
+            pltpu.SemaphoreType.DMA((2, 4, 4)),
+            pltpu.SemaphoreType.DMA((2, nr)),
         ],
         compiler_params=pltpu.CompilerParams(collective_id=cid, has_side_effects=True,
                                              vmem_limit_bytes=64 * 1024 * 1024),
-    )(*parts, *weights)
-    gathered = [o.reshape(n * rows, cols) for o in res[:narr]]
-    return gathered, res[narr:]
+    )(tokens, cotangent, w_in, w_out)
+    return ([o.reshape(nr * piece, model) for o in res[:2]]
+            + [o.reshape(n * rows, cols) for o in res[2:4]] + list(res[4:]))
 
 
 def _ag_body(nx, narr, chunks, weights, outs, prods, sr, rr, sc, rc):
@@ -224,12 +232,7 @@
     return y, z, d
 
 
-def _row_ag_kernel(ny, *refs):
-    ins = refs[:2]
-    weights = refs[2:4]
-    outs = refs[4:6]
-    terms = refs[6:8]
-    sa, sb, rsem = refs[8:]
+def _row_ag_body(ny, ins, weights, outs, terms, sa, sb, rsem):
 
     def product(a, slot):
         if a == 0:
@@ -237,17 +240,13 @@
         else:
             value = lax.dot_general(outs[a][slot], weights[a][...], (((1,), (1,)), ((), ())),
                                     preferred_element_type=jnp.float32)
-        terms[a][slot] = value.astype(terms[a].dtype)
+        _piece(terms[a], slot)[...] = value.astype(terms[a].dtype)
 
     col = lax.axis_index("col")
     y, z, d = _row_ids()
     me = y * 4 + z
-    barrier = pltpu.get_barrier_semaphore()
     peers = (y * 4 + lax.rem(z + 4 + d, 4), y * 4 + lax.rem(z + 4 - d, 4),
              lax.rem(y + ny + d, ny) * 4 + z, lax.rem(y + ny - d, ny) * 4 + z)
-    for p in peers:
-        pl.semaphore_signal(barrier, inc=1, device_id=(p, col), device_id_type=MESH)
-    pl.semaphore_wait(barrier, 4)
     geo = []
     for a in range(2):
         if a == 0:
@@ -308,28 +307,6 @@
                 product(a, slot)
     for cp in sends:
         cp.wait_send()
-
-
-def row_all_gather(first, second, w_first, w_second, cid):
-    n = lax.axis_size("row")
-    ny = n // 4
-    rows, cols = first.shape
-    width = w_first.shape[1]
-    outs = pl.pallas_call(
-        functools.partial(_row_ag_kernel, ny),
-        out_shape=[jax.ShapeDtypeStruct((n, rows, cols), first.dtype)] * 2
-        + [jax.ShapeDtypeStruct((n, rows, width), jnp.bfloat16)] * 2,
-        in_specs=[pl.BlockSpec(memory_space=pltpu.VMEM)] * 4,
-        out_specs=[pl.BlockSpec(memory_space=pltpu.VMEM)] * 4,
-        scratch_shapes=[
-            pltpu.SemaphoreType.DMA((2, 4)),
-            pltpu.SemaphoreType.DMA((2, 4, 4)),
-            pltpu.SemaphoreType.DMA((2, n)),
-        ],
-        compiler_params=pltpu.CompilerParams(collective_id=cid, has_side_effects=True,
-                                             vmem_limit_bytes=64 * 1024 * 1024),
-    )(first, second, w_first, w_second)
-    return [o.reshape(n * rows, o.shape[2]) for o in outs]
 
 
 def _piece(ref, slot):
@@ -452,8 +429,7 @@
 
 
 def local(tokens, w_in, w_out, cotangent):
-    tokens_all, upstream_all, pre_term, dact_term = row_all_gather(tokens, cotangent, w_in, w_out, 3)
-    (act_all, dpre_all), (mixed, back) = col_exchange([pre_term, dact_term], [w_out, w_in], 1)
+    tokens_all, upstream_all, act_all, dpre_all, mixed, back = fused_block(tokens, cotangent, w_in, w_out, 1)
     block_rows = (tokens.astype(jnp.float32) + mixed).astype(jnp.bfloat16)
     block_out = lax.all_to_all(block_rows, "col", split_axis=0, concat_axis=1, tiled=True)
     grad_out = lax.dot_general(

time: 181 us -> 172 us (0.950)
  Pallas kernels: 160 us -> 150 us
    pallas_call x2 -> x1, Pallas kernels: 160 us -> 150 us  [fused_block(): pl.pallas_call(functools.partial(_col_kernel, nx, ny, narr), out_shape=[j...]
    dot_general x1, matrix products: 6.69 us -> 3.69 us  [local(): lax.dot_general(act_all, upstream_all, (((0,), (0,)), ((), ())), preferre...]
    dot_general x1, matrix products: 3.67 us -> 6.63 us  [local(): lax.dot_general(tokens_all, dpre_all, (((0,), (0,)), ((), ())), preferred...]
where the time goes in v19:
time: 172 us
  Pallas kernels  150 us (87%)
  matrix products  10.3 us (6%)
  starting transfers between devices  7.32 us (4%)
  other arithmetic  2.35 us (1%)
    pallas_call x1, Pallas kernels, fused_block(): pl.pallas_call(functools.partial(_col_kernel, nx, ny, narr), out_shape=[j...  150 us
    all_to_all x1, starting transfers between devices, local(): lax.all_to_all(block_rows, 'col', split_axis=0, concat_axis=1, tiled=True)  7.32 us
    dot_general x1, matrix products, local(): lax.dot_general(tokens_all, dpre_all, (((0,), (0,)), ((), ())), preferred...  6.63 us
    dot_general x1, matrix products, local(): lax.dot_general(act_all, upstream_all, (((0,), (0,)), ((), ())), preferre...  3.69 us
  transfers between devices with their start and end apart: 1, of which 0 were waited for; matrix products, arithmetic and copies ran while one was open for 6% of the time, Pallas kernels for 0%

profile of v19, /device:TPU:1, one launch (start us, length us, event | category | flops | bytes accessed | tf_op | source)
XLA Modules:
  0.0 171.8 jit_solution(4815988976711499851)
XLA Ops:
  0.6 150.4 %shard_map.75 = (bf16[16,128,512]{2,1,0:T(8,128)(2,1)}, bf16[16,128,512]{2,1,0:T(8,128)(2,1)}, bf16[8,256,1024]{2,1,0:T(8,128)(2,1)}, bf16[8,256,1024]{2,1,0:T(8...) custom-call(bf16[128,512]{1,0:T(8,128)(2,1)} %refs_0_.1, bf16[128,512]{1,0:T(8,128)(2,1)} %refs_1_.1, ...), custom_call_target="tpu_custom_call" | custom-call | tf_op jit(solution)/shard_map/pallas_call | solution.py:135
  151.1 1.7 add_convert_fusion.1
  152.7 7.3 %all-to-all-start = ((bf16[8,16,512]{2,1,0:T(8,128)(2,1)}), bf16[8,16,512]{2,1,0:T(8,128)(2,1)S(1)}, u32[]{:S(2)}, u32[]{:S(2)}) async-start(bf16[8,16,512]{2,1,0:T(8,128)(2,1)} %bitcast), calls=%async_computation | async-start | bytes 262144 | tf_op jit(solution)/shard_map/all_to_all | solution.py:434
  160.1 0.0 copy-start
  160.1 0.0 copy-start.1
  160.1 6.6 %fusion = f32[512,1024]{1,0:T(8,128)} fusion(bf16[2048,512]{1,0:T(8,128)(2,1)} %bitcast.17, bf16[2048,1024]{1,0:T(8,128)(2,1)} %bitcast.16), kind=kOutput, calls=%fused_computation.2 | convolution fusion | flops 2147483648 | bytes 8388608 | tf_op jit(solution)/shard_map/dot_general | solution.py:438
  166.7 0.0 copy-done
  166.7 0.0 copy-done.1
  166.7 0.0 copy-start.2
  166.7 0.0 copy-start.3
  166.7 3.7 %fusion.1 = f32[1024,512]{1,0:T(8,128)} fusion(bf16[2048,1024]{1,0:T(8,128)(2,1)S(1)} %bitcast.12, bf16[2048,512]{1,0:T(8,128)(2,1)S(1)} %bitcast.13), kind=kOutput, calls=%fused_computation.3 | convolution fusion | flops 2147483648 | bytes 8388608 | tf_op jit(solution)/shard_map/dot_general | solution.py:435
  170.4 0.0 copy-done.2
  170.4 0.0 copy-done.3
  170.4 0.7 add_convert_fusion
  171.1 0.0 all-to-all-done
  171.1 0.7 copy.9
Async XLA Ops:
  152.7 18.4 %all-to-all-start = ((bf16[8,16,512]{2,1,0:T(8,128)(2,1)}), bf16[8,16,512]{2,1,0:T(8,128)(2,1)S(1)}, u32[]{:S(2)}, u32[]{:S(2)}) async-start(bf16[8,16,512]{2,1,0:T(8,128)(2,1)} %bitcast), calls=%async_computation | async-start | bytes 262144 | tf_op jit(solution)/shard_map/all_to_all | solution.py:434
  160.1 6.6 %copy-start = (bf16[8,256,1024]{2,1,0:T(8,128)(2,1)S(1)}, bf16[8,256,1024]{2,1,0:T(8,128)(2,1)}, u32[]{:S(2)}) copy-start(bf16[8,256,1024]{2,1,0:T(8,128)(2,1)} %get-tuple-element.14) | copy-start | bytes 12582916
  160.1 6.6 %copy-start.1 = (bf16[16,128,512]{2,1,0:T(8,128)(2,1)S(1)}, bf16[16,128,512]{2,1,0:T(8,128)(2,1)}, u32[]{:S(2)}) copy-start(bf16[16,128,512]{2,1,0:T(8,128)(2,1)} %get-tuple-element.15) | copy-start | bytes 6291460
  166.7 3.7 %copy-start.2 = (bf16[128,512]{1,0:T(8,128)(2,1)S(1)}, bf16[128,512]{1,0:T(8,128)(2,1)}, u32[]{:S(2)}) copy-start(bf16[128,512]{1,0:T(8,128)(2,1)} %refs_1_.1) | copy-start | bytes 393220
  166.7 3.7 %copy-start.3 = (f32[128,512]{1,0:T(8,128)S(1)}, f32[128,512]{1,0:T(8,128)}, u32[]{:S(2)}) copy-start(f32[128,512]{1,0:T(8,128)} %get-tuple-element.11) | copy-start | bytes 786436

commit v20 on v19

--- a/solution.py
+++ b/solution.py
@@ -118,7 +118,7 @@
     own = [o.at[2 * x + k] for o in outs]
     _rs_body(nx, narr, parts, own, *scratch[:7])
     _ag_body(nx, narr, own, weights, outs, prods, *scratch[7:11])
-    _row_rs_body(ny, prods, sums, *scratch[11:20])
+    _row_rs_body(ny, prods, sums, [tokens, cot], *scratch[11:20])
 
 
 def fused_block(tokens, cotangent, w_in, w_out, cid):
@@ -136,7 +136,7 @@
         functools.partial(_col_kernel, nx, ny, narr),
         out_shape=[jax.ShapeDtypeStruct((nr, piece, model), jnp.bfloat16)] * 2
         + [jax.ShapeDtypeStruct((n, rows, cols), jnp.bfloat16)] * narr
-        + [jax.ShapeDtypeStruct((piece, width), jnp.float32)] * narr,
+        + [jax.ShapeDtypeStruct((piece, width), jnp.bfloat16)] * narr,
         in_specs=[pl.BlockSpec(memory_space=pltpu.VMEM)] * 4,
         out_specs=[pl.BlockSpec(memory_space=pltpu.VMEM)] * 6,
         scratch_shapes=[pltpu.VMEM((n, rows, cols), jnp.bfloat16)] * narr
@@ -314,7 +314,7 @@
     return ref.at[slot // 2, pl.ds(pl.multiple_of((slot % 2) * half, half), half)]
 
 
-def _row_rs_body(ny, ins, outs, sb1, rb1, ssum, sb2, rb2, s1, r1, s2, r2):
+def _row_rs_body(ny, ins, outs, addends, sb1, rb1, ssum, sb2, rb2, s1, r1, s2, r2):
     col = lax.axis_index("col")
     y, z, d = _row_ids()
     geo = [(4, ny, z, y, lambda pa, pb: pb * 4 + pa), (ny, 4, y, z, lambda pa, pb: pa * 4 + pb)]
@@ -368,7 +368,8 @@
             second[a][t].wait_recv()
     for a in range(2):
         na, nb, pa, pb, slot_of = geo[a]
-        outs[a][...] = rb2[a, 2].astype(jnp.float32) + ssum[a, pb]
+        outs[a][...] = (addends[a][...].astype(jnp.float32) + rb2[a, 2].astype(jnp.float32)
+                        + ssum[a, pb]).astype(outs[a].dtype)
     for cp in sends:
         cp.wait_send()
 
@@ -429,8 +430,8 @@
 
 
 def local(tokens, w_in, w_out, cotangent):
-    tokens_all, upstream_all, act_all, dpre_all, mixed, back = fused_block(tokens, cotangent, w_in, w_out, 1)
-    block_rows = (tokens.astype(jnp.float32) + mixed).astype(jnp.bfloat16)
+    tokens_all, upstream_all, act_all, dpre_all, block_rows, grad_tokens = fused_block(
+        tokens, cotangent, w_in, w_out, 1)
     block_out = lax.all_to_all(block_rows, "col", split_axis=0, concat_axis=1, tiled=True)
     grad_out = lax.dot_general(
         act_all, upstream_all, (((0,), (0,)), ((), ())), preferred_element_type=jnp.float32
@@ -438,7 +439,6 @@
     grad_in = lax.dot_general(
         tokens_all, dpre_all, (((0,), (0,)), ((), ())), preferred_element_type=jnp.float32
     )
-    grad_tokens = (cotangent.astype(jnp.float32) + back).astype(jnp.bfloat16)
     return (block_out, grad_tokens, grad_in, grad_out)
 
 

time: 172 us -> 170 us (0.988)
  other arithmetic: 2.35 us -> 0 us
    convert_element_type x2 -> x0, other arithmetic: 2.35 us -> none  [the longest x1 1.67 us: local(): block_rows = (tokens.astype(jnp.float32) + mixed).astype(jnp.bfloat16)]
where the time goes in v20:
time: 170 us
  Pallas kernels  150 us (88%)
  matrix products  10.3 us (6%)
  starting transfers between devices  7.33 us (4%)
    pallas_call x1, Pallas kernels, fused_block(): pl.pallas_call(functools.partial(_col_kernel, nx, ny, narr), out_shape=[j...  150 us
    all_to_all x1, starting transfers between devices, local(): lax.all_to_all(block_rows, 'col', split_axis=0, concat_axis=1, tiled=True)  7.33 us
    dot_general x1, matrix products, local(): lax.dot_general(tokens_all, dpre_all, (((0,), (0,)), ((), ())), preferred...  6.63 us
    dot_general x1, matrix products, local(): lax.dot_general(act_all, upstream_all, (((0,), (0,)), ((), ())), preferre...  3.68 us
  transfers between devices with their start and end apart: 1, of which 0 were waited for; matrix products, arithmetic and copies ran while one was open for 6% of the time, Pallas kernels for 0%

profile of v20, /device:TPU:1, one launch (start us, length us, event | category | flops | bytes accessed | tf_op | source)
XLA Modules:
  0.0 170.0 jit_solution(15050562845676715854)
XLA Ops:
  0.6 150.4 %shard_map.75 = (bf16[16,128,512]{2,1,0:T(8,128)(2,1)}, bf16[16,128,512]{2,1,0:T(8,128)(2,1)}, bf16[8,256,1024]{2,1,0:T(8,128)(2,1)}, bf16[8,256,1024]{2,1,0:T(8...) custom-call(bf16[128,512]{1,0:T(8,128)(2,1)} %refs_0_.1, bf16[128,512]{1,0:T(8,128)(2,1)} %refs_1_.1, ...), custom_call_target="tpu_custom_call" | custom-call | tf_op jit(solution)/shard_map/pallas_call | solution.py:135
  151.0 7.3 %all-to-all-start = ((bf16[8,16,512]{2,1,0:T(8,128)(2,1)}), bf16[8,16,512]{2,1,0:T(8,128)(2,1)S(1)}, u32[]{:S(2)}, u32[]{:S(2)}) async-start(bf16[8,16,512]{2,1,0:T(8,128)(2,1)} %bitcast.15), calls=%async_computation | async-start | bytes 262144 | tf_op jit(solution)/shard_map/all_to_all | solution.py:435
  158.4 0.0 copy-start
  158.4 0.0 copy-start.1
  158.4 6.6 %fusion = f32[512,1024]{1,0:T(8,128)} fusion(bf16[2048,512]{1,0:T(8,128)(2,1)} %bitcast.18, bf16[2048,1024]{1,0:T(8,128)(2,1)} %bitcast.17), kind=kOutput, calls=%fused_computation | convolution fusion | flops 2147483648 | bytes 8388608 | tf_op jit(solution)/shard_map/dot_general | solution.py:439
  165.0 0.0 copy-done
  165.0 0.0 copy-done.1
  165.0 0.0 copy-start.2
  165.0 3.7 %fusion.1 = f32[1024,512]{1,0:T(8,128)} fusion(bf16[2048,1024]{1,0:T(8,128)(2,1)S(1)} %bitcast.12, bf16[2048,512]{1,0:T(8,128)(2,1)S(1)} %bitcast.13), kind=kOutput, calls=%fused_computation.1 | convolution fusion | flops 2147483648 | bytes 8388608 | tf_op jit(solution)/shard_map/dot_general | solution.py:436
  168.7 0.0 all-to-all-done
  168.7 0.7 copy.9
  169.4 0.0 copy-done.2
  169.4 0.7 copy.11
Async XLA Ops:
  151.0 17.7 %all-to-all-start = ((bf16[8,16,512]{2,1,0:T(8,128)(2,1)}), bf16[8,16,512]{2,1,0:T(8,128)(2,1)S(1)}, u32[]{:S(2)}, u32[]{:S(2)}) async-start(bf16[8,16,512]{2,1,0:T(8,128)(2,1)} %bitcast.15), calls=%async_computation | async-start | bytes 262144 | tf_op jit(solution)/shard_map/all_to_all | solution.py:435
  158.4 6.6 %copy-start = (bf16[8,256,1024]{2,1,0:T(8,128)(2,1)S(1)}, bf16[8,256,1024]{2,1,0:T(8,128)(2,1)}, u32[]{:S(2)}) copy-start(bf16[8,256,1024]{2,1,0:T(8,128)(2,1)} %get-tuple-element.14) | copy-start | bytes 12582916
  158.4 6.6 %copy-start.1 = (bf16[16,128,512]{2,1,0:T(8,128)(2,1)S(1)}, bf16[16,128,512]{2,1,0:T(8,128)(2,1)}, u32[]{:S(2)}) copy-start(bf16[16,128,512]{2,1,0:T(8,128)(2,1)} %get-tuple-element.15) | copy-start | bytes 6291460
  165.0 4.4 %copy-start.2 = (bf16[128,512]{1,0:T(8,128)(2,1)S(1)}, bf16[128,512]{1,0:T(8,128)(2,1)}, u32[]{:S(2)}) copy-start(bf16[128,512]{1,0:T(8,128)(2,1)} %get-tuple-element.21) | copy-start | bytes 393220

commit v21 on v20

--- a/solution.py
+++ b/solution.py
@@ -21,8 +21,9 @@
 
 def _greet(row, k, x, nxt, prv):
     barrier = pltpu.get_barrier_semaphore()
-    for peer in (2 * x + 1 - k, 2 * nxt + k, 2 * prv + k):
-        pl.semaphore_signal(barrier, inc=1, device_id=(row, peer), device_id_type=MESH)
+    me_c = 2 * x + k
+    for o in range(1, 2 * nx):
+        pl.semaphore_signal(barrier, inc=1, device_id=(row, lax.rem(me_c + o, 2 * nx)), device_id_type=MESH)
     pl.semaphore_wait(barrier, 3)
 
 
@@ -100,25 +101,42 @@
     panels = refs[4:6]
     outs = refs[6:8]
     sums = refs[8:10]
-    parts = refs[10:12]
-    prods = refs[12:14]
-    scratch = refs[14:]
+    final = refs[10]
+    parts = refs[11:13]
+    prods = refs[13:15]
+    scratch = refs[15:]
     weights = [w_out, w_in]
     row = lax.axis_index("row")
     x, k, d, nxt, prv = _col_ids(nx)
     barrier = pltpu.get_barrier_semaphore()
-    for peer in (2 * x + 1 - k, 2 * nxt + k, 2 * prv + k):
-        pl.semaphore_signal(barrier, inc=1, device_id=(row, peer), device_id_type=MESH)
+    me_c = 2 * x + k
+    for o in range(1, 2 * nx):
+        pl.semaphore_signal(barrier, inc=1, device_id=(row, lax.rem(me_c + o, 2 * nx)), device_id_type=MESH)
     y, z, dr = _row_ids()
     for p in (y * 4 + lax.rem(z + 4 + dr, 4), y * 4 + lax.rem(z + 4 - dr, 4),
               lax.rem(y + ny + dr, ny) * 4 + z, lax.rem(y + ny - dr, ny) * 4 + z):
         pl.semaphore_signal(barrier, inc=1, device_id=(p, 2 * x + k), device_id_type=MESH)
-    pl.semaphore_wait(barrier, 7)
+    pl.semaphore_wait(barrier, 2 * nx - 1 + 4)
     _row_ag_body(ny, [tokens, cot], [w_in, w_out], panels, parts, *scratch[20:23])
     own = [o.at[2 * x + k] for o in outs]
     _rs_body(nx, narr, parts, own, *scratch[:7])
     _ag_body(nx, narr, own, weights, outs, prods, *scratch[7:11])
     _row_rs_body(ny, prods, sums, [tokens, cot], *scratch[11:20])
+    span = final.shape[0]
+    width = sums[0].shape[1]
+    final[:, pl.ds(pl.multiple_of(me_c * width, width), width)] = sums[0][pl.ds(pl.multiple_of(me_c * span, span), span), :]
+    spread = []
+    for o in range(1, 2 * nx):
+        peer = lax.rem(me_c + o, 2 * nx)
+        cp = pltpu.make_async_remote_copy(
+            src_ref=sums[0].at[pl.ds(pl.multiple_of(peer * span, span), span)],
+            dst_ref=final.at[:, pl.ds(pl.multiple_of(me_c * width, width), width)],
+            send_sem=scratch[23].at[o], recv_sem=scratch[24].at[o],
+            device_id=(row, peer), device_id_type=MESH)
+        cp.start()
+        spread.append(cp)
+    for cp in spread:
+        cp.wait()
 
 
 def fused_block(tokens, cotangent, w_in, w_out, cid):
@@ -136,9 +154,10 @@
         functools.partial(_col_kernel, nx, ny, narr),
         out_shape=[jax.ShapeDtypeStruct((nr, piece, model), jnp.bfloat16)] * 2
         + [jax.ShapeDtypeStruct((n, rows, cols), jnp.bfloat16)] * narr
-        + [jax.ShapeDtypeStruct((piece, width), jnp.bfloat16)] * narr,
+        + [jax.ShapeDtypeStruct((piece, width), jnp.bfloat16)] * narr
+        + [jax.ShapeDtypeStruct((piece // n, width * n), jnp.bfloat16)],
         in_specs=[pl.BlockSpec(memory_space=pltpu.VMEM)] * 4,
-        out_specs=[pl.BlockSpec(memory_space=pltpu.VMEM)] * 6,
+        out_specs=[pl.BlockSpec(memory_space=pltpu.VMEM)] * 7,
         scratch_shapes=[pltpu.VMEM((n, rows, cols), jnp.bfloat16)] * narr
         + [pltpu.VMEM((n, rows, width), jnp.bfloat16)] * narr + [
             pltpu.VMEM((narr, nx, rows, cols), jnp.bfloat16),
@@ -164,6 +183,8 @@
             pltpu.SemaphoreType.DMA((2, 4)),
             pltpu.SemaphoreType.DMA((2, 4, 4)),
             pltpu.SemaphoreType.DMA((2, nr)),
+            pltpu.SemaphoreType.DMA((n,)),
+            pltpu.SemaphoreType.DMA((n,)),
         ],
         compiler_params=pltpu.CompilerParams(collective_id=cid, has_side_effects=True,
                                              vmem_limit_bytes=64 * 1024 * 1024),
@@ -430,9 +451,8 @@
 
 
 def local(tokens, w_in, w_out, cotangent):
-    tokens_all, upstream_all, act_all, dpre_all, block_rows, grad_tokens = fused_block(
+    tokens_all, upstream_all, act_all, dpre_all, block_rows, grad_tokens, block_out = fused_block(
         tokens, cotangent, w_in, w_out, 1)
-    block_out = lax.all_to_all(block_rows, "col", split_axis=0, concat_axis=1, tiled=True)
     grad_out = lax.dot_general(
         act_all, upstream_all, (((0,), (0,)), ((), ())), preferred_element_type=jnp.float32
     )

time: 170 us -> 171 us (level)
  Pallas kernels: 150 us -> 159 us
  starting transfers between devices: 7.33 us -> 0 us
    pallas_call x1, Pallas kernels: 150 us -> 159 us  [fused_block(): pl.pallas_call(functools.partial(_col_kernel, nx, ny, narr), out_shape=[j...]
    all_to_all x1 -> x0, starting transfers between devices: 7.33 us -> none  [local(): lax.all_to_all(block_rows, 'col', split_axis=0, concat_axis=1, tiled=True)]
  transfers between devices with their start and end apart: 1 -> 0, of which waited for: 0 -> 0; matrix products, arithmetic and copies ran while one was open for 6% -> 0% of each run, Pallas kernels for 0% -> 0%
where the time goes in v21:
time: 171 us
  Pallas kernels  159 us (93%)
  matrix products  10.3 us (6%)
    pallas_call x1, Pallas kernels, fused_block(): pl.pallas_call(functools.partial(_col_kernel, nx, ny, narr), out_shape=[j...  159 us
    dot_general x1, matrix products, local(): lax.dot_general(tokens_all, dpre_all, (((0,), (0,)), ((), ())), preferred...  6.64 us
    dot_general x1, matrix products, local(): lax.dot_general(act_all, upstream_all, (((0,), (0,)), ((), ())), preferre...  3.68 us

profile of v21, /device:TPU:1, one launch (start us, length us, event | category | flops | bytes accessed | tf_op | source)
XLA Modules:
  0.0 170.9 jit_solution(11310981989936720257)
XLA Ops:
  0.6 158.6 %shard_map.75 = (bf16[16,128,512]{2,1,0:T(8,128)(2,1)}, bf16[16,128,512]{2,1,0:T(8,128)(2,1)}, bf16[8,256,1024]{2,1,0:T(8,128)(2,1)}, bf16[8,256,1024]{2,1,0:T(8...) custom-call(bf16[128,512]{1,0:T(8,128)(2,1)} %refs_0_.1, ...), custom_call_target="tpu_custom_call" | custom-call | tf_op jit(solution)/shard_map/pallas_call | solution.py:153
  159.2 0.0 copy-start
  159.2 0.0 copy-start.1
  159.2 6.6 %fusion = f32[512,1024]{1,0:T(8,128)} fusion(bf16[2048,512]{1,0:T(8,128)(2,1)} %bitcast.11, bf16[2048,1024]{1,0:T(8,128)(2,1)} %bitcast.10), kind=kOutput, calls=%fused_computation | convolution fusion | flops 2147483648 | bytes 8388608 | tf_op jit(solution)/shard_map/dot_general | solution.py:459
  165.8 0.0 copy-done
  165.8 0.0 copy-done.1
  165.9 0.0 copy-start.3
  165.9 0.0 copy-start.2
  165.9 3.7 %fusion.1 = f32[1024,512]{1,0:T(8,128)} fusion(bf16[2048,1024]{1,0:T(8,128)(2,1)S(1)} %bitcast.8, bf16[2048,512]{1,0:T(8,128)(2,1)S(1)} %bitcast.9), kind=kOutput, calls=%fused_computation.1 | convolution fusion | flops 2147483648 | bytes 8388608 | tf_op jit(solution)/shard_map/dot_general | solution.py:456
  169.5 0.0 copy-done.3
  169.5 0.7 copy.10
  170.2 0.0 copy-done.2
  170.2 0.7 copy.11
Async XLA Ops:
  159.2 6.7 %copy-start = (bf16[8,256,1024]{2,1,0:T(8,128)(2,1)S(1)}, bf16[8,256,1024]{2,1,0:T(8,128)(2,1)}, u32[]{:S(2)}) copy-start(bf16[8,256,1024]{2,1,0:T(8,128)(2,1)} %get-tuple-element.14) | copy-start | bytes 12582916
  159.2 6.7 %copy-start.1 = (bf16[16,128,512]{2,1,0:T(8,128)(2,1)S(1)}, bf16[16,128,512]{2,1,0:T(8,128)(2,1)}, u32[]{:S(2)}) copy-start(bf16[16,128,512]{2,1,0:T(8,128)(2,1)} %get-tuple-element.15) | copy-start | bytes 6291460
  165.9 3.7 %copy-start.3 = (bf16[16,4096]{1,0:T(8,128)(2,1)S(1)}, bf16[16,4096]{1,0:T(8,128)(2,1)}, u32[]{:S(2)}) copy-start(bf16[16,4096]{1,0:T(8,128)(2,1)} %get-tuple-element.20) | copy-start | bytes 393220
  165.9 4.3 %copy-start.2 = (bf16[128,512]{1,0:T(8,128)(2,1)S(1)}, bf16[128,512]{1,0:T(8,128)(2,1)}, u32[]{:S(2)}) copy-start(bf16[128,512]{1,0:T(8,128)(2,1)} %get-tuple-element.21) | copy-start | bytes 393220
